TPU v7x, 128 devices: a whole 4x4x4 slice. The times are simulated.
128 devices in a mesh: user: 4 (over y_lo, core), item: 32 (over z, y_hi, x).
Axes of the slice: x: 4, y: 4 (y_hi: 2, y_lo: 2; y = y_hi * 2 + y_lo), z: 4, core: 2. Of those that a mesh axis runs over, the one named last changes fastest.
Arguments:
- users: bfloat16 [4096, 256], P('user'), may hold values from -40 to 40
- catalog_vectors: bfloat16 [262144, 256], P('item'), may hold values from -8 to 8
- positives: int32 [4096], P('user'), may hold values from 0 to 262143
Outputs:
- loss: float32 [4096], P('user')
- user_grad: bfloat16 [4096, 256], P('user')
- item_grad: bfloat16 [262144, 256], P(('item', 'user'))
All inputs are finite; a program needn't handle non-finite values.
Results may differ from a plain program's by a relative error of at most 0.0034.
Values may be sent and summed in bfloat16 or wider, within the bound.
No kernel may reach another device: no remote copies, remote signals or barrier semaphores. Data moves between devices by JAX's collectives and lax.ppermute only.
A program may use at most 64 MiB of HBM per device.

v0:
```python
import math

import jax
import jax.numpy as jnp
from jax import lax
from jax.sharding import PartitionSpec as P

sharpness_divisor = 4.0


def per_device(users, catalog_vectors, positives):
    rows = users.shape[0]
    count = catalog_vectors.shape[0]
    width = catalog_vectors.shape[1]
    block = math.gcd(count, 2048)
    nblock = count // block
    offset = lax.axis_index("item") * count
    local_pos = positives - offset
    stacked = catalog_vectors.reshape(nblock, block, width)
    numbers = jnp.arange(nblock, dtype=jnp.int32)
    columns = lax.broadcasted_iota(jnp.int32, (rows, block), 1)

    def scores_of(piece, number):
        raw_affinity_scores = lax.dot_general(
            users, piece, (((1,), (1,)), ((), ())), preferred_element_type=jnp.float32
        )
        positive_indicator = columns + number * block == local_pos[:, None]
        return (raw_affinity_scores / sharpness_divisor, positive_indicator)

    def first_pass(carry, inputs):
        piece, number = inputs
        run_max, run_sum, run_pos = carry
        affinity_grid, positive_indicator = scores_of(piece, number)
        new_max = jnp.maximum(run_max, jnp.max(affinity_grid, axis=1))
        run_sum = run_sum * jnp.exp(run_max - new_max) + jnp.sum(
            jnp.exp(affinity_grid - new_max[:, None]), axis=1
        )
        run_pos = run_pos + jnp.sum(jnp.where(positive_indicator, affinity_grid, 0.0), axis=1)
        return ((new_max, run_sum, run_pos), None)

    start = (
        jnp.full((rows,), -jnp.inf, jnp.float32),
        jnp.zeros((rows,), jnp.float32),
        jnp.zeros((rows,), jnp.float32),
    )
    (local_max, local_sum, local_hit), _ = lax.scan(first_pass, start, (stacked, numbers))
    global_max = lax.pmax(local_max, "item")
    global_sum, global_hit = lax.psum(
        (local_sum * jnp.exp(local_max - global_max), local_hit), "item"
    )
    lse = global_max + jnp.log(global_sum)
    loss = lse - global_hit

    def second_pass(accumulated_sum, inputs):
        piece, number = inputs
        affinity_grid, positive_indicator = scores_of(piece, number)
        normalized_probabilities = (
            jnp.exp(affinity_grid - lse[:, None]) - positive_indicator.astype(jnp.float32)
        ).astype(jnp.bfloat16)
        accumulated_sum = accumulated_sum + jnp.dot(
            normalized_probabilities, piece, preferred_element_type=jnp.float32
        )
        item_part = (
            lax.dot_general(
                normalized_probabilities,
                users,
                (((0,), (0,)), ((), ())),
                preferred_element_type=jnp.float32,
            )
            / sharpness_divisor
        )
        return (accumulated_sum, item_part)

    accumulated_sum, item_parts = lax.scan(
        second_pass, jnp.zeros((rows, width), jnp.float32), (stacked, numbers)
    )
    item_grad = lax.psum_scatter(
        item_parts.reshape(count, width), "user", scatter_dimension=0, tiled=True
    ).astype(jnp.bfloat16)
    customer_cost_addend = accumulated_sum / sharpness_divisor
    user_grad = lax.psum(customer_cost_addend, "item").astype(jnp.bfloat16)
    return (loss, user_grad, item_grad)


def solution(mesh):
    in_specs = (P("user", None), P("item", None), P("user"))
    out_specs = (P("user"), P("user", None), P(("item", "user"), None))
    return jax.shard_map(
        per_device, mesh=mesh, in_specs=in_specs, out_specs=out_specs, check_vma=False
    )
```

profile of v0, /device:TPU:0, one launch (start us, length us, event | category | flops | bytes accessed | tf_op | source)
XLA Modules:
  0.0 499.4 jit_solution(3598270233500023841)
XLA Ops:
  7.3 0.7 broadcast_subtract_fusion
  8.0 47.3 %while.28 = (s32[]{:T(128)}, f32[1024]{0:T(1024)S(1)}, f32[1024]{0:T(1024)S(1)}, f32[1024]{0:T(1024)S(1)}, bf16[4,2048,256]{2,1,0:T(8,128)(2,1)}, /*index=5*/bf1...) while((s32[]{:T(128)}, f32[1024]{0:T(1024)S(1)}, ...), condition=%wide.region_4.5_spmd.clone, body=%wide.region_0.4_spmd.clone.sunk | while | flops 1092622336 | bytes 18424468 | solution.py:46
  8.0 5.9 %multiply_reduce_fusion.2 = (f32[1024]{0:T(1024)S(1)}, f32[2048,1024]{1,0:T(8,128)}) fusion(bf16[1024,256]{1,0:T(8,128)(2,1)} %get-tuple-element.340, bf16[4,2048,256]{2,1,0:T(8,128)(2,1)} %get-tuple-element.339, s32[]{:T(128)} %get-tuple-element.324), kind=kOutput, calls=%fused_computation.9.clone.1 | convolution fusion | flops 1077935104 | bytes 9966080 | tf_op jit(solution)/shard_map/while/body/eval_jaxpr/dot_general | solution.py:24
  15.1 4.7 fusion.39
  19.8 5.9 %multiply_reduce_fusion.2 = (f32[1024]{0:T(1024)S(1)}, f32[2048,1024]{1,0:T(8,128)}) fusion(bf16[1024,256]{1,0:T(8,128)(2,1)} %get-tuple-element.340, bf16[4,2048,256]{2,1,0:T(8,128)(2,1)} %get-tuple-element.339, s32[]{:T(128)} %get-tuple-element.324), kind=kOutput, calls=%fused_computation.9.clone.1 | convolution fusion | flops 1077935104 | bytes 9966080 | tf_op jit(solution)/shard_map/while/body/eval_jaxpr/dot_general | solution.py:24
  26.9 4.7 fusion.39
  31.6 5.9 %multiply_reduce_fusion.2 = (f32[1024]{0:T(1024)S(1)}, f32[2048,1024]{1,0:T(8,128)}) fusion(bf16[1024,256]{1,0:T(8,128)(2,1)} %get-tuple-element.340, bf16[4,2048,256]{2,1,0:T(8,128)(2,1)} %get-tuple-element.339, s32[]{:T(128)} %get-tuple-element.324), kind=kOutput, calls=%fused_computation.9.clone.1 | convolution fusion | flops 1077935104 | bytes 9966080 | tf_op jit(solution)/shard_map/while/body/eval_jaxpr/dot_general | solution.py:24
  38.7 4.7 fusion.39
  43.5 5.9 %multiply_reduce_fusion.2 = (f32[1024]{0:T(1024)S(1)}, f32[2048,1024]{1,0:T(8,128)}) fusion(bf16[1024,256]{1,0:T(8,128)(2,1)} %get-tuple-element.340, bf16[4,2048,256]{2,1,0:T(8,128)(2,1)} %get-tuple-element.339, s32[]{:T(128)} %get-tuple-element.324), kind=kOutput, calls=%fused_computation.9.clone.1 | convolution fusion | flops 1077935104 | bytes 9966080 | tf_op jit(solution)/shard_map/while/body/eval_jaxpr/dot_general | solution.py:24
  50.6 4.7 fusion.39
  55.3 97.8 %pmax.7 = f32[1024]{0:T(1024)S(1)} all-reduce(f32[1024]{0:T(1024)S(1)} %get-tuple-element.100), channel_id=1, replica_groups=mesh['user'=4,'item'=32] {'item'}, use_global_device_ids=true, to_apply=%region_5.6 | all-reduce | flops 1024 | bytes 8192 | tf_op jit(solution)/shard_map/pmax | solution.py:47
  153.1 88.9 %psum.21 = f32[1024]{0:T(1024)S(1)} all-reduce(f32[1024]{0:T(1024)S(1)} %exponential_multiply_fusion), channel_id=1, replica_groups=mesh['user'=4,'item'=32] {'item'}, use_global_device_ids=true, to_apply=%region_6.7 | all-reduce | flops 1024 | bytes 8192 | tf_op jit(solution)/shard_map/psum | solution.py:48
  242.0 54.9 %while.29 = (s32[]{:T(128)}, f32[1024,256]{1,0:T(8,128)S(1)}, f32[4,2048,256]{2,1,0:T(8,128)}, bf16[4,2048,256]{2,1,0:T(8,128)(2,1)}, bf16[1024,256]{1,0:T(8,128...) while((s32[]{:T(128)}, f32[1024,256]{1,0:T(8,128)S(1)}, ...), condition=%wide.region_9.10_spmd.clone, body=%wide.region_8.9_spmd.clone.sunk | while | flops 3236954112 | bytes 38807748 | solution.py:74
  243.3 3.7 fusion.46
  247.0 2.0 copy-done.1
  249.0 2.6 fusion.47
  251.6 4.1 convolution_add_fusion.2
  257.0 3.7 fusion.46
  260.8 2.0 copy-done.1
  262.7 2.6 fusion.47
  265.3 4.1 convolution_add_fusion.2
  270.7 3.7 fusion.46
  274.4 2.0 copy-done.1
  276.4 2.6 fusion.47
  279.0 4.1 convolution_add_fusion.2
  284.4 3.7 fusion.46
  288.2 2.0 copy-done.1
  290.2 2.6 fusion.47
  292.8 4.1 convolution_add_fusion.2
  297.0 192.2 %all-reduce.2 = (f32[1024]{0:T(1024)S(1)}, bf16[1024,256]{1,0:T(8,128)(2,1)}) all-reduce(f32[1024]{0:T(1024)S(1)} %get-tuple-element.102, f32[1024,256]{1,0:T(8,128)S(1)} %broadcast_multiply_fusion), channel_id=1, replica_groups=mesh['user'=4,'item'=32] {'item'}, use_global_device_ids=true, to_apply=%region_7.8 | all-reduce | flops 263168 | bytes 1581056 | tf_op jit(solution)/shard_map/psum | solution.py:48
  489.3 0.6 sub.38
  489.9 2.7 convert_element_type.13
  (45 shorter events, 4.9 us)
Async XLA Ops:
  7.2 482.7 %reduce-scatter.2.cloned.1.call-start = ((), (), s32[]{:S(2)}) async-start(), calls=%async_computation.1 | async-start | bytes 10485760 | tf_op jit(solution)/shard_map/reduce_scatter | solution.py:77
  243.3 5.7 %copy-start = (bf16[1024,256]{1,0:T(8,128)(2,1)S(1)}, bf16[1024,256]{1,0:T(8,128)(2,1)}, u32[]{:S(2)}) copy-start(bf16[1024,256]{1,0:T(8,128)(2,1)} %get-tuple-element.372) | copy-start | bytes 1572868 | tf_op jit(solution)/shard_map/while
  247.0 2.0 copy-start.1
  257.0 5.7 %copy-start = (bf16[1024,256]{1,0:T(8,128)(2,1)S(1)}, bf16[1024,256]{1,0:T(8,128)(2,1)}, u32[]{:S(2)}) copy-start(bf16[1024,256]{1,0:T(8,128)(2,1)} %get-tuple-element.372) | copy-start | bytes 1572868 | tf_op jit(solution)/shard_map/while
  260.7 2.0 copy-start.1
  270.7 5.7 %copy-start = (bf16[1024,256]{1,0:T(8,128)(2,1)S(1)}, bf16[1024,256]{1,0:T(8,128)(2,1)}, u32[]{:S(2)}) copy-start(bf16[1024,256]{1,0:T(8,128)(2,1)} %get-tuple-element.372) | copy-start | bytes 1572868 | tf_op jit(solution)/shard_map/while
  274.4 2.0 copy-start.1
  284.4 5.7 %copy-start = (bf16[1024,256]{1,0:T(8,128)(2,1)S(1)}, bf16[1024,256]{1,0:T(8,128)(2,1)}, u32[]{:S(2)}) copy-start(bf16[1024,256]{1,0:T(8,128)(2,1)} %get-tuple-element.372) | copy-start | bytes 1572868 | tf_op jit(solution)/shard_map/while
  288.2 2.0 copy-start.1
Sparse Core Ops, SparseCore 0:
  297.1 85.7 reduce-scatter.1
where the time goes:
time: 500 us; the launch traced here: 499 us
  blocking collectives  379 us (76%)
  matrix products  65.3 us (13%)
  other arithmetic  22.9 us (5%)
  between operations  14.1 us (3%)
  local copies, waits for them, and re-layouts  12.6 us (3%)
  loops' own time  5.52 us (1%)
    psum x2, blocking collectives, per_device(): lax.psum((local_sum * jnp.exp(local_max - global_max), local_hit), 'item')  281 us
    pmax x1, blocking collectives, per_device(): global_max = lax.pmax(local_max, 'item')  97.8 us
    dot_general x8, matrix products, scores_of(): lax.dot_general(users, piece, (((1,), (1,)), ((), ())), preferred_element...  38.3 us
    reduce_sum x4, other arithmetic, first_pass(): jnp.sum(jnp.where(positive_indicator, affinity_grid, 0.0), axis=1)  18.8 us
    dot_general x4, matrix products, second_pass(): jnp.dot(normalized_probabilities, piece, preferred_element_type=jnp.float32)  16.5 us
    dot_general x4, matrix products, second_pass(): lax.dot_general(normalized_probabilities, users, (((0,), (0,)), ((), ()))...  10.4 us
  transfers between devices with their start and end apart: 1, of which 0 were waited for; matrix products, arithmetic and copies ran while one was open for 0% of the time, Pallas kernels for 0%

commit v1 on v0

v1 whole, which is shorter than its diff:
```python
import functools
import math

import jax
import jax.numpy as jnp
from jax import lax
from jax.experimental import pallas as pl
from jax.experimental.pallas import tpu as pltpu
from jax.sharding import Mesh
from jax.sharding import PartitionSpec as P

sharpness_divisor = 4.0
SCALE = math.log2(math.e) / sharpness_divisor
NT = (((1,), (1,)), ((), ()))
ITEM = ("z", "y_hi", "x")
USER = ("y_lo", "core")


def exp_of(x):
    return jnp.exp2(x * SCALE)


def pass1_kernel(tile, rb, pos_ref, u_ref, cat_ref, acc_ref, hit_ref, st_ref, c_ref, m_ref, l_ref, sem):
    rows = u_ref.shape[0]
    count, width = cat_ref.shape
    n = count // tile
    copies = []
    for i in range(n):
        part = pl.ds(i * tile, tile)
        copies.append(pltpu.make_async_copy(cat_ref.at[part], c_ref.at[part], sem.at[i]))
        copies[-1].start()
    acc_ref[...] = jnp.zeros_like(acc_ref)
    hit_ref[...] = jnp.zeros_like(hit_ref)
    m_ref[...] = jnp.full_like(m_ref, -1e38)
    l_ref[...] = jnp.zeros_like(l_ref)
    for i in range(n):
        copies[i].wait()
        c = c_ref[i * tile : (i + 1) * tile]
        for b in range(rows // rb):
            sl = slice(b * rb, (b + 1) * rb)
            r = lax.dot_general(u_ref[sl], c, NT, preferred_element_type=jnp.float32)
            m_old = m_ref[sl]
            m_new = jnp.maximum(m_old, jnp.max(r, axis=1, keepdims=True))
            alpha = exp_of(m_old - m_new)
            m_ref[sl] = m_new
            total = l_ref[sl] * alpha
            ps = []
            for j in range(tile // 128):
                p = exp_of(r[:, j * 128 : (j + 1) * 128] - m_new)
                total = total + p
                ps.append(p.astype(jnp.bfloat16))
            l_ref[sl] = total
            wide = jnp.concatenate([alpha] * (width // 128), axis=1)
            acc_ref[sl] = acc_ref[sl] * wide + jnp.dot(
                jnp.concatenate(ps, axis=1), c, preferred_element_type=jnp.float32
            )

    @pl.loop(0, rows // 8)
    def _(g):
        here = [pos_ref[g * 8 + j] for j in range(8)]
        mine = [(h >= 0) & (h < count) for h in here]
        some = functools.reduce(jnp.logical_or, mine)

        @pl.when(some)
        def _():
            for j in range(8):

                @pl.when(mine[j])
                def _():
                    start = pl.multiple_of((here[j] >> 4) << 4, 16)
                    group = c_ref[pl.ds(start, 16), :].astype(jnp.float32)
                    inside = lax.broadcasted_iota(jnp.int32, group.shape, 0) == (here[j] & 15)
                    row = jnp.sum(jnp.where(inside, group, 0.0), axis=0, keepdims=True)
                    hit_ref[pl.ds(g * 8 + j, 1), :] = row

    for b in range(rows // 128):
        sl = slice(b * 128, (b + 1) * 128)
        total = jnp.sum(l_ref[sl], axis=1, keepdims=True)
        hit_score = jnp.sum(hit_ref[sl] * u_ref[sl].astype(jnp.float32), axis=1, keepdims=True)
        st_ref[0:1, sl] = m_ref[sl].T[0:1]
        st_ref[1:2, sl] = jnp.broadcast_to(total, (128, 128)).T[0:1]
        st_ref[2:3, sl] = jnp.broadcast_to(hit_score, (128, 128)).T[0:1]


def pass1(users, catalog, local_pos, tile=2048, rb=256):
    rows, width = users.shape
    count = catalog.shape[0]
    vmem = pl.BlockSpec(memory_space=pltpu.VMEM)
    return pl.pallas_call(
        functools.partial(pass1_kernel, tile, rb),
        in_specs=[pl.BlockSpec(memory_space=pltpu.SMEM), vmem, pl.BlockSpec(memory_space=pl.ANY)],
        out_specs=[vmem, vmem, vmem],
        out_shape=[
            jax.ShapeDtypeStruct((rows, width), jnp.float32),
            jax.ShapeDtypeStruct((rows, width), jnp.float32),
            jax.ShapeDtypeStruct((3, rows), jnp.float32),
        ],
        scratch_shapes=[
            pltpu.VMEM((count, width), jnp.bfloat16),
            pltpu.VMEM((rows, 128), jnp.float32),
            pltpu.VMEM((rows, 128), jnp.float32),
            pltpu.SemaphoreType.DMA((count // tile,)),
        ],
        cost_estimate=pl.CostEstimate(
            flops=4 * rows * count * width, bytes_accessed=2 * count * width, transcendentals=rows * count
        ),
        name="pass1",
    )(local_pos, users, catalog)


def pass2_kernel(tile, base_ref, c_ref, *refs):
    us, stats, out_ref = refs[:4], refs[4:8], refs[-1]
    first = base_ref[1] + pl.program_id(0) * tile
    c = c_ref[...]
    item = (lax.broadcasted_iota(jnp.int32, (tile, 128), 0) + first).astype(jnp.float32)
    total = jnp.zeros((tile, c.shape[1]), jnp.float32)
    for u_ref, st_ref in zip(us, stats):
        u = u_ref[...]
        r = lax.dot_general(c, u, NT, preferred_element_type=jnp.float32)
        ws = []
        for j in range(u.shape[0] // 128):
            sl = slice(j * 128, (j + 1) * 128)
            w = exp_of(r[:, sl] - st_ref[0:1, sl])
            w = jnp.where(st_ref[1:2, sl] == item, w - 1.0, w)
            ws.append(w.astype(jnp.bfloat16))
        total = total + jnp.dot(jnp.concatenate(ws, axis=1), u, preferred_element_type=jnp.float32)
    out_ref[...] = (total / sharpness_divisor).astype(out_ref.dtype)


def pass2(base, catalog, us, stats, items, part, parts, before, tile=512):
    rows, width = us[0].shape
    n = items // tile // parts
    lead = part * n
    resident = lambda i, b: (0, 0)
    in_specs = [pl.BlockSpec((tile, width), lambda i, b: (b[0] * (items // tile) + lead + i, 0))]
    in_specs += [pl.BlockSpec((rows, width), resident)] * 4
    in_specs += [pl.BlockSpec((2, rows), resident)] * 4
    args = [base + jnp.array([0, lead * tile], jnp.int32), catalog, *us, *stats]
    aliases = {}
    if before is not None:
        in_specs.append(pl.BlockSpec(memory_space=pl.ANY))
        aliases = {len(args): 0}
        args.append(before)
    return pl.pallas_call(
        functools.partial(pass2_kernel, tile),
        grid_spec=pltpu.PrefetchScalarGridSpec(
            num_scalar_prefetch=1,
            grid=(n,),
            in_specs=in_specs,
            out_specs=pl.BlockSpec((tile, width), lambda i, b: (lead + i, 0)),
        ),
        out_shape=jax.ShapeDtypeStruct((items, width), jnp.bfloat16),
        input_output_aliases=aliases,
        cost_estimate=pl.CostEstimate(
            flops=4 * rows * 4 * (items // parts) * width,
            bytes_accessed=2 * rows * 4 * width,
            transcendentals=rows * 4 * items // parts,
        ),
        name=f"pass2_{part}",
    )(*args)


def swap(x, axis, size, k):
    return lax.ppermute(x, axis, [(i, i ^ k) for i in range(size)])


def tree(a):
    return (a[0] + a[1]) + (a[2] + a[3]) if len(a) == 4 else a[0] + a[1]


def merge_stats(parts):
    top = functools.reduce(jnp.maximum, [p[0] for p in parts])
    total = tree([p[1] * exp_of(p[0] - top) for p in parts])
    return jnp.stack([top, total, tree([p[2] for p in parts])])


def gather_chunks(x, axis, size):
    mine = lax.axis_index(axis)
    got = jnp.stack([x] + [swap(x, axis, size, k) for k in range(1, size)])
    pieces = [lax.dynamic_index_in_dim(got, mine ^ k, keepdims=False) for k in range(size)]
    return jnp.concatenate(pieces, axis=0)


def scatter_sum(x, axis, size, dtype):
    mine = lax.axis_index(axis)
    chunks = x.reshape(size, x.shape[0] // size, x.shape[1])
    own = lax.dynamic_index_in_dim(chunks, mine, keepdims=False)
    others = []
    for k in range(1, size):
        piece = lax.dynamic_index_in_dim(chunks, mine ^ k, keepdims=False).astype(dtype)
        others.append(swap(piece, axis, size, k).astype(jnp.float32))
    return tree([own] + others)


def per_device(users, catalog, positives):
    rows = users.shape[0]
    count = catalog.shape[0]
    items = count // 4
    shard = lax.axis_index(ITEM)
    member = lax.axis_index(USER)
    us = [users] + [swap(users, USER, 4, k) for k in (1, 2, 3)]
    partial, hits, stats = pass1(users, catalog, positives - shard * count)
    all_stats = stats
    for axis, size in (("x", 4), ("z", 4), ("y_hi", 2)):
        all_stats = merge_stats([all_stats] + [swap(all_stats, axis, size, k) for k in range(1, size)])
    lse = all_stats[0] / sharpness_divisor + jnp.log(all_stats[1])
    loss = lse - all_stats[2] / sharpness_divisor
    lse4 = lse * sharpness_divisor

    mine = jnp.stack([lse4, positives.astype(jnp.float32)])
    infos = [mine] + [swap(mine, USER, 4, k) for k in (1, 2, 3)]
    base = jnp.stack([member, shard * count + member * items])
    item_grad = None
    parts = 4
    for part in range(parts):
        item_grad = pass2(base, catalog, us, infos, items, part, parts, item_grad)

    weight = exp_of(stats[0] - lse4)
    value = (partial * weight[:, None] - hits) / sharpness_divisor
    value = scatter_sum(value, "x", 4, jnp.bfloat16)
    value = scatter_sum(value, "z", 4, jnp.float32)
    value = tree([value, swap(value, "y_hi", 2, 1)]).astype(jnp.bfloat16)
    value = gather_chunks(value, "z", 4)
    user_grad = gather_chunks(value, "x", 4)
    return loss, user_grad, item_grad


def solution(mesh):
    grid = Mesh(mesh.devices.reshape(2, 2, 4, 2, 4), USER + ITEM)
    return jax.shard_map(
        per_device,
        mesh=grid,
        in_specs=(P(USER, None), P(ITEM, None), P(USER)),
        out_specs=(P(USER), P(USER, None), P(ITEM + USER, None)),
        check_vma=False,
    )
```

time: 500 us -> 136 us (0.27)
  blocking collectives: 379 us -> 0 us
  matrix products: 65.3 us -> 0 us
  Pallas kernels: 0 us -> 47.1 us
  waiting for transfers between devices: 0.02 us -> 40.7 us
  starting transfers between devices: 0.04 us -> 36.4 us
  other arithmetic: 22.9 us -> 7.03 us
  between operations: 14.1 us -> 0.88 us
  local copies, waits for them, and re-layouts: 12.6 us -> 2.63 us
  loops' own time: 5.52 us -> 0 us
    psum x2 -> x0, blocking collectives: 281 us -> none  [per_device(): lax.psum((local_sum * jnp.exp(local_max - global_max), local_hit), 'item')]
    pmax x1 -> x0, blocking collectives: 97.8 us -> none  [per_device(): global_max = lax.pmax(local_max, 'item')]
    dot_general x16 -> x0, matrix products: 65.3 us -> none  [the longest x8 38.3 us: scores_of(): lax.dot_general(users, piece, (((1,), (1,)), ((), ())), preferred_element...]
    pallas_call x0 -> x5, Pallas kernels: none -> 47.1 us  [the longest x4 24.1 us: pass2(): pl.pallas_call(functools.partial(pass2_kernel, tile), grid_spec=pltpu.Pre...]
    ppermute x0 -> x26, waiting for transfers between devices: none -> 40.7 us  [swap(): return lax.ppermute(x, axis, [(i, i ^ k) for i in range(size)])]
    ppermute x0 -> x26, starting transfers between devices: none -> 36.4 us  [swap(): return lax.ppermute(x, axis, [(i, i ^ k) for i in range(size)])]
    reduce_sum x4 -> x0, other arithmetic: 18.8 us -> none  [first_pass(): jnp.sum(jnp.where(positive_indicator, affinity_grid, 0.0), axis=1)]
    while x20 -> x0, local copies, waits for them, and re-layouts: 7.91 us -> none
  transfers between devices with their start and end apart: 1 -> 26, of which waited for: 0 -> 16; matrix products, arithmetic and copies ran while one was open for 0% -> 3% of each run, Pallas kernels for 0% -> 0%
where the time goes in v1:
time: 136 us; the launch traced here: 135 us
  Pallas kernels  47.1 us (35%)
  waiting for transfers between devices  40.7 us (30%)
  starting transfers between devices  36.4 us (27%)
  other arithmetic  7.03 us (5%)
  local copies, waits for them, and re-layouts  2.63 us (2%)
    ppermute x26, waiting for transfers between devices, swap(): return lax.ppermute(x, axis, [(i, i ^ k) for i in range(size)])  40.7 us
    ppermute x26, starting transfers between devices, swap(): return lax.ppermute(x, axis, [(i, i ^ k) for i in range(size)])  36.4 us
    pallas_call x4, Pallas kernels, pass2(): pl.pallas_call(functools.partial(pass2_kernel, tile), grid_spec=pltpu.Pre...  24.1 us
    pallas_call x1, Pallas kernels, pass1(): pl.pallas_call(functools.partial(pass1_kernel, tile, rb), in_specs=[pl.Bl...  23 us
  transfers between devices with their start and end apart: 26, of which 16 were waited for; matrix products, arithmetic and copies ran while one was open for 3% of the time, Pallas kernels for 0%

profile of v1, /device:TPU:0, one launch (start us, length us, event | category | flops | bytes accessed | tf_op | source)
XLA Modules:
  0.0 134.8 jit_solution(15826412811762666990)
XLA Ops:
  0.6 1.4 %fusion.9 = (f32[1024]{0:T(1024)S(1)}, s32[1024]{0:T(1024)}) fusion(s32[1024]{0:T(1024)} %param.9, s32[]{:T(128)S(6)} %mul.159), kind=kLoop, calls=%fused_computation.53 | loop fusion | flops 2048 | bytes 12292 | tf_op jit(solution)/shard_map/convert_element_type | solution.py:210
  2.0 23.0 %pass1.1 = (f32[1024,256]{1,0:T(8,128)}, f32[1024,256]{1,0:T(8,128)}, f32[3,1024]{1,0:T(4,128)}) custom-call(s32[1024]{0:T(1024)} %get-tuple-element.53.pos_ref, bf16[1024,256]{1,0:T(8,128)(2,1)} %refs_0_.7, bf16[8192,256]{1,0:T(8,128)(2,1)} %c_ref.7), custom_call_target="tpu_custom_call" | custom-call | flops 8589934592 | bytes 4194304 | tf_op jit(solution)/shard_map/pass1/pallas_call | solution.py:89
  25.0 2.7 %collective-permute-start.2 = (f32[3,1024]{1,0:T(4,128)}, f32[3,1024]{1,0:T(4,128)S(1)}, u32[]{:S(2)}, u32[]{:S(2)}) collective-permute-start(f32[3,1024]{1,0:T(4,128)} %get-tuple-element.6), channel_id=1, source_target_pairs={{0,3},{1,2},{2,1},{3,0},{4,7},{5,6},{6,5},{7,4},{8,11},{9,10},{10,... | collective-permute-start | bytes 36872 | tf_op jit(solution)/shard_map/ppermute | solution.py:164
  29.2 1.1 collective-permute-done.2
  30.3 2.9 %collective-permute-done.1 = f32[3,1024]{1,0:T(4,128)S(1)} collective-permute-done((f32[3,1024]{1,0:T(4,128)}, f32[3,1024]{1,0:T(4,128)S(1)}, u32[]{:S(2)}, u32[]{:S(2)}) %collective-permute-start.1) | collective-permute-done | bytes 12320 | tf_op jit(solution)/shard_map/ppermute | solution.py:164
  34.1 4.2 %collective-permute-start.5 = (f32[3,1024]{1,0:T(4,128)S(1)}, f32[3,1024]{1,0:T(4,128)S(1)}, u32[]{:S(2)}, u32[]{:S(2)}) collective-permute-start(f32[3,1024]{1,0:T(4,128)S(1)} %pad_maximum_fusion.4), channel_id=1, source_target_pairs={{0,24},{8,16},{16,8},{24,0},{1,25},{9,17},{17,9},{25,1},{2,26},{10... | collective-permute-start | bytes 36872 | tf_op jit(solution)/shard_map/ppermute | solution.py:164
  40.0 3.5 %collective-permute-done.4 = f32[3,1024]{1,0:T(4,128)S(1)} collective-permute-done((f32[3,1024]{1,0:T(4,128)S(1)}, f32[3,1024]{1,0:T(4,128)S(1)}, u32[]{:S(2)}, u32[]{:S(2)}) %collective-permute-start.4) | collective-permute-done | bytes 12320 | tf_op jit(solution)/shard_map/ppermute | solution.py:164
  43.7 4.0 %collective-permute-start.6 = (f32[3,1024]{1,0:T(4,128)S(1)}, f32[3,1024]{1,0:T(4,128)S(1)}, u32[]{:S(2)}, u32[]{:S(2)}) collective-permute-start(f32[3,1024]{1,0:T(4,128)S(1)} %pad_maximum_fusion.5), channel_id=1, source_target_pairs={{0,4},{4,0},{1,5},{5,1},{2,6},{6,2},{3,7},{7,3},{8,12},{12,8},{9,1... | collective-permute-start | bytes 36872 | tf_op jit(solution)/shard_map/ppermute | solution.py:164
  48.4 1.0 collective-permute-done.6
  49.5 1.7 %subtract_multiply_fusion = f32[1024,256]{1,0:T(8,128)S(1)} fusion(f32[1024,256]{1,0:T(8,128)} %get-tuple-element.8, f32[1024,256]{1,0:T(8,128)} %get-tuple-element.7, f32[1024]{0:T(1024)S(1)} %get-tuple-element.11), kind=kLoop, calls=%fused_computation | loop fusion | flops 786432 | bytes 3149824 | tf_op jit(solution)/shard_map/div | solution.py:219
  52.2 1.3 collective-permute-start.8
  53.5 2.0 %collective-permute-start.7 = (bf16[256,256]{1,0:T(8,128)(2,1)S(1)}, bf16[256,256]{1,0:T(8,128)(2,1)S(1)}, u32[]{:S(2)}, u32[]{:S(2)}) collective-permute-start(bf16[256,256]{1,0:T(8,128)(2,1)S(1)} %get-tuple-element.17), channel_id=1, source_target_pairs={{0,1},{1,0},{2,3},{3,2},{4,5},{5,4},{6,7},{7,6},{8,9},{9,8},{10,11... | collective-permute-start | bytes 393224 | tf_op jit(solution)/shard_map/ppermute | solution.py:164
  55.5 3.5 %collective-permute-done.9 = bf16[256,256]{1,0:T(8,128)(2,1)S(1)} collective-permute-done((bf16[256,256]{1,0:T(8,128)(2,1)S(1)}, bf16[256,256]{1,0:T(8,128)(2,1)S(1)}, u32[]{:S(2)}, u32[]{:S(2)}) %collective-permute-start.9) | collective-permute-done | bytes 131104 | tf_op jit(solution)/shard_map/ppermute | solution.py:164
  60.0 2.2 %collective-permute-start.11 = (f32[64,256]{1,0:T(8,128)S(1)}, f32[64,256]{1,0:T(8,128)S(1)}, u32[]{:S(2)}, u32[]{:S(2)}) collective-permute-start(f32[64,256]{1,0:T(8,128)S(1)} %get-tuple-element.25), channel_id=1, source_target_pairs={{0,16},{8,24},{16,0},{24,8},{1,17},{9,25},{17,1},{25,9},{2,18},{10... | collective-permute-start | bytes 196616 | tf_op jit(solution)/shard_map/ppermute | solution.py:164
  62.2 2.5 %collective-permute-start.12 = (f32[64,256]{1,0:T(8,128)S(1)}, f32[64,256]{1,0:T(8,128)S(1)}, u32[]{:S(2)}, u32[]{:S(2)}) collective-permute-start(f32[64,256]{1,0:T(8,128)S(1)} %get-tuple-element.24), channel_id=1, source_target_pairs={{0,24},{8,16},{16,8},{24,0},{1,25},{9,17},{17,9},{25,1},{2,26},{10... | collective-permute-start | bytes 196616 | tf_op jit(solution)/shard_map/ppermute | solution.py:164
  64.7 1.2 collective-permute-done.11
  65.9 1.8 %collective-permute-done.12 = f32[64,256]{1,0:T(8,128)S(1)} collective-permute-done((f32[64,256]{1,0:T(8,128)S(1)}, f32[64,256]{1,0:T(8,128)S(1)}, u32[]{:S(2)}, u32[]{:S(2)}) %collective-permute-start.12) | collective-permute-done | bytes 65568 | tf_op jit(solution)/shard_map/ppermute | solution.py:164
  67.7 3.6 %collective-permute-start.13 = (f32[64,256]{1,0:T(8,128)S(1)}, f32[64,256]{1,0:T(8,128)S(1)}, u32[]{:S(2)}, u32[]{:S(2)}) collective-permute-start(f32[64,256]{1,0:T(8,128)S(1)} %fusion.4), channel_id=1, source_target_pairs={{0,4},{4,0},{1,5},{5,1},{2,6},{6,2},{3,7},{7,3},{8,12},{12,8},{9,1... | collective-permute-start | bytes 196616 | tf_op jit(solution)/shard_map/ppermute | solution.py:164
  71.3 2.2 %collective-permute-done.13 = f32[64,256]{1,0:T(8,128)S(1)} collective-permute-done((f32[64,256]{1,0:T(8,128)S(1)}, f32[64,256]{1,0:T(8,128)S(1)}, u32[]{:S(2)}, u32[]{:S(2)}) %collective-permute-start.13) | collective-permute-done | bytes 65568 | tf_op jit(solution)/shard_map/ppermute | solution.py:164
  73.5 2.6 %collective-permute-start.16 = (bf16[64,256]{1,0:T(8,128)(2,1)S(1)}, bf16[64,256]{1,0:T(8,128)(2,1)S(1)}, u32[]{:S(2)}, u32[]{:S(2)}) collective-permute-start(bf16[64,256]{1,0:T(8,128)(2,1)S(1)} %add_convert_fusion), channel_id=1, source_target_pairs={{0,24},{8,16},{16,8},{24,0},{1,25},{9,17},{17,9},{25,1},{2,26},{10... | collective-permute-start | bytes 98312 | tf_op jit(solution)/shard_map/ppermute | solution.py:164
  77.7 1.0 collective-permute-done.16
  78.8 2.8 %collective-permute-done.15 = bf16[64,256]{1,0:T(8,128)(2,1)S(1)} collective-permute-done((bf16[64,256]{1,0:T(8,128)(2,1)S(1)}, bf16[64,256]{1,0:T(8,128)(2,1)S(1)}, u32[]{:S(2)}, u32[]{:S(2)}) %collective-permute-start.15) | collective-permute-done | bytes 32800 | tf_op jit(solution)/shard_map/ppermute | solution.py:164
  81.6 1.4 %collective-permute-start.19 = (bf16[256,256]{1,0:T(8,128)(2,1)S(1)}, bf16[256,256]{1,0:T(8,128)(2,1)S(1)}, u32[]{:S(2)}, u32[]{:S(2)}) collective-permute-start(bf16[256,256]{1,0:T(8,128)(2,1)S(1)} %get-tuple-element.28), channel_id=1, source_target_pairs={{0,3},{1,2},{2,1},{3,0},{4,7},{5,6},{6,5},{7,4},{8,11},{9,10},{10,... | collective-permute-start | bytes 393224 | tf_op jit(solution)/shard_map/ppermute | solution.py:164
  83.0 1.6 %collective-permute-start.21 = (bf16[1024,256]{1,0:T(8,128)(2,1)S(1)}, bf16[1024,256]{1,0:T(8,128)(2,1)S(1)}, u32[]{:S(2)}, u32[]{:S(2)}) collective-permute-start(bf16[1024,256]{1,0:T(8,128)(2,1)S(1)} %copy-done), channel_id=1, source_target_pairs={{0,64},{32,96},{64,0},{96,32},{1,65},{33,97},{65,1},{97,33},{2,66}... | collective-permute-start | bytes 1572872 | tf_op jit(solution)/shard_map/ppermute | solution.py:164
  85.5 1.4 %collective-permute-start.18 = (bf16[256,256]{1,0:T(8,128)(2,1)S(1)}, bf16[256,256]{1,0:T(8,128)(2,1)S(1)}, u32[]{:S(2)}, u32[]{:S(2)}) collective-permute-start(bf16[256,256]{1,0:T(8,128)(2,1)S(1)} %get-tuple-element.28), channel_id=1, source_target_pairs={{0,2},{1,3},{2,0},{3,1},{4,6},{5,7},{6,4},{7,5},{8,10},{9,11},{10,... | collective-permute-start | bytes 393224 | tf_op jit(solution)/shard_map/ppermute | solution.py:164
  89.5 3.8 %collective-permute-done.18 = bf16[256,256]{1,0:T(8,128)(2,1)S(1)} collective-permute-done((bf16[256,256]{1,0:T(8,128)(2,1)S(1)}, bf16[256,256]{1,0:T(8,128)(2,1)S(1)}, u32[]{:S(2)}, u32[]{:S(2)}) %collective-permute-start.18) | collective-permute-done | bytes 131104 | tf_op jit(solution)/shard_map/ppermute | solution.py:164
  93.4 1.4 %collective-permute-done.17 = bf16[256,256]{1,0:T(8,128)(2,1)S(1)} collective-permute-done((bf16[256,256]{1,0:T(8,128)(2,1)S(1)}, bf16[256,256]{1,0:T(8,128)(2,1)S(1)}, u32[]{:S(2)}, u32[]{:S(2)}) %collective-permute-start.17) | collective-permute-done | bytes 131104 | tf_op jit(solution)/shard_map/ppermute | solution.py:164
  97.0 11.8 %collective-permute-done.24.refs_6_ = f32[2,1024]{1,0:T(2,128)S(1)} collective-permute-done((f32[2,1024]{1,0:T(2,128)S(1)}, f32[2,1024]{1,0:T(2,128)S(1)}, u32[]{:S(2)}, u32[]{:S(2)}) %collective-permute-start.24) | collective-permute-done | bytes 8224 | tf_op jit(solution)/shard_map/ppermute | solution.py:164
  110.7 6.0 %pass2_0.1.refs_8_ = bf16[2048,256]{1,0:T(8,128)(2,1)} custom-call(s32[2]{0:T(128)} %copy-done.8, bf16[8192,256]{1,0:T(8,128)(2,1)} %c_ref.7, bf16[1024,256]{1,0:T(8,128)(2,1)} %refs_0_.7, bf16[1024,256]{1,0:T(8,128)(2,1)} %copy-done.1, bf16[1024,256]{1,0:T(8,128)(2,1)} %copy-done.2, bf16[1024,256]{1,0:T(8,128)(2,1)} %copy-done.3, f32[2,1024]{1,0:T(2,128)} %copy-done.4, ...), custom_call_target="tpu_custom_call" | custom-call | flops 2147483648 | bytes 2097152 | tf_op jit(solution)/shard_map/pass2_0/pallas_call | solution.py:144
  116.7 6.0 %pass2_1.1.refs_8_ = bf16[2048,256]{1,0:T(8,128)(2,1)} custom-call(s32[2]{0:T(128)} %get-tuple-element.9.base_ref, bf16[8192,256]{1,0:T(8,128)(2,1)} %c_ref.7, bf16[1024,256]{1,0:T(8,128)(2,1)} %refs_0_.7, bf16[1024,256]{1,0:T(8,128)(2,1)} %copy-done.1, bf16[1024,256]{1,0:T(8,128)(2,1)} %copy-done.2, ...), custom_call_target="tpu_custom_call", output_to_operand_aliasing={{}: (10, {})} | custom-call | flops 2147483648 | bytes 2097152 | tf_op jit(solution)/shard_map/pass2_1/pallas_call | solution.py:144
  122.7 6.0 %pass2_2.1.refs_8_ = bf16[2048,256]{1,0:T(8,128)(2,1)} custom-call(s32[2]{0:T(128)} %get-tuple-element.54.base_ref, bf16[8192,256]{1,0:T(8,128)(2,1)} %c_ref.7, bf16[1024,256]{1,0:T(8,128)(2,1)} %refs_0_.7, bf16[1024,256]{1,0:T(8,128)(2,1)} %copy-done.1, bf16[1024,256]{1,0:T(8,128)(2,1)} %copy-done.2, ...), custom_call_target="tpu_custom_call", output_to_operand_aliasing={{}: (10, {})} | custom-call | flops 2147483648 | bytes 2097152 | tf_op jit(solution)/shard_map/pass2_2/pallas_call | solution.py:144
  128.8 6.0 %pass2_3.1 = bf16[2048,256]{1,0:T(8,128)(2,1)} custom-call(s32[2]{0:T(128)} %get-tuple-element.55.base_ref, bf16[8192,256]{1,0:T(8,128)(2,1)} %c_ref.7, bf16[1024,256]{1,0:T(8,128)(2,1)} %refs_0_.7, bf16[1024,256]{1,0:T(8,128)(2,1)} %copy-done.1, bf16[1024,256]{1,0:T(8,128)(2,1)} %copy-done.2, ...), custom_call_target="tpu_custom_call", output_to_operand_aliasing={{}: (10, {})} | custom-call | flops 2147483648 | bytes 2097152 | tf_op jit(solution)/shard_map/pass2_3/pallas_call | solution.py:144
  (67 shorter events, 16.1 us)
Async XLA Ops:
  25.0 58.0 %copy-start = (bf16[1024,256]{1,0:T(8,128)(2,1)S(1)}, bf16[1024,256]{1,0:T(8,128)(2,1)}, u32[]{:S(2)}) copy-start(bf16[1024,256]{1,0:T(8,128)(2,1)} %refs_0_.7) | copy-start | bytes 1572868
  25.0 5.2 %collective-permute-start.2 = (f32[3,1024]{1,0:T(4,128)}, f32[3,1024]{1,0:T(4,128)S(1)}, u32[]{:S(2)}, u32[]{:S(2)}) collective-permute-start(f32[3,1024]{1,0:T(4,128)} %get-tuple-element.6), channel_id=1, source_target_pairs={{0,3},{1,2},{2,1},{3,0},{4,7},{5,6},{6,5},{7,4},{8,11},{9,10},{10,... | collective-permute-start | bytes 36872 | tf_op jit(solution)/shard_map/ppermute | solution.py:164
  27.7 5.5 %collective-permute-start.1 = (f32[3,1024]{1,0:T(4,128)}, f32[3,1024]{1,0:T(4,128)S(1)}, u32[]{:S(2)}, u32[]{:S(2)}) collective-permute-start(f32[3,1024]{1,0:T(4,128)} %get-tuple-element.6), channel_id=1, source_target_pairs={{0,2},{1,3},{2,0},{3,1},{4,6},{5,7},{6,4},{7,5},{8,10},{9,11},{10,... | collective-permute-start | bytes 36872 | tf_op jit(solution)/shard_map/ppermute | solution.py:164
  28.7 4.5 %collective-permute-start = (f32[3,1024]{1,0:T(4,128)}, f32[3,1024]{1,0:T(4,128)S(1)}, u32[]{:S(2)}, u32[]{:S(2)}) collective-permute-start(f32[3,1024]{1,0:T(4,128)} %get-tuple-element.6), channel_id=1, source_target_pairs={{0,1},{1,0},{2,3},{3,2},{4,5},{5,4},{6,7},{7,6},{8,9},{9,8},{10,11... | collective-permute-start | bytes 36872 | tf_op jit(solution)/shard_map/ppermute | solution.py:164
  34.1 5.9 %collective-permute-start.5 = (f32[3,1024]{1,0:T(4,128)S(1)}, f32[3,1024]{1,0:T(4,128)S(1)}, u32[]{:S(2)}, u32[]{:S(2)}) collective-permute-start(f32[3,1024]{1,0:T(4,128)S(1)} %pad_maximum_fusion.4), channel_id=1, source_target_pairs={{0,24},{8,16},{16,8},{24,0},{1,25},{9,17},{17,9},{25,1},{2,26},{10... | collective-permute-start | bytes 36872 | tf_op jit(solution)/shard_map/ppermute | solution.py:164
  38.3 5.2 %collective-permute-start.4 = (f32[3,1024]{1,0:T(4,128)S(1)}, f32[3,1024]{1,0:T(4,128)S(1)}, u32[]{:S(2)}, u32[]{:S(2)}) collective-permute-start(f32[3,1024]{1,0:T(4,128)S(1)} %pad_maximum_fusion.4), channel_id=1, source_target_pairs={{0,16},{8,24},{16,0},{24,8},{1,17},{9,25},{17,1},{25,9},{2,18},{10... | collective-permute-start | bytes 36872 | tf_op jit(solution)/shard_map/ppermute | solution.py:164
  38.3 5.2 %collective-permute-start.3 = (f32[3,1024]{1,0:T(4,128)S(1)}, f32[3,1024]{1,0:T(4,128)S(1)}, u32[]{:S(2)}, u32[]{:S(2)}) collective-permute-start(f32[3,1024]{1,0:T(4,128)S(1)} %pad_maximum_fusion.4), channel_id=1, source_target_pairs={{0,8},{8,0},{16,24},{24,16},{1,9},{9,1},{17,25},{25,17},{2,10},{10... | collective-permute-start | bytes 36872 | tf_op jit(solution)/shard_map/ppermute | solution.py:164
  43.7 5.7 %collective-permute-start.6 = (f32[3,1024]{1,0:T(4,128)S(1)}, f32[3,1024]{1,0:T(4,128)S(1)}, u32[]{:S(2)}, u32[]{:S(2)}) collective-permute-start(f32[3,1024]{1,0:T(4,128)S(1)} %pad_maximum_fusion.5), channel_id=1, source_target_pairs={{0,4},{4,0},{1,5},{5,1},{2,6},{6,2},{3,7},{7,3},{8,12},{12,8},{9,1... | collective-permute-start | bytes 36872 | tf_op jit(solution)/shard_map/ppermute | solution.py:164
  51.3 7.7 %collective-permute-start.9 = (bf16[256,256]{1,0:T(8,128)(2,1)S(1)}, bf16[256,256]{1,0:T(8,128)(2,1)S(1)}, u32[]{:S(2)}, u32[]{:S(2)}) collective-permute-start(bf16[256,256]{1,0:T(8,128)(2,1)S(1)} %get-tuple-element.18), channel_id=1, source_target_pairs={{0,3},{1,2},{2,1},{3,0},{4,7},{5,6},{6,5},{7,4},{8,11},{9,10},{10,... | collective-permute-start | bytes 393224 | tf_op jit(solution)/shard_map/ppermute | solution.py:164
  52.2 6.8 %collective-permute-start.8 = (bf16[256,256]{1,0:T(8,128)(2,1)S(1)}, bf16[256,256]{1,0:T(8,128)(2,1)S(1)}, u32[]{:S(2)}, u32[]{:S(2)}) collective-permute-start(bf16[256,256]{1,0:T(8,128)(2,1)S(1)} %get-tuple-element.19), channel_id=1, source_target_pairs={{0,2},{1,3},{2,0},{3,1},{4,6},{5,7},{6,4},{7,5},{8,10},{9,11},{10,... | collective-permute-start | bytes 393224 | tf_op jit(solution)/shard_map/ppermute | solution.py:164
  53.5 6.3 %collective-permute-start.7 = (bf16[256,256]{1,0:T(8,128)(2,1)S(1)}, bf16[256,256]{1,0:T(8,128)(2,1)S(1)}, u32[]{:S(2)}, u32[]{:S(2)}) collective-permute-start(bf16[256,256]{1,0:T(8,128)(2,1)S(1)} %get-tuple-element.17), channel_id=1, source_target_pairs={{0,1},{1,0},{2,3},{3,2},{4,5},{5,4},{6,7},{7,6},{8,9},{9,8},{10,11... | collective-permute-start | bytes 393224 | tf_op jit(solution)/shard_map/ppermute | solution.py:164
  59.9 4.8 %collective-permute-start.10 = (f32[64,256]{1,0:T(8,128)S(1)}, f32[64,256]{1,0:T(8,128)S(1)}, u32[]{:S(2)}, u32[]{:S(2)}) collective-permute-start(f32[64,256]{1,0:T(8,128)S(1)} %get-tuple-element.26), channel_id=1, source_target_pairs={{0,8},{8,0},{16,24},{24,16},{1,9},{9,1},{17,25},{25,17},{2,10},{10... | collective-permute-start | bytes 196616 | tf_op jit(solution)/shard_map/ppermute | solution.py:164
  60.0 5.8 %collective-permute-start.11 = (f32[64,256]{1,0:T(8,128)S(1)}, f32[64,256]{1,0:T(8,128)S(1)}, u32[]{:S(2)}, u32[]{:S(2)}) collective-permute-start(f32[64,256]{1,0:T(8,128)S(1)} %get-tuple-element.25), channel_id=1, source_target_pairs={{0,16},{8,24},{16,0},{24,8},{1,17},{9,25},{17,1},{25,9},{2,18},{10... | collective-permute-start | bytes 196616 | tf_op jit(solution)/shard_map/ppermute | solution.py:164
  62.2 5.5 %collective-permute-start.12 = (f32[64,256]{1,0:T(8,128)S(1)}, f32[64,256]{1,0:T(8,128)S(1)}, u32[]{:S(2)}, u32[]{:S(2)}) collective-permute-start(f32[64,256]{1,0:T(8,128)S(1)} %get-tuple-element.24), channel_id=1, source_target_pairs={{0,24},{8,16},{16,8},{24,0},{1,25},{9,17},{17,9},{25,1},{2,26},{10... | collective-permute-start | bytes 196616 | tf_op jit(solution)/shard_map/ppermute | solution.py:164
  67.7 5.8 %collective-permute-start.13 = (f32[64,256]{1,0:T(8,128)S(1)}, f32[64,256]{1,0:T(8,128)S(1)}, u32[]{:S(2)}, u32[]{:S(2)}) collective-permute-start(f32[64,256]{1,0:T(8,128)S(1)} %fusion.4), channel_id=1, source_target_pairs={{0,4},{4,0},{1,5},{5,1},{2,6},{6,2},{3,7},{7,3},{8,12},{12,8},{9,1... | collective-permute-start | bytes 196616 | tf_op jit(solution)/shard_map/ppermute | solution.py:164
  73.5 5.2 %collective-permute-start.16 = (bf16[64,256]{1,0:T(8,128)(2,1)S(1)}, bf16[64,256]{1,0:T(8,128)(2,1)S(1)}, u32[]{:S(2)}, u32[]{:S(2)}) collective-permute-start(bf16[64,256]{1,0:T(8,128)(2,1)S(1)} %add_convert_fusion), channel_id=1, source_target_pairs={{0,24},{8,16},{16,8},{24,0},{1,25},{9,17},{17,9},{25,1},{2,26},{10... | collective-permute-start | bytes 98312 | tf_op jit(solution)/shard_map/ppermute | solution.py:164
  76.1 5.4 %collective-permute-start.15 = (bf16[64,256]{1,0:T(8,128)(2,1)S(1)}, bf16[64,256]{1,0:T(8,128)(2,1)S(1)}, u32[]{:S(2)}, u32[]{:S(2)}) collective-permute-start(bf16[64,256]{1,0:T(8,128)(2,1)S(1)} %add_convert_fusion), channel_id=1, source_target_pairs={{0,16},{8,24},{16,0},{24,8},{1,17},{9,25},{17,1},{25,9},{2,18},{10... | collective-permute-start | bytes 98312 | tf_op jit(solution)/shard_map/ppermute | solution.py:164
  76.8 4.8 %collective-permute-start.14 = (bf16[64,256]{1,0:T(8,128)(2,1)S(1)}, bf16[64,256]{1,0:T(8,128)(2,1)S(1)}, u32[]{:S(2)}, u32[]{:S(2)}) collective-permute-start(bf16[64,256]{1,0:T(8,128)(2,1)S(1)} %add_convert_fusion), channel_id=1, source_target_pairs={{0,8},{8,0},{16,24},{24,16},{1,9},{9,1},{17,25},{25,17},{2,10},{10... | collective-permute-start | bytes 98312 | tf_op jit(solution)/shard_map/ppermute | solution.py:164
  81.6 6.3 %collective-permute-start.19 = (bf16[256,256]{1,0:T(8,128)(2,1)S(1)}, bf16[256,256]{1,0:T(8,128)(2,1)S(1)}, u32[]{:S(2)}, u32[]{:S(2)}) collective-permute-start(bf16[256,256]{1,0:T(8,128)(2,1)S(1)} %get-tuple-element.28), channel_id=1, source_target_pairs={{0,3},{1,2},{2,1},{3,0},{4,7},{5,6},{6,5},{7,4},{8,11},{9,10},{10,... | collective-permute-start | bytes 393224 | tf_op jit(solution)/shard_map/ppermute | solution.py:164
  83.0 25.8 %collective-permute-start.20 = (bf16[1024,256]{1,0:T(8,128)(2,1)S(1)}, bf16[1024,256]{1,0:T(8,128)(2,1)S(1)}, u32[]{:S(2)}, u32[]{:S(2)}) collective-permute-start(bf16[1024,256]{1,0:T(8,128)(2,1)S(1)} %copy-done), channel_id=1, source_target_pairs={{0,32},{32,0},{64,96},{96,64},{1,33},{33,1},{65,97},{97,65},{2,34}... | collective-permute-start | bytes 1572872 | tf_op jit(solution)/shard_map/ppermute | solution.py:164
  83.0 25.9 %collective-permute-start.21 = (bf16[1024,256]{1,0:T(8,128)(2,1)S(1)}, bf16[1024,256]{1,0:T(8,128)(2,1)S(1)}, u32[]{:S(2)}, u32[]{:S(2)}) collective-permute-start(bf16[1024,256]{1,0:T(8,128)(2,1)S(1)} %copy-done), channel_id=1, source_target_pairs={{0,64},{32,96},{64,0},{96,32},{1,65},{33,97},{65,1},{97,33},{2,66}... | collective-permute-start | bytes 1572872 | tf_op jit(solution)/shard_map/ppermute | solution.py:164
  84.6 24.2 %collective-permute-start.22 = (bf16[1024,256]{1,0:T(8,128)(2,1)S(1)}, bf16[1024,256]{1,0:T(8,128)(2,1)S(1)}, u32[]{:S(2)}, u32[]{:S(2)}) collective-permute-start(bf16[1024,256]{1,0:T(8,128)(2,1)S(1)} %copy-done), channel_id=1, source_target_pairs={{0,96},{32,64},{64,32},{96,0},{1,97},{33,65},{65,33},{97,1},{2,98}... | collective-permute-start | bytes 1572872 | tf_op jit(solution)/shard_map/ppermute | solution.py:164
  85.5 23.4 %copy-start.8 = (s32[2]{0:T(128)}, s32[2]{0:T(128)S(1)}, u32[]{:S(2)}) copy-start(s32[2]{0:T(128)S(1)} %get-tuple-element.10.base_ref) | copy-start | bytes 28
  85.5 7.9 %collective-permute-start.18 = (bf16[256,256]{1,0:T(8,128)(2,1)S(1)}, bf16[256,256]{1,0:T(8,128)(2,1)S(1)}, u32[]{:S(2)}, u32[]{:S(2)}) collective-permute-start(bf16[256,256]{1,0:T(8,128)(2,1)S(1)} %get-tuple-element.28), channel_id=1, source_target_pairs={{0,2},{1,3},{2,0},{3,1},{4,6},{5,7},{6,4},{7,5},{8,10},{9,11},{10,... | collective-permute-start | bytes 393224 | tf_op jit(solution)/shard_map/ppermute | solution.py:164
  87.9 6.9 %collective-permute-start.17 = (bf16[256,256]{1,0:T(8,128)(2,1)S(1)}, bf16[256,256]{1,0:T(8,128)(2,1)S(1)}, u32[]{:S(2)}, u32[]{:S(2)}) collective-permute-start(bf16[256,256]{1,0:T(8,128)(2,1)S(1)} %get-tuple-element.28), channel_id=1, source_target_pairs={{0,1},{1,0},{2,3},{3,2},{4,5},{5,4},{6,7},{7,6},{8,9},{9,8},{10,11... | collective-permute-start | bytes 393224 | tf_op jit(solution)/shard_map/ppermute | solution.py:164
  89.5 19.4 %copy-start.4 = (f32[2,1024]{1,0:T(2,128)}, f32[2,1024]{1,0:T(2,128)S(1)}, u32[]{:S(2)}) copy-start(f32[2,1024]{1,0:T(2,128)S(1)} %pad_maximum_fusion.6.refs_4_) | copy-start | bytes 24580
  93.4 2.5 %collective-permute-start.23 = (f32[2,1024]{1,0:T(2,128)S(1)}, f32[2,1024]{1,0:T(2,128)S(1)}, u32[]{:S(2)}, u32[]{:S(2)}) collective-permute-start(f32[2,1024]{1,0:T(2,128)S(1)} %pad_maximum_fusion.6.refs_4_), channel_id=1, source_target_pairs={{0,32},{32,0},{64,96},{96,64},{1,33},{33,1},{65,97},{97,65},{2,34}... | collective-permute-start | bytes 24584 | tf_op jit(solution)/shard_map/ppermute | solution.py:164
  94.8 14.0 %collective-permute-start.24 = (f32[2,1024]{1,0:T(2,128)S(1)}, f32[2,1024]{1,0:T(2,128)S(1)}, u32[]{:S(2)}, u32[]{:S(2)}) collective-permute-start(f32[2,1024]{1,0:T(2,128)S(1)} %pad_maximum_fusion.6.refs_4_), channel_id=1, source_target_pairs={{0,64},{32,96},{64,0},{96,32},{1,65},{33,97},{65,1},{97,33},{2,66}... | collective-permute-start | bytes 24584 | tf_op jit(solution)/shard_map/ppermute | solution.py:164
  95.9 13.0 %copy-start.5 = (f32[2,1024]{1,0:T(2,128)}, f32[2,1024]{1,0:T(2,128)S(1)}, u32[]{:S(2)}) copy-start(f32[2,1024]{1,0:T(2,128)S(1)} %collective-permute-done.23.refs_5_) | copy-start | bytes 24580
  95.9 12.9 %collective-permute-start.25 = (f32[2,1024]{1,0:T(2,128)S(1)}, f32[2,1024]{1,0:T(2,128)S(1)}, u32[]{:S(2)}, u32[]{:S(2)}) collective-permute-start(f32[2,1024]{1,0:T(2,128)S(1)} %pad_maximum_fusion.6.refs_4_), channel_id=1, source_target_pairs={{0,96},{32,64},{64,32},{96,0},{1,97},{33,65},{65,33},{97,1},{2,98}... | collective-permute-start | bytes 24584 | tf_op jit(solution)/shard_map/ppermute | solution.py:164
  108.9 1.0 copy-start.2
  109.9 0.8 copy-start.3
  (3 other events, 2.0 us)

commit v2 on v1

v2 whole, which is shorter than its diff:
```python
import functools
import math

import jax
import jax.numpy as jnp
from jax import lax
from jax.experimental import pallas as pl
from jax.experimental.pallas import tpu as pltpu
from jax.sharding import Mesh
from jax.sharding import PartitionSpec as P

sharpness_divisor = 4.0
SCALE = math.log2(math.e) / sharpness_divisor
NT = (((1,), (1,)), ((), ()))
ITEM = ("z", "y_hi", "x")
USER = ("y_lo", "core")
VMEM = pl.BlockSpec(memory_space=pltpu.VMEM)
SMEM = pl.BlockSpec(memory_space=pltpu.SMEM)
f32 = jnp.float32
bf16 = jnp.bfloat16


def exp_of(x):
    return jnp.exp2(x * SCALE)


def struct(*shape, dtype=f32):
    return jax.ShapeDtypeStruct(shape, dtype)


def as_row(column):
    return jnp.broadcast_to(column, (128, 128)).T[0:1]


def as_column(row):
    return jnp.broadcast_to(row, (128, 128)).T


def pass1_kernel(tile, rb, pos_ref, me_ref, u_ref, cat_ref, *refs):
    out_refs, (st_ref, c_ref, acc_ref, hit_ref, m_ref, l_ref, sem) = refs[:4], refs[4:]
    rows = u_ref.shape[0]
    count, width = cat_ref.shape
    n = count // tile
    copies = []
    for i in range(n):
        part = pl.ds(i * tile, tile)
        copies.append(pltpu.make_async_copy(cat_ref.at[part], c_ref.at[part], sem.at[i]))
        copies[-1].start()
    acc_ref[...] = jnp.zeros_like(acc_ref)
    hit_ref[...] = jnp.zeros_like(hit_ref)
    m_ref[...] = jnp.full_like(m_ref, -1e38)
    l_ref[...] = jnp.zeros_like(l_ref)
    for i in range(n):
        copies[i].wait()
        c = c_ref[i * tile : (i + 1) * tile]
        for b in range(rows // rb):
            sl = slice(b * rb, (b + 1) * rb)
            r = lax.dot_general(u_ref[sl], c, NT, preferred_element_type=f32)
            m_old = m_ref[sl]
            m_new = jnp.maximum(m_old, jnp.max(r, axis=1, keepdims=True))
            alpha = exp_of(m_old - m_new)
            m_ref[sl] = m_new
            total = l_ref[sl] * alpha
            ps = []
            for j in range(tile // 128):
                p = exp_of(r[:, j * 128 : (j + 1) * 128] - m_new)
                total = total + p
                ps.append(p.astype(bf16))
            l_ref[sl] = total
            wide = jnp.concatenate([alpha] * (width // 128), axis=1)
            acc_ref[sl] = acc_ref[sl] * wide + jnp.dot(
                jnp.concatenate(ps, axis=1), c, preferred_element_type=f32
            )

    @pl.loop(0, rows // 8)
    def _(g):
        here = [pos_ref[g * 8 + j] for j in range(8)]
        mine = [(h >= 0) & (h < count) for h in here]
        some = functools.reduce(jnp.logical_or, mine)

        @pl.when(some)
        def _():
            for j in range(8):

                @pl.when(mine[j])
                def _():
                    start = pl.multiple_of((here[j] >> 4) << 4, 16)
                    group = c_ref[pl.ds(start, 16), :].astype(f32)
                    inside = lax.broadcasted_iota(jnp.int32, group.shape, 0) == (here[j] & 15)
                    row = jnp.sum(jnp.where(inside, group, 0.0), axis=0, keepdims=True)
                    hit_ref[pl.ds(g * 8 + j, 1), :] = row

    for b in range(rows // 128):
        sl = slice(b * 128, (b + 1) * 128)
        total = jnp.sum(l_ref[sl], axis=1, keepdims=True)
        acc_ref[sl] = acc_ref[sl] * (1.0 / total)
        hit_score = jnp.sum(hit_ref[sl] * u_ref[sl].astype(f32), axis=1, keepdims=True)
        part = slice(b % 2 * 128, b % 2 * 128 + 128)
        st_ref[b // 2 : b // 2 + 1, part] = m_ref[sl].T[0:1] + sharpness_divisor * jnp.log(as_row(total))
        st_ref[4 + b // 2 : 5 + b // 2, part] = as_row(hit_score)
    chunk = rows // 4
    for k, out_ref in enumerate(out_refs):
        part = pl.ds(pl.multiple_of((me_ref[0] ^ k) * chunk, chunk), chunk)
        out_ref[0:chunk] = acc_ref[part, :].astype(bf16)
        out_ref[chunk:] = hit_ref[part, :].astype(bf16)


def pass1(users, catalog, local_pos, me, tile=2048, rb=256):
    rows, width = users.shape
    count = catalog.shape[0]
    return pl.pallas_call(
        functools.partial(pass1_kernel, tile, rb),
        in_specs=[SMEM, SMEM, VMEM, pl.BlockSpec(memory_space=pl.ANY)],
        out_specs=[VMEM] * 5,
        out_shape=[struct(rows // 2, width, dtype=bf16)] * 4 + [struct(8, rows // 4)],
        scratch_shapes=[
            pltpu.VMEM((count, width), bf16),
            pltpu.VMEM((rows, width), f32),
            pltpu.VMEM((rows, width), f32),
            pltpu.VMEM((rows, 128), f32),
            pltpu.VMEM((rows, 128), f32),
            pltpu.SemaphoreType.DMA((count // tile,)),
        ],
        cost_estimate=pl.CostEstimate(
            flops=4 * rows * count * width, bytes_accessed=2 * count * width, transcendentals=rows * count
        ),
        name="pass1",
    )(local_pos, me, users, catalog)


def merge_kernel(me_ref, all_ref, p0, p1, p2, p3, i0, i1, i2, i3, loss_ref, w_ref):
    x, member, shard = me_ref[0], me_ref[1], me_ref[2]
    shards = all_ref.shape[0] // 4
    for k, (pos_ref, info_ref) in enumerate(zip((p0, p1, p2, p3), (i0, i1, i2, i3))):
        first = (member ^ k) * shards
        stats = all_ref[pl.ds(first, shards)]
        top = jnp.max(stats, axis=0)
        lse4 = top + sharpness_divisor * jnp.log(jnp.sum(exp_of(stats - top[None]), axis=0))
        info_ref[0:4] = lse4[0:4]
        info_ref[4:8] = pos_ref[...].astype(f32)
        if k == 0:
            loss_ref[...] = (lse4[0:4] - jnp.sum(stats, axis=0)[4:8]) / sharpness_divisor
    for k in range(4):
        mine = all_ref[member * shards + (shard ^ k), pl.ds(x, 1), :]
        w_ref[k : k + 1] = exp_of(mine - i0[pl.ds(x, 1), :])
    w_ref[4:8] = jnp.zeros_like(w_ref[4:8])


def merge(me, every, positions):
    width = every.shape[2]
    return pl.pallas_call(
        merge_kernel,
        in_specs=[SMEM] + [VMEM] * 5,
        out_specs=[VMEM] * 6,
        out_shape=[struct(8, width)] * 4 + [struct(4, width), struct(8, width)],
        name="merge",
    )(me, every, *positions)


def combine_kernel(w_ref, a0, a1, a2, a3, out_ref):
    chunk, width = out_ref.shape
    for h in range(chunk // 128):
        sl = slice(h * 128, (h + 1) * 128)
        low = slice(chunk + h * 128, chunk + (h + 1) * 128)
        total = jnp.zeros((128, width), f32)
        for k, a_ref in enumerate((a0, a1, a2, a3)):
            column = as_column(w_ref[k : k + 1, sl])
            wide = jnp.concatenate([column] * (width // 128), axis=1)
            total = total + wide * a_ref[sl].astype(f32) - a_ref[low].astype(f32)
        out_ref[sl] = (total / sharpness_divisor).astype(out_ref.dtype)


def combine(weights, parts):
    rows, width = parts[0].shape
    return pl.pallas_call(
        combine_kernel,
        in_specs=[VMEM] * 5,
        out_specs=VMEM,
        out_shape=struct(rows // 2, width, dtype=bf16),
        name="combine",
    )(weights, *parts)


def pass2_kernel(tile, base_ref, c_ref, *refs):
    us, infos, out_ref = refs[:4], refs[4:8], refs[-1]
    first = base_ref[1] + pl.program_id(0) * tile
    c = c_ref[...]
    item = (lax.broadcasted_iota(jnp.int32, (tile, 128), 0) + first).astype(f32)
    total = jnp.zeros((tile, c.shape[1]), f32)
    for u_ref, info_ref in zip(us, infos):
        u = u_ref[...]
        r = lax.dot_general(c, u, NT, preferred_element_type=f32)
        ws = []
        for j in range(u.shape[0] // 128):
            part = slice(j % 2 * 128, j % 2 * 128 + 128)
            w = exp_of(r[:, j * 128 : (j + 1) * 128] - info_ref[j // 2 : j // 2 + 1, part])
            hit = info_ref[4 + j // 2 : 5 + j // 2, part] == item
            ws.append(jnp.where(hit, w - 1.0, w).astype(bf16))
        total = total + jnp.dot(jnp.concatenate(ws, axis=1), u, preferred_element_type=f32)
    out_ref[...] = (total / sharpness_divisor).astype(out_ref.dtype)


def pass2(base, catalog, us, infos, items, start, stop, before, tile=512):
    rows, width = us[0].shape
    lead = start // tile
    n = (stop - start) // tile
    resident = lambda i, b: (0, 0)
    in_specs = [pl.BlockSpec((tile, width), lambda i, b: (b[0] * (items // tile) + lead + i, 0))]
    in_specs += [pl.BlockSpec((rows, width), resident)] * 4
    in_specs += [pl.BlockSpec((8, rows // 4), resident)] * 4
    args = [base + jnp.array([0, start], jnp.int32), catalog, *us, *infos]
    aliases = {}
    if before is not None:
        in_specs.append(pl.BlockSpec(memory_space=pl.ANY))
        aliases = {len(args): 0}
        args.append(before)
    return pl.pallas_call(
        functools.partial(pass2_kernel, tile),
        grid_spec=pltpu.PrefetchScalarGridSpec(
            num_scalar_prefetch=1,
            grid=(n,),
            in_specs=in_specs,
            out_specs=pl.BlockSpec((tile, width), lambda i, b: (lead + i, 0)),
        ),
        out_shape=struct(items, width, dtype=bf16),
        input_output_aliases=aliases,
        cost_estimate=pl.CostEstimate(
            flops=16 * rows * (stop - start) * width,
            bytes_accessed=8 * rows * width,
            transcendentals=4 * rows * (stop - start),
        ),
        name="pass2",
    )(*args)


def swap(x, axis, size, k):
    return lax.ppermute(x, axis, [(i, i ^ k) for i in range(size)])


def per_device(users, catalog, positives):
    rows = users.shape[0]
    count = catalog.shape[0]
    items = count // 4
    x, member, shard = lax.axis_index("x"), lax.axis_index(USER), lax.axis_index(ITEM)
    me = jnp.stack([x, member, shard])
    pos = positives.reshape(4, rows // 4)
    over = swap(users, USER, 4, 2)
    us = [users, swap(users, USER, 4, 1), over, swap(over, USER, 4, 1)]
    positions = [pos] + [swap(pos, USER, 4, k) for k in (1, 2, 3)]
    *pieces, stats = pass1(users, catalog, positives - shard * count, me)
    got = [pieces[0]] + [swap(pieces[k], "x", 4, k) for k in (1, 2, 3)]
    every = jnp.broadcast_to(stats[None], (128,) + stats.shape)
    every = lax.all_to_all(every, USER + ITEM, 0, 0, tiled=True)
    *infos, loss, weights = merge(me, every, positions)
    value = combine(weights, got)
    base = jnp.stack([member, shard * count + member * items])

    a = [value] + [swap(value, "z", 4, k) for k in (1, 2, 3)]
    item_grad = pass2(base, catalog, us, infos, items, 0, SPLIT[0], None)
    a = [v.astype(f32) for v in a]
    value = (a[0] + a[1]) + (a[2] + a[3])
    other = swap(value, "y_hi", 2, 1)
    item_grad = pass2(base, catalog, us, infos, items, SPLIT[0], SPLIT[1], item_grad)
    value = (value + other).astype(bf16)
    got = [value] + [swap(value, "x", 4, k) for k in (1, 2, 3)]
    item_grad = pass2(base, catalog, us, infos, items, SPLIT[1], items, item_grad)
    got = jnp.stack(got)
    user_grad = jnp.concatenate(
        [lax.dynamic_index_in_dim(got, x ^ k, keepdims=False) for k in range(4)], axis=0
    )
    return loss.reshape(rows), user_grad, item_grad


SPLIT = (512, 1024)


def solution(mesh):
    grid = Mesh(mesh.devices.reshape(2, 2, 4, 2, 4), USER + ITEM)

    return jax.shard_map(
        per_device,
        mesh=grid,
        in_specs=(P(USER, None), P(ITEM, None), P(USER)),
        out_specs=(P(USER), P(USER, None), P(ITEM + USER, None)),
        check_vma=False,
    )
```

time: 136 us -> 116 us (0.85)
  waiting for transfers between devices: 40.7 us -> 25.4 us
  starting transfers between devices: 36.4 us -> 30.1 us
  local copies, waits for them, and re-layouts: 2.63 us -> 5.68 us
  other arithmetic: 7.03 us -> 4.95 us
  Pallas kernels: 47.1 us -> 48.6 us
    ppermute x26 -> x16, starting transfers between devices: 36.4 us -> 18.9 us  [swap(): return lax.ppermute(x, axis, [(i, i ^ k) for i in range(size)])]
    ppermute x26 -> x16, waiting for transfers between devices: 40.7 us -> 25.4 us  [swap(): return lax.ppermute(x, axis, [(i, i ^ k) for i in range(size)])]
    all_to_all x0 -> x1, starting transfers between devices: none -> 11.2 us  [per_device(): every = lax.all_to_all(every, USER + ITEM, 0, 0, tiled=True)]
    pallas_call x1 -> x3, Pallas kernels: 23 us -> 27.4 us  [the longest x1 23.2 us: pass1(): pl.pallas_call(functools.partial(pass1_kernel, tile, rb), in_specs=[SMEM,...]
    pallas_call x4 -> x3, Pallas kernels: 24.1 us -> 21.2 us  [pass2(): pl.pallas_call(functools.partial(pass2_kernel, tile), grid_spec=pltpu.Pre...]
    unnamed x18 -> x25, local copies, waits for them, and re-layouts: 1.77 us -> 3.89 us
    div x1 -> x0, other arithmetic: 1.75 us -> none  [per_device(): value = (partial * weight[:, None] - hits) / sharpness_divisor]
    broadcast_in_dim x0 -> x1, local copies, waits for them, and re-layouts: none -> 1.73 us  [per_device(): every = jnp.broadcast_to(stats[None], (128,) + stats.shape)]
  transfers between devices with their start and end apart: 26 -> 17, of which waited for: 16 -> 5; matrix products, arithmetic and copies ran while one was open for 3% -> 3% of each run, Pallas kernels for 0% -> 22%
where the time goes in v2:
time: 116 us
  Pallas kernels  48.6 us (42%)
  starting transfers between devices  30.1 us (26%)
  waiting for transfers between devices  25.4 us (22%)
  local copies, waits for them, and re-layouts  5.68 us (5%)
  other arithmetic  4.95 us (4%)
    ppermute x16, waiting for transfers between devices, swap(): return lax.ppermute(x, axis, [(i, i ^ k) for i in range(size)])  25.4 us
    pallas_call x1, Pallas kernels, pass1(): pl.pallas_call(functools.partial(pass1_kernel, tile, rb), in_specs=[SMEM,...  23.2 us
    pallas_call x3, Pallas kernels, pass2(): pl.pallas_call(functools.partial(pass2_kernel, tile), grid_spec=pltpu.Pre...  21.2 us
    ppermute x16, starting transfers between devices, swap(): return lax.ppermute(x, axis, [(i, i ^ k) for i in range(size)])  18.9 us
    all_to_all x1, starting transfers between devices, per_device(): every = lax.all_to_all(every, USER + ITEM, 0, 0, tiled=True)  11.2 us
    unnamed x25, local copies, waits for them, and re-layouts  3.89 us
  transfers between devices with their start and end apart: 17, of which 5 were waited for; matrix products, arithmetic and copies ran while one was open for 3% of the time, Pallas kernels for 22%

profile of v2, /device:TPU:0, one launch (start us, length us, event | category | flops | bytes accessed | tf_op | source)
XLA Modules:
  0.0 115.5 jit_solution(6834873948229625519)
XLA Ops:
  0.6 1.3 %broadcast_subtract_fusion.pos_ref = s32[1024]{0:T(1024)} fusion(s32[1024]{0:T(1024)} %param.8, s32[]{:T(128)S(6)} %mul.19), kind=kLoop, calls=%fused_computation.8 | loop fusion | flops 1024 | bytes 8196 | tf_op jit(solution)/shard_map/sub | solution.py:250
  1.9 0.6 pad_add_fusion.me_ref
  2.6 23.2 %pass1.1 = (bf16[512,256]{1,0:T(8,128)(2,1)}, bf16[512,256]{1,0:T(8,128)(2,1)}, bf16[512,256]{1,0:T(8,128)(2,1)}, bf16[512,256]{1,0:T(8,128)(2,1)}, f32[8,256]{1,0:T(8,128)}) custom-call(s32[1024]{0:T(1024)} %broadcast_subtract_fusion.pos_ref, s32[3]{0:T(128)} %pad_add_fusion.me_ref, bf16[1024,256]{1,0:T(8,128)(2,1)} %refs_0_.5, bf16[8192,256]{1,0:T(8,128)(2,1)} %c_ref.5), custom_call_target="tpu_custom_call" | custom-call | flops 8589934592 | bytes 4194304 | tf_op jit(solution)/shard_map/pass1/pallas_call | solution.py:111
  25.8 1.7 %broadcast_in_dim.2 = f32[128,8,256]{2,1,0:T(8,128)} broadcast(f32[8,256]{1,0:T(8,128)} %get-tuple-element.14), dimensions={1,2} | broadcast | bytes 1056768 | tf_op jit(solution)/shard_map/broadcast_in_dim | solution.py:252
  27.5 11.2 %all-to-all-start = ((f32[128,8,256]{2,1,0:T(8,128)}), f32[128,8,256]{2,1,0:T(8,128)S(1)}, u32[]{:S(2)}, u32[]{:S(2)}) async-start(f32[128,8,256]{2,1,0:T(8,128)} %broadcast_in_dim.2), calls=%async_computation | async-start | bytes 2097152 | tf_op jit(solution)/shard_map/all_to_all | solution.py:253
  38.7 1.0 collective-permute-start.14
  39.7 1.5 %collective-permute-start.3 = (bf16[512,256]{1,0:T(8,128)(2,1)}, bf16[512,256]{1,0:T(8,128)(2,1)S(1)}, u32[]{:S(2)}, u32[]{:S(2)}) collective-permute-start(bf16[512,256]{1,0:T(8,128)(2,1)} %get-tuple-element.18), channel_id=1, source_target_pairs={{0,1},{1,0},{2,3},{3,2},{4,5},{5,4},{6,7},{7,6},{8,9},{9,8},{10,11... | collective-permute-start | bytes 786440 | tf_op jit(solution)/shard_map/ppermute | solution.py:237
  41.2 2.7 %collective-permute-start.4 = (bf16[512,256]{1,0:T(8,128)(2,1)}, bf16[512,256]{1,0:T(8,128)(2,1)}, u32[]{:S(2)}, u32[]{:S(2)}) collective-permute-start(bf16[512,256]{1,0:T(8,128)(2,1)} %get-tuple-element.19), channel_id=1, source_target_pairs={{0,2},{1,3},{2,0},{3,1},{4,6},{5,7},{6,4},{7,5},{8,10},{9,11},{10,... | collective-permute-start | bytes 786440 | tf_op jit(solution)/shard_map/ppermute | solution.py:237
  43.9 0.6 collective-permute-start.5
  44.5 1.2 collective-permute-done.p1
  45.7 1.1 collective-permute-start.1
  46.7 15.8 %collective-permute-done.1.p2 = s32[4,256]{1,0:T(4,128)S(1)} collective-permute-done((s32[4,256]{1,0:T(4,128)S(1)}, s32[4,256]{1,0:T(4,128)S(1)}, u32[]{:S(2)}, u32[]{:S(2)}) %collective-permute-start.1) | collective-permute-done | bytes 4128 | tf_op jit(solution)/shard_map/ppermute | solution.py:237
  62.5 3.0 %collective-permute-done.2.p3 = s32[4,256]{1,0:T(4,128)S(1)} collective-permute-done((s32[4,256]{1,0:T(4,128)S(1)}, s32[4,256]{1,0:T(4,128)S(1)}, u32[]{:S(2)}, u32[]{:S(2)}) %collective-permute-start.2) | collective-permute-done | bytes 4128 | tf_op jit(solution)/shard_map/ppermute | solution.py:237
  66.1 0.6 multiply_add_fusion.1
  66.7 1.0 copy-done
  67.7 2.1 %merge.1 = (f32[8,256]{1,0:T(8,128)}, f32[8,256]{1,0:T(8,128)}, f32[8,256]{1,0:T(8,128)}, f32[8,256]{1,0:T(8,128)}, f32[4,256]{1,0:T(4,128)}, /*index=5*/f32[8,256]{1,0:T(8,128)}) custom-call(s32[3]{0:T(128)} %pad_add_fusion.me_ref, f32[128,8,256]{2,1,0:T(8,128)} %copy-done, s32[4,256]{1,0:T(4,128)} %copy-done.6, s32[4,256]{1,0:T(4,128)} %copy-done.8, ...), custom_call_target="tpu_custom_call" | custom-call | tf_op jit(solution)/shard_map/merge/pallas_call | solution.py:151
  69.8 0.7 copy-done.5
  70.5 2.1 %combine.1 = bf16[256,256]{1,0:T(8,128)(2,1)} custom-call(f32[8,256]{1,0:T(8,128)} %get-tuple-element.16.w_ref, bf16[512,256]{1,0:T(8,128)(2,1)} %get-tuple-element.17.a0, bf16[512,256]{1,0:T(8,128)(2,1)} %copy-done.5, bf16[512,256]{1,0:T(8,128)(2,1)} %collective-permute-done.4.a2, bf16[512,256]{1,0:T(8,128)(2,1)} %collective-permute-done.5.a3), custom_call_target="tpu_custom_call" | custom-call | tf_op jit(solution)/shard_map/combine/pallas_call | solution.py:175
  72.6 3.4 %collective-permute-start.8 = (bf16[256,256]{1,0:T(8,128)(2,1)}, bf16[256,256]{1,0:T(8,128)(2,1)S(1)}, u32[]{:S(2)}, u32[]{:S(2)}) collective-permute-start(bf16[256,256]{1,0:T(8,128)(2,1)} %combine.1), channel_id=1, source_target_pairs={{0,24},{8,16},{16,8},{24,0},{1,25},{9,17},{17,9},{25,1},{2,26},{10... | collective-permute-start | bytes 393224 | tf_op jit(solution)/shard_map/ppermute | solution.py:237
  76.3 0.5 collective-permute-start.6
  77.4 1.3 %copy.11 = f32[1,2,4,128]{3,1,2,0:T(2,128)} copy(f32[1,2,4,128]{3,2,1,0:T(4,128)} %bitcast.23) | data formatting | bytes 8192
  78.7 3.5 %collective-permute-done.8 = bf16[256,256]{1,0:T(8,128)(2,1)S(1)} collective-permute-done((bf16[256,256]{1,0:T(8,128)(2,1)}, bf16[256,256]{1,0:T(8,128)(2,1)S(1)}, u32[]{:S(2)}, u32[]{:S(2)}) %collective-permute-start.8) | collective-permute-done | bytes 131104 | tf_op jit(solution)/shard_map/ppermute | solution.py:237
  82.1 1.9 %collective-permute-done.7 = bf16[256,256]{1,0:T(8,128)(2,1)S(1)} collective-permute-done((bf16[256,256]{1,0:T(8,128)(2,1)}, bf16[256,256]{1,0:T(8,128)(2,1)S(1)}, u32[]{:S(2)}, u32[]{:S(2)}) %collective-permute-start.7) | collective-permute-done | bytes 131104 | tf_op jit(solution)/shard_map/ppermute | solution.py:237
  84.1 1.0 add_add_fusion
  85.0 3.1 %collective-permute-start.9 = (f32[256,256]{1,0:T(8,128)S(1)}, f32[256,256]{1,0:T(8,128)S(1)}, u32[]{:S(2)}, u32[]{:S(2)}) collective-permute-start(f32[256,256]{1,0:T(8,128)S(1)} %add_add_fusion), channel_id=1, source_target_pairs={{0,4},{4,0},{1,5},{5,1},{2,6},{6,2},{3,7},{7,3},{8,12},{12,8},{9,1... | collective-permute-start | bytes 786440 | tf_op jit(solution)/shard_map/ppermute | solution.py:237
  88.2 0.8 copy-done.3
  89.1 6.0 %pass2.3.refs_8_ = bf16[2048,256]{1,0:T(8,128)(2,1)} custom-call(s32[2]{0:T(128)} %copy-done.11, bf16[8192,256]{1,0:T(8,128)(2,1)} %c_ref.5, bf16[1024,256]{1,0:T(8,128)(2,1)} %refs_0_.5, bf16[1024,256]{1,0:T(8,128)(2,1)} %copy-done.3, bf16[1024,256]{1,0:T(8,128)(2,1)} %copy-done.2, bf16[1024,256]{1,0:T(8,128)(2,1)} %copy-done.4, ...), custom_call_target="tpu_custom_call" | custom-call | flops 2147483648 | bytes 2097152 | tf_op jit(solution)/shard_map/pass2/pallas_call | solution.py:217
  95.2 6.0 %pass2.4.refs_8_ = bf16[2048,256]{1,0:T(8,128)(2,1)} custom-call(s32[2]{0:T(128)} %get-tuple-element.25.base_ref, bf16[8192,256]{1,0:T(8,128)(2,1)} %c_ref.5, bf16[1024,256]{1,0:T(8,128)(2,1)} %refs_0_.5, bf16[1024,256]{1,0:T(8,128)(2,1)} %copy-done.3, bf16[1024,256]{1,0:T(8,128)(2,1)} %copy-done.2, ...), custom_call_target="tpu_custom_call", output_to_operand_aliasing={{}: (10, {})} | custom-call | flops 2147483648 | bytes 2097152 | tf_op jit(solution)/shard_map/pass2/pallas_call | solution.py:217
  101.2 2.8 %collective-permute-start.12 = (bf16[256,256]{1,0:T(8,128)(2,1)S(1)}, bf16[256,256]{1,0:T(8,128)(2,1)S(1)}, u32[]{:S(2)}, u32[]{:S(2)}) collective-permute-start(bf16[256,256]{1,0:T(8,128)(2,1)S(1)} %add_convert_fusion), channel_id=1, source_target_pairs={{0,3},{1,2},{2,1},{3,0},{4,7},{5,6},{6,5},{7,4},{8,11},{9,10},{10,... | collective-permute-start | bytes 393224 | tf_op jit(solution)/shard_map/ppermute | solution.py:237
  104.0 0.8 collective-permute-start.11
  105.4 9.1 %pass2.5 = bf16[2048,256]{1,0:T(8,128)(2,1)} custom-call(s32[2]{0:T(128)} %multiply_add_fusion.base_ref, bf16[8192,256]{1,0:T(8,128)(2,1)} %c_ref.5, bf16[1024,256]{1,0:T(8,128)(2,1)} %refs_0_.5, bf16[1024,256]{1,0:T(8,128)(2,1)} %copy-done.3, bf16[1024,256]{1,0:T(8,128)(2,1)} %copy-done.2, ...), custom_call_target="tpu_custom_call", output_to_operand_aliasing={{}: (10, {})} | custom-call | flops 4294967296 | bytes 2097152 | tf_op jit(solution)/shard_map/pass2/pallas_call | solution.py:217
  114.7 0.8 pad_maximum_fusion.1
  (44 shorter events, 2.4 us)
Async XLA Ops:
  2.5 36.1 %copy-start.1 = (bf16[1024,256]{1,0:T(8,128)(2,1)S(1)}, bf16[1024,256]{1,0:T(8,128)(2,1)}, u32[]{:S(2)}) copy-start(bf16[1024,256]{1,0:T(8,128)(2,1)} %refs_0_.5) | copy-start | bytes 1572868
  2.6 41.9 %copy-start.7 = (s32[1024]{0:T(1024)S(1)}, s32[1024]{0:T(1024)}, u32[]{:S(2)}) copy-start(s32[1024]{0:T(1024)} %param.8) | copy-start | bytes 12292
  27.5 39.2 %all-to-all-start = ((f32[128,8,256]{2,1,0:T(8,128)}), f32[128,8,256]{2,1,0:T(8,128)S(1)}, u32[]{:S(2)}, u32[]{:S(2)}) async-start(f32[128,8,256]{2,1,0:T(8,128)} %broadcast_in_dim.2), calls=%async_computation | async-start | bytes 2097152 | tf_op jit(solution)/shard_map/all_to_all | solution.py:253
  38.7 26.9 %collective-permute-start.14 = (bf16[1024,256]{1,0:T(8,128)(2,1)S(1)}, bf16[1024,256]{1,0:T(8,128)(2,1)S(1)}, u32[]{:S(2)}, u32[]{:S(2)}) collective-permute-start(bf16[1024,256]{1,0:T(8,128)(2,1)S(1)} %copy-done.1), channel_id=1, source_target_pairs={{0,64},{32,96},{64,0},{96,32},{1,65},{33,97},{65,1},{97,33},{2,66}... | collective-permute-start | bytes 1572872 | tf_op jit(solution)/shard_map/ppermute | solution.py:237
  39.7 30.0 %collective-permute-start.3 = (bf16[512,256]{1,0:T(8,128)(2,1)}, bf16[512,256]{1,0:T(8,128)(2,1)S(1)}, u32[]{:S(2)}, u32[]{:S(2)}) collective-permute-start(bf16[512,256]{1,0:T(8,128)(2,1)} %get-tuple-element.18), channel_id=1, source_target_pairs={{0,1},{1,0},{2,3},{3,2},{4,5},{5,4},{6,7},{7,6},{8,9},{9,8},{10,11... | collective-permute-start | bytes 786440 | tf_op jit(solution)/shard_map/ppermute | solution.py:237
  41.2 28.6 %collective-permute-start.4 = (bf16[512,256]{1,0:T(8,128)(2,1)}, bf16[512,256]{1,0:T(8,128)(2,1)}, u32[]{:S(2)}, u32[]{:S(2)}) collective-permute-start(bf16[512,256]{1,0:T(8,128)(2,1)} %get-tuple-element.19), channel_id=1, source_target_pairs={{0,2},{1,3},{2,0},{3,1},{4,6},{5,7},{6,4},{7,5},{8,10},{9,11},{10,... | collective-permute-start | bytes 786440 | tf_op jit(solution)/shard_map/ppermute | solution.py:237
  43.9 25.9 %collective-permute-start.5 = (bf16[512,256]{1,0:T(8,128)(2,1)}, bf16[512,256]{1,0:T(8,128)(2,1)}, u32[]{:S(2)}, u32[]{:S(2)}) collective-permute-start(bf16[512,256]{1,0:T(8,128)(2,1)} %get-tuple-element.20), channel_id=1, source_target_pairs={{0,3},{1,2},{2,1},{3,0},{4,7},{5,6},{6,5},{7,4},{8,11},{9,10},{10,... | collective-permute-start | bytes 786440 | tf_op jit(solution)/shard_map/ppermute | solution.py:237
  44.4 22.2 %copy-start.6 = (s32[4,256]{1,0:T(4,128)}, s32[4,256]{1,0:T(4,128)S(1)}, u32[]{:S(2)}) copy-start(s32[4,256]{1,0:T(4,128)S(1)} %reshape.13.p0) | copy-start | bytes 12292
  44.4 1.2 %collective-permute-start = (s32[4,256]{1,0:T(4,128)S(1)}, s32[4,256]{1,0:T(4,128)S(1)}, u32[]{:S(2)}, u32[]{:S(2)}) collective-permute-start(s32[4,256]{1,0:T(4,128)S(1)} %reshape.13.p0), channel_id=1, source_target_pairs={{0,32},{32,0},{64,96},{96,64},{1,33},{33,1},{65,97},{97,65},{2,34}... | collective-permute-start | bytes 12296 | tf_op jit(solution)/shard_map/ppermute | solution.py:237
  45.7 21.0 %copy-start.8 = (s32[4,256]{1,0:T(4,128)}, s32[4,256]{1,0:T(4,128)S(1)}, u32[]{:S(2)}) copy-start(s32[4,256]{1,0:T(4,128)S(1)} %collective-permute-done.p1) | copy-start | bytes 12292
  45.7 16.8 %collective-permute-start.1 = (s32[4,256]{1,0:T(4,128)S(1)}, s32[4,256]{1,0:T(4,128)S(1)}, u32[]{:S(2)}, u32[]{:S(2)}) collective-permute-start(s32[4,256]{1,0:T(4,128)S(1)} %reshape.13.p0), channel_id=1, source_target_pairs={{0,64},{32,96},{64,0},{96,32},{1,65},{33,97},{65,1},{97,33},{2,66}... | collective-permute-start | bytes 12296 | tf_op jit(solution)/shard_map/ppermute | solution.py:237
  62.5 4.2 %copy-start.9 = (s32[4,256]{1,0:T(4,128)}, s32[4,256]{1,0:T(4,128)S(1)}, u32[]{:S(2)}) copy-start(s32[4,256]{1,0:T(4,128)S(1)} %collective-permute-done.1.p2) | copy-start | bytes 12292
  62.5 3.0 %collective-permute-start.2 = (s32[4,256]{1,0:T(4,128)S(1)}, s32[4,256]{1,0:T(4,128)S(1)}, u32[]{:S(2)}, u32[]{:S(2)}) collective-permute-start(s32[4,256]{1,0:T(4,128)S(1)} %reshape.13.p0), channel_id=1, source_target_pairs={{0,96},{32,64},{64,32},{96,0},{1,97},{33,65},{65,33},{97,1},{2,98}... | collective-permute-start | bytes 12296 | tf_op jit(solution)/shard_map/ppermute | solution.py:237
  65.5 1.2 copy-start.10
  65.5 22.6 %collective-permute-start.13 = (bf16[1024,256]{1,0:T(8,128)(2,1)S(1)}, bf16[1024,256]{1,0:T(8,128)(2,1)S(1)}, u32[]{:S(2)}, u32[]{:S(2)}) collective-permute-start(bf16[1024,256]{1,0:T(8,128)(2,1)S(1)} %copy-done.1), channel_id=1, source_target_pairs={{0,32},{32,0},{64,96},{96,64},{1,33},{33,1},{65,97},{97,65},{2,34}... | collective-permute-start | bytes 1572872 | tf_op jit(solution)/shard_map/ppermute | solution.py:237
  65.5 22.6 %copy-start.2 = (bf16[1024,256]{1,0:T(8,128)(2,1)}, bf16[1024,256]{1,0:T(8,128)(2,1)S(1)}, u32[]{:S(2)}) copy-start(bf16[1024,256]{1,0:T(8,128)(2,1)S(1)} %collective-permute-done.14.refs_2_) | copy-start | bytes 1572868
  65.6 22.6 %collective-permute-start.15 = (bf16[1024,256]{1,0:T(8,128)(2,1)S(1)}, bf16[1024,256]{1,0:T(8,128)(2,1)S(1)}, u32[]{:S(2)}, u32[]{:S(2)}) collective-permute-start(bf16[1024,256]{1,0:T(8,128)(2,1)S(1)} %collective-permute-done.14.refs_2_), channel_id=1, source_target_pairs={{0,32},{32,0},{64,96},{96,64},{1,33},{33,1},{65,97},{97,65},{2,34}... | collective-permute-start | bytes 1572872 | tf_op jit(solution)/shard_map/ppermute | solution.py:237
  66.7 21.5 %copy-start.11 = (s32[2]{0:T(128)}, s32[2]{0:T(128)S(1)}, u32[]{:S(2)}) copy-start(s32[2]{0:T(128)S(1)} %get-tuple-element.26.base_ref) | copy-start | bytes 28
  66.7 1.0 copy-start
  69.8 0.7 copy-start.5
  72.6 9.6 %collective-permute-start.8 = (bf16[256,256]{1,0:T(8,128)(2,1)}, bf16[256,256]{1,0:T(8,128)(2,1)S(1)}, u32[]{:S(2)}, u32[]{:S(2)}) collective-permute-start(bf16[256,256]{1,0:T(8,128)(2,1)} %combine.1), channel_id=1, source_target_pairs={{0,24},{8,16},{16,8},{24,0},{1,25},{9,17},{17,9},{25,1},{2,26},{10... | collective-permute-start | bytes 393224 | tf_op jit(solution)/shard_map/ppermute | solution.py:237
  76.0 8.1 %collective-permute-start.7 = (bf16[256,256]{1,0:T(8,128)(2,1)}, bf16[256,256]{1,0:T(8,128)(2,1)S(1)}, u32[]{:S(2)}, u32[]{:S(2)}) collective-permute-start(bf16[256,256]{1,0:T(8,128)(2,1)} %combine.1), channel_id=1, source_target_pairs={{0,16},{8,24},{16,0},{24,8},{1,17},{9,25},{17,1},{25,9},{2,18},{10... | collective-permute-start | bytes 393224 | tf_op jit(solution)/shard_map/ppermute | solution.py:237
  76.3 7.8 %collective-permute-start.6 = (bf16[256,256]{1,0:T(8,128)(2,1)}, bf16[256,256]{1,0:T(8,128)(2,1)S(1)}, u32[]{:S(2)}, u32[]{:S(2)}) collective-permute-start(bf16[256,256]{1,0:T(8,128)(2,1)} %combine.1), channel_id=1, source_target_pairs={{0,8},{8,0},{16,24},{24,16},{1,9},{9,1},{17,25},{25,17},{2,10},{10... | collective-permute-start | bytes 393224 | tf_op jit(solution)/shard_map/ppermute | solution.py:237
  85.0 16.2 %collective-permute-start.9 = (f32[256,256]{1,0:T(8,128)S(1)}, f32[256,256]{1,0:T(8,128)S(1)}, u32[]{:S(2)}, u32[]{:S(2)}) collective-permute-start(f32[256,256]{1,0:T(8,128)S(1)} %add_add_fusion), channel_id=1, source_target_pairs={{0,4},{4,0},{1,5},{5,1},{2,6},{6,2},{3,7},{7,3},{8,12},{12,8},{9,1... | collective-permute-start | bytes 786440 | tf_op jit(solution)/shard_map/ppermute | solution.py:237
  88.1 0.8 copy-start.3
  88.2 1.0 copy-start.4
  101.2 13.3 %collective-permute-start.12 = (bf16[256,256]{1,0:T(8,128)(2,1)S(1)}, bf16[256,256]{1,0:T(8,128)(2,1)S(1)}, u32[]{:S(2)}, u32[]{:S(2)}) collective-permute-start(bf16[256,256]{1,0:T(8,128)(2,1)S(1)} %add_convert_fusion), channel_id=1, source_target_pairs={{0,3},{1,2},{2,1},{3,0},{4,7},{5,6},{6,5},{7,4},{8,11},{9,10},{10,... | collective-permute-start | bytes 393224 | tf_op jit(solution)/shard_map/ppermute | solution.py:237
  104.0 10.5 %collective-permute-start.11 = (bf16[256,256]{1,0:T(8,128)(2,1)S(1)}, bf16[256,256]{1,0:T(8,128)(2,1)S(1)}, u32[]{:S(2)}, u32[]{:S(2)}) collective-permute-start(bf16[256,256]{1,0:T(8,128)(2,1)S(1)} %add_convert_fusion), channel_id=1, source_target_pairs={{0,2},{1,3},{2,0},{3,1},{4,6},{5,7},{6,4},{7,5},{8,10},{9,11},{10,... | collective-permute-start | bytes 393224 | tf_op jit(solution)/shard_map/ppermute | solution.py:237
  104.9 9.7 %collective-permute-start.10 = (bf16[256,256]{1,0:T(8,128)(2,1)S(1)}, bf16[256,256]{1,0:T(8,128)(2,1)S(1)}, u32[]{:S(2)}, u32[]{:S(2)}) collective-permute-start(bf16[256,256]{1,0:T(8,128)(2,1)S(1)} %add_convert_fusion), channel_id=1, source_target_pairs={{0,1},{1,0},{2,3},{3,2},{4,5},{5,4},{6,7},{7,6},{8,9},{9,8},{10,11... | collective-permute-start | bytes 393224 | tf_op jit(solution)/shard_map/ppermute | solution.py:237

commit v3 on v2

v3 whole, which is shorter than its diff:
```python
import functools
import math

import jax
import jax.numpy as jnp
from jax import lax
from jax.experimental import pallas as pl
from jax.experimental.pallas import tpu as pltpu
from jax.sharding import Mesh
from jax.sharding import PartitionSpec as P

sharpness_divisor = 4.0
SCALE = math.log2(math.e) / sharpness_divisor
NT = (((1,), (1,)), ((), ()))
ITEM = ("z", "y_hi", "x")
USER = ("y_lo", "core")
VMEM = pl.BlockSpec(memory_space=pltpu.VMEM)
SMEM = pl.BlockSpec(memory_space=pltpu.SMEM)
ANY = pl.BlockSpec(memory_space=pl.ANY)
f32 = jnp.float32
bf16 = jnp.bfloat16


def exp_of(x):
    return jnp.exp2(x * SCALE)


def struct(*shape, dtype=f32):
    return jax.ShapeDtypeStruct(shape, dtype)


def as_row(column):
    return jnp.broadcast_to(column, (128, 128)).T[0:1]


def as_column(row):
    return jnp.broadcast_to(row, (128, 128)).T


def pass1_kernel(tile, rb, u_ref, cat_ref, *refs):
    out_refs, every_ref, (c_ref, acc_ref, m_ref, l_ref, st_ref, sem) = refs[:4], refs[4], refs[5:]
    rows = u_ref.shape[0]
    count, width = cat_ref.shape
    n = count // tile
    copies = []
    for i in range(n):
        part = pl.ds(i * tile, tile)
        copies.append(pltpu.make_async_copy(cat_ref.at[part], c_ref.at[part], sem.at[i]))
        copies[-1].start()
    acc_ref[...] = jnp.zeros_like(acc_ref)
    m_ref[...] = jnp.full_like(m_ref, -1e38)
    l_ref[...] = jnp.zeros_like(l_ref)
    for i in range(n):
        copies[i].wait()
        c = c_ref[i * tile : (i + 1) * tile]
        for b in range(rows // rb):
            sl = slice(b * rb, (b + 1) * rb)
            r = lax.dot_general(u_ref[sl], c, NT, preferred_element_type=f32)
            m_old = m_ref[sl]
            m_new = jnp.maximum(m_old, jnp.max(r, axis=1, keepdims=True))
            alpha = exp_of(m_old - m_new)
            m_ref[sl] = m_new
            total = l_ref[sl] * alpha
            ps = []
            for j in range(tile // 128):
                p = exp_of(r[:, j * 128 : (j + 1) * 128] - m_new)
                total = total + p
                ps.append(p.astype(bf16))
            l_ref[sl] = total
            wide = jnp.concatenate([alpha] * (width // 128), axis=1)
            acc_ref[sl] = acc_ref[sl] * wide + jnp.dot(
                jnp.concatenate(ps, axis=1), c, preferred_element_type=f32
            )
    for b in range(rows // 128):
        sl = slice(b * 128, (b + 1) * 128)
        total = jnp.sum(l_ref[sl], axis=1, keepdims=True)
        acc_ref[sl] = acc_ref[sl] * (1.0 / total)
        st_ref[b : b + 1] = m_ref[sl].T[0:1] + sharpness_divisor * jnp.log(as_row(total))
    every_ref[...] = jnp.broadcast_to(st_ref[...][None], every_ref.shape)
    x = lax.axis_index("x")
    chunk = rows // 4
    for k, out_ref in enumerate(out_refs):
        part = pl.ds(pl.multiple_of((x ^ k) * chunk, chunk), chunk)
        out_ref[...] = acc_ref[part, :].astype(bf16)


def pass1(users, catalog, tile=2048, rb=256):
    rows, width = users.shape
    count = catalog.shape[0]
    return pl.pallas_call(
        functools.partial(pass1_kernel, tile, rb),
        in_specs=[VMEM, ANY],
        out_specs=[VMEM] * 5,
        out_shape=[struct(rows // 4, width, dtype=bf16)] * 4 + [struct(128, rows // 128, 128)],
        scratch_shapes=[
            pltpu.VMEM((count, width), bf16),
            pltpu.VMEM((rows, width), f32),
            pltpu.VMEM((rows, 128), f32),
            pltpu.VMEM((rows, 128), f32),
            pltpu.VMEM((rows // 128, 128), f32),
            pltpu.SemaphoreType.DMA((count // tile,)),
        ],
        cost_estimate=pl.CostEstimate(
            flops=4 * rows * count * width, bytes_accessed=2 * count * width, transcendentals=rows * count
        ),
        name="pass1",
    )(users, catalog)


def hits_kernel(pos_ref, u_ref, c_ref, *refs):
    out_refs, own_ref, hit_ref, sp_ref = refs[:4], refs[4], refs[5], refs[6]
    rows, width = u_ref.shape
    count = c_ref.shape[0]
    items = own_ref.shape[0]
    x, member, shard = lax.axis_index("x"), lax.axis_index(USER), lax.axis_index(ITEM)
    own_ref[...] = c_ref[pl.ds(pl.multiple_of(member * items, items), items), :]
    hit_ref[...] = jnp.zeros_like(hit_ref)
    base = shard * count

    @pl.loop(0, rows // 8)
    def _(g):
        here = [pos_ref[g * 8 + j] - base for j in range(8)]
        mine = [(h >= 0) & (h < count) for h in here]

        @pl.when(functools.reduce(jnp.logical_or, mine))
        def _():
            for j in range(8):

                @pl.when(mine[j])
                def _():
                    start = pl.multiple_of((here[j] >> 4) << 4, 16)
                    group = c_ref[pl.ds(start, 16), :].astype(f32)
                    inside = lax.broadcasted_iota(jnp.int32, group.shape, 0) == (here[j] & 15)
                    row = jnp.sum(jnp.where(inside, group, 0.0), axis=0, keepdims=True)
                    hit_ref[pl.ds(g * 8 + j, 1), :] = row

    for b in range(rows // 128):
        sl = slice(b * 128, (b + 1) * 128)
        score = jnp.sum(hit_ref[sl] * u_ref[sl].astype(f32), axis=1, keepdims=True)
        sp_ref[b : b + 1] = as_row(score)
    chunk = rows // 4
    for k, out_ref in enumerate(out_refs):
        part = pl.ds(pl.multiple_of((x ^ k) * chunk, chunk), chunk)
        out_ref[0:chunk] = hit_ref[part, :].astype(bf16)
        rest = jnp.concatenate([sp_ref[pl.ds((x ^ k) * 2 + h, 1), :] for h in range(2)], axis=1)
        terms = []
        for _ in range(3):
            term = rest.astype(bf16).astype(f32)
            rest = rest - term
            terms.append(term)
        terms.append(jnp.zeros((13, width), f32))
        out_ref[chunk:] = jnp.concatenate(terms, axis=0).astype(bf16)


def find_hits(positives, users, catalog):
    rows, width = users.shape
    count = catalog.shape[0]
    return pl.pallas_call(
        hits_kernel,
        in_specs=[SMEM, VMEM, VMEM],
        out_specs=[VMEM] * 5,
        out_shape=[struct(rows // 4 + 16, width, dtype=bf16)] * 4 + [struct(count // 4, width, dtype=bf16)],
        scratch_shapes=[pltpu.VMEM((rows, width), f32), pltpu.VMEM((rows // 128, 128), f32)],
        cost_estimate=pl.CostEstimate(
            flops=rows * count * width // 2, bytes_accessed=2 * count * width, transcendentals=0
        ),
        name="hits",
    )(positives, users, catalog)


def combine_kernel(all_ref, *refs):
    u_refs, h_refs, l_refs, out_ref = refs[:4], refs[4:8], refs[8:12], refs[12]
    x, member, shard = lax.axis_index("x"), lax.axis_index(USER), lax.axis_index(ITEM)
    shards = all_ref.shape[0] // 4
    chunk, width = u_refs[0].shape
    for k, l_ref in enumerate(l_refs):
        stats = all_ref[pl.ds((member ^ k) * shards, shards)]
        top = jnp.max(stats, axis=0)
        l_ref[...] = top + sharpness_divisor * jnp.log(jnp.sum(exp_of(stats - top[None]), axis=0))
    for h in range(chunk // 128):
        sl = slice(h * 128, (h + 1) * 128)
        row = pl.ds(x * 2 + h, 1)
        total = jnp.zeros((128, width), f32)
        for k in range(4):
            weight = exp_of(all_ref[member * shards + (shard ^ k), row, :] - l_refs[0][row, :])
            wide = jnp.concatenate([as_column(weight)] * (width // 128), axis=1)
            total = total + wide * u_refs[k][sl].astype(f32) - h_refs[k][sl].astype(f32)
        out_ref[sl] = (total / sharpness_divisor).astype(bf16)
    scores = [h_ref[chunk:].astype(f32) for h_ref in h_refs]
    out_ref[chunk:] = ((scores[0] + scores[1]) + (scores[2] + scores[3])).astype(bf16)


def combine(every, us, hs):
    rows, width = hs[0].shape
    return pl.pallas_call(
        combine_kernel,
        in_specs=[VMEM] * 9,
        out_specs=[VMEM] * 5,
        out_shape=[struct(*every.shape[1:])] * 4 + [struct(rows, width, dtype=bf16)],
        name="combine",
    )(every, *us, *hs)


def finish_kernel(lse_ref, *refs):
    parts, out_ref, loss_ref = refs[:4], refs[4], refs[5]
    x = lax.axis_index("x")
    chunk = out_ref.shape[0] // 4
    for k, part in enumerate(parts):
        out_ref[pl.ds(pl.multiple_of((x ^ k) * chunk, chunk), chunk), :] = part[0:chunk]
        terms = part[chunk:].astype(f32)
        score = terms[0:1] + terms[1:2] + terms[2:3]
        for h in range(2):
            row = pl.ds((x ^ k) * 2 + h, 1)
            loss_ref[row, :] = (lse_ref[row, :] - score[:, h * 128 : (h + 1) * 128]) / sharpness_divisor


def finish(lse4, parts, rows):
    width = parts[0].shape[1]
    return pl.pallas_call(
        finish_kernel,
        in_specs=[VMEM] * 5,
        out_specs=[VMEM] * 2,
        out_shape=[struct(rows, width, dtype=bf16), struct(*lse4.shape)],
        name="finish",
    )(lse4, *parts)


def pass2_kernel(tile, lead, c_ref, *refs):
    us, lses, poss, out_ref = refs[:4], refs[4:8], refs[8:12], refs[-1]
    member, shard = lax.axis_index(USER), lax.axis_index(ITEM)
    start = (lead + pl.program_id(0)) * tile
    items = c_ref.shape[0]
    c = c_ref[pl.ds(pl.multiple_of(start, tile), tile), :]
    item = lax.broadcasted_iota(jnp.int32, (tile, 128), 0) + (shard * 4 + member) * items + start
    total = jnp.zeros((tile, c.shape[1]), f32)
    for u_ref, l_ref, pos_ref in zip(us, lses, poss):
        u = u_ref[...]
        r = lax.dot_general(c, u, NT, preferred_element_type=f32)
        ws = []
        for j in range(u.shape[0] // 128):
            w = exp_of(r[:, j * 128 : (j + 1) * 128] - l_ref[j : j + 1])
            ws.append(jnp.where(pos_ref[j : j + 1] == item, w - 1.0, w).astype(bf16))
        total = total + jnp.dot(jnp.concatenate(ws, axis=1), u, preferred_element_type=f32)
    out_ref[...] = (total / sharpness_divisor).astype(out_ref.dtype)


def pass2(own, us, lses, poss, start, stop, before, tile=512):
    items, width = own.shape
    rows = us[0].shape[0]
    lead = start // tile
    in_specs = [VMEM] * 13
    args = [own, *us, *lses, *poss]
    aliases = {}
    if before is not None:
        in_specs.append(ANY)
        aliases = {len(args): 0}
        args.append(before)
    return pl.pallas_call(
        functools.partial(pass2_kernel, tile, lead),
        grid=((stop - start) // tile,),
        in_specs=in_specs,
        out_specs=pl.BlockSpec((tile, width), lambda i: (lead + i, 0)),
        out_shape=struct(items, width, dtype=bf16),
        input_output_aliases=aliases,
        cost_estimate=pl.CostEstimate(
            flops=16 * rows * (stop - start) * width,
            bytes_accessed=8 * rows * width,
            transcendentals=4 * rows * (stop - start),
        ),
        name="pass2",
    )(*args)


def swap(x, axis, size, k):
    return lax.ppermute(x, axis, [(i, i ^ k) for i in range(size)])


def per_device(users, catalog, positives):
    rows = users.shape[0]
    items = catalog.shape[0] // 4
    pos = positives.reshape(rows // 128, 128)
    over = swap(users, USER, 4, 2)
    us = [users, swap(users, USER, 4, 1), over, swap(over, USER, 4, 1)]
    poss = [pos] + [swap(pos, USER, 4, k) for k in (1, 2, 3)]
    *pieces, every = pass1(users, catalog)
    every = lax.all_to_all(every, USER + ITEM, 0, 0, tiled=True)
    *hits, own = find_hits(positives, users, catalog)
    pieces = [pieces[0]] + [swap(pieces[k], "x", 4, k) for k in (1, 2, 3)]
    hits = [hits[0]] + [swap(hits[k], "x", 4, k) for k in (1, 2, 3)]
    *lses, value = combine(every, pieces, hits)

    a = [value] + [swap(value, "z", 4, k) for k in (1, 2, 3)]
    item_grad = pass2(own, us, lses, poss, 0, SPLIT[0], None)
    a = [v.astype(f32) for v in a]
    value = (a[0] + a[1]) + (a[2] + a[3])
    other = swap(value, "y_hi", 2, 1)
    item_grad = pass2(own, us, lses, poss, SPLIT[0], SPLIT[1], item_grad)
    value = (value + other).astype(bf16)
    got = [value] + [swap(value, "x", 4, k) for k in (1, 2, 3)]
    item_grad = pass2(own, us, lses, poss, SPLIT[1], items, item_grad)
    user_grad, loss = finish(lses[0], got, rows)
    return loss.reshape(rows), user_grad, item_grad


SPLIT = (512, 1024)


def solution(mesh):
    grid = Mesh(mesh.devices.reshape(2, 2, 4, 2, 4), USER + ITEM)

    return jax.shard_map(
        per_device,
        mesh=grid,
        in_specs=(P(USER, None), P(ITEM, None), P(USER)),
        out_specs=(P(USER), P(USER, None), P(ITEM + USER, None)),
        check_vma=False,
    )
```

time: 116 us -> 114 us (0.983)
  starting transfers between devices: 30.1 us -> 36.4 us
  waiting for transfers between devices: 25.4 us -> 20.8 us
  other arithmetic: 4.95 us -> 1.01 us
  Pallas kernels: 48.6 us -> 51.1 us
  local copies, waits for them, and re-layouts: 5.68 us -> 3.22 us
    ppermute x16 -> x19, starting transfers between devices: 18.9 us -> 25.3 us  [swap(): return lax.ppermute(x, axis, [(i, i ^ k) for i in range(size)])]
    ppermute x16 -> x19, waiting for transfers between devices: 25.4 us -> 20.8 us  [swap(): return lax.ppermute(x, axis, [(i, i ^ k) for i in range(size)])]
    pallas_call x6 -> x7, Pallas kernels: 48.6 us -> 51.1 us  [the longest x3 20 us: pass2(): pl.pallas_call(functools.partial(pass2_kernel, tile, lead), grid=((stop -...]
    broadcast_in_dim x1 -> x0, local copies, waits for them, and re-layouts: 1.73 us -> none  [per_device(): every = jnp.broadcast_to(stats[None], (128,) + stats.shape)]
    sub x1 -> x0, other arithmetic: 1.28 us -> none  [per_device(): *pieces, stats = pass1(users, catalog, positives - shard * count, me)]
    unnamed x25 -> x42, local copies, waits for them, and re-layouts: 3.89 us -> 3.22 us
  transfers between devices with their start and end apart: 17 -> 20, of which waited for: 5 -> 5; matrix products, arithmetic and copies ran while one was open for 3% -> 1% of each run, Pallas kernels for 22% -> 28%
where the time goes in v3:
time: 114 us; the launch traced here: 113 us
  Pallas kernels  51.1 us (45%)
  starting transfers between devices  36.4 us (32%)
  waiting for transfers between devices  20.8 us (18%)
  local copies, waits for them, and re-layouts  3.22 us (3%)
    ppermute x19, starting transfers between devices, swap(): return lax.ppermute(x, axis, [(i, i ^ k) for i in range(size)])  25.3 us
    ppermute x19, waiting for transfers between devices, swap(): return lax.ppermute(x, axis, [(i, i ^ k) for i in range(size)])  20.8 us
    pallas_call x3, Pallas kernels, pass2(): pl.pallas_call(functools.partial(pass2_kernel, tile, lead), grid=((stop -...  20 us
    pallas_call x1, Pallas kernels, pass1(): pl.pallas_call(functools.partial(pass1_kernel, tile, rb), in_specs=[VMEM,...  17.2 us
    all_to_all x1, starting transfers between devices, per_device(): every = lax.all_to_all(every, USER + ITEM, 0, 0, tiled=True)  11.2 us
    pallas_call x1, Pallas kernels, find_hits(): pl.pallas_call(hits_kernel, in_specs=[SMEM, VMEM, VMEM], out_specs=[VMEM]...  9.41 us
    unnamed x42, local copies, waits for them, and re-layouts  3.22 us
    pallas_call x1, Pallas kernels, combine(): pl.pallas_call(combine_kernel, in_specs=[VMEM] * 9, out_specs=[VMEM] * 5,...  2.51 us
  transfers between devices with their start and end apart: 20, of which 5 were waited for; matrix products, arithmetic and copies ran while one was open for 1% of the time, Pallas kernels for 28%

profile of v3, /device:TPU:0, one launch (start us, length us, event | category | flops | bytes accessed | tf_op | source)
XLA Modules:
  0.0 113.5 jit_solution(13031016650423035075)
XLA Ops:
  0.6 17.2 %pass1.1 = (bf16[256,256]{1,0:T(8,128)(2,1)}, bf16[256,256]{1,0:T(8,128)(2,1)}, bf16[256,256]{1,0:T(8,128)(2,1)}, bf16[256,256]{1,0:T(8,128)(2,1)}, f32[128,8,128]{2,1,0:T(8,128)}) custom-call(bf16[1024,256]{1,0:T(8,128)(2,1)} %refs_0_.5, bf16[8192,256]{1,0:T(8,128)(2,1)} %c_ref.1), custom_call_target="tpu_custom_call" | custom-call | flops 8589934592 | bytes 4194304 | tf_op jit(solution)/shard_map/pass1/pallas_call | solution.py:90
  17.9 11.2 %all-to-all-start = ((f32[128,8,128]{2,1,0:T(8,128)}), f32[128,8,128]{2,1,0:T(8,128)S(1)}, u32[]{:S(2)}, u32[]{:S(2)}) async-start(f32[128,8,128]{2,1,0:T(8,128)} %get-tuple-element.20), calls=%async_computation | async-start | bytes 1048576 | tf_op jit(solution)/shard_map/all_to_all | solution.py:286
  29.1 1.0 collective-permute-start.14
  30.1 1.5 %collective-permute-start = (bf16[256,256]{1,0:T(8,128)(2,1)}, bf16[256,256]{1,0:T(8,128)(2,1)S(1)}, u32[]{:S(2)}, u32[]{:S(2)}) collective-permute-start(bf16[256,256]{1,0:T(8,128)(2,1)} %get-tuple-element.22), channel_id=1, source_target_pairs={{0,1},{1,0},{2,3},{3,2},{4,5},{5,4},{6,7},{7,6},{8,9},{9,8},{10,11... | collective-permute-start | bytes 393224 | tf_op jit(solution)/shard_map/ppermute | solution.py:275
  31.6 2.7 %collective-permute-start.1 = (bf16[256,256]{1,0:T(8,128)(2,1)}, bf16[256,256]{1,0:T(8,128)(2,1)S(1)}, u32[]{:S(2)}, u32[]{:S(2)}) collective-permute-start(bf16[256,256]{1,0:T(8,128)(2,1)} %get-tuple-element.23), channel_id=1, source_target_pairs={{0,2},{1,3},{2,0},{3,1},{4,6},{5,7},{6,4},{7,5},{8,10},{9,11},{10,... | collective-permute-start | bytes 393224 | tf_op jit(solution)/shard_map/ppermute | solution.py:275
  34.3 9.4 %hits.1 = (bf16[272,256]{1,0:T(8,128)(2,1)}, bf16[272,256]{1,0:T(8,128)(2,1)}, bf16[272,256]{1,0:T(8,128)(2,1)}, bf16[272,256]{1,0:T(8,128)(2,1)}, bf16[2048,256]{1,0:T(8,128)(2,1)}) custom-call(s32[1024]{0:T(1024)} %pos_ref.1, bf16[1024,256]{1,0:T(8,128)(2,1)} %refs_0_.5, bf16[8192,256]{1,0:T(8,128)(2,1)} %c_ref.1), custom_call_target="tpu_custom_call" | custom-call | flops 1073741824 | bytes 4194304 | tf_op jit(solution)/shard_map/hits/pallas_call | solution.py:158
  43.9 2.0 %collective-permute-start.4 = (bf16[272,256]{1,0:T(8,128)(2,1)}, bf16[272,256]{1,0:T(8,128)(2,1)S(1)}, u32[]{:S(2)}, u32[]{:S(2)}) collective-permute-start(bf16[272,256]{1,0:T(8,128)(2,1)} %get-tuple-element.27), channel_id=1, source_target_pairs={{0,2},{1,3},{2,0},{3,1},{4,6},{5,7},{6,4},{7,5},{8,10},{9,11},{10,... | collective-permute-start | bytes 417800 | tf_op jit(solution)/shard_map/ppermute | solution.py:275
  45.8 2.6 %collective-permute-start.5 = (bf16[272,256]{1,0:T(8,128)(2,1)}, bf16[272,256]{1,0:T(8,128)(2,1)S(1)}, u32[]{:S(2)}, u32[]{:S(2)}) collective-permute-start(bf16[272,256]{1,0:T(8,128)(2,1)} %get-tuple-element.28), channel_id=1, source_target_pairs={{0,3},{1,2},{2,1},{3,0},{4,7},{5,6},{6,5},{7,4},{8,11},{9,10},{10,... | collective-permute-start | bytes 417800 | tf_op jit(solution)/shard_map/ppermute | solution.py:275
  48.4 0.7 collective-permute-start.2
  49.1 8.0 %collective-permute-done.2.refs_3_ = bf16[256,256]{1,0:T(8,128)(2,1)S(1)} collective-permute-done((bf16[256,256]{1,0:T(8,128)(2,1)S(1)}, bf16[256,256]{1,0:T(8,128)(2,1)S(1)}, u32[]{:S(2)}, u32[]{:S(2)}) %collective-permute-start.2) | collective-permute-done | bytes 131104 | tf_op jit(solution)/shard_map/ppermute | solution.py:275
  57.3 0.6 copy-done.12
  58.2 2.5 %combine.1 = (f32[8,128]{1,0:T(8,128)}, f32[8,128]{1,0:T(8,128)}, f32[8,128]{1,0:T(8,128)}, f32[8,128]{1,0:T(8,128)}, bf16[272,256]{1,0:T(8,128)(2,1)}) custom-call(f32[128,8,128]{2,1,0:T(8,128)} %copy-done, bf16[256,256]{1,0:T(8,128)(2,1)} %get-tuple-element.21.refs_0_, bf16[256,256]{1,0:T(8,128)(2,1)} %copy-done.10, bf16[256,256]{1,0:T(8,128)(2,1)} %copy-done.11, ...), custom_call_target="tpu_custom_call" | custom-call | tf_op jit(solution)/shard_map/combine/pallas_call | solution.py:195
  60.7 1.2 %collective-permute-start.6 = (bf16[272,256]{1,0:T(8,128)(2,1)}, bf16[272,256]{1,0:T(8,128)(2,1)S(1)}, u32[]{:S(2)}, u32[]{:S(2)}) collective-permute-start(bf16[272,256]{1,0:T(8,128)(2,1)} %get-tuple-element.30), channel_id=1, source_target_pairs={{0,8},{8,0},{16,24},{24,16},{1,9},{9,1},{17,25},{25,17},{2,10},{10... | collective-permute-start | bytes 417800 | tf_op jit(solution)/shard_map/ppermute | solution.py:275
  61.9 3.2 %collective-permute-start.7 = (bf16[272,256]{1,0:T(8,128)(2,1)}, bf16[272,256]{1,0:T(8,128)(2,1)S(1)}, u32[]{:S(2)}, u32[]{:S(2)}) collective-permute-start(bf16[272,256]{1,0:T(8,128)(2,1)} %get-tuple-element.30), channel_id=1, source_target_pairs={{0,16},{8,24},{16,0},{24,8},{1,17},{9,25},{17,1},{25,9},{2,18},{10... | collective-permute-start | bytes 417800 | tf_op jit(solution)/shard_map/ppermute | solution.py:275
  65.1 0.3 collective-permute-start.8
  65.4 0.5 collective-permute-start.15
  65.9 1.5 %collective-permute-done.6 = bf16[272,256]{1,0:T(8,128)(2,1)S(1)} collective-permute-done((bf16[272,256]{1,0:T(8,128)(2,1)}, bf16[272,256]{1,0:T(8,128)(2,1)S(1)}, u32[]{:S(2)}, u32[]{:S(2)}) %collective-permute-start.6) | collective-permute-done | bytes 139296 | tf_op jit(solution)/shard_map/ppermute | solution.py:275
  67.4 3.6 %collective-permute-done.7 = bf16[272,256]{1,0:T(8,128)(2,1)S(1)} collective-permute-done((bf16[272,256]{1,0:T(8,128)(2,1)}, bf16[272,256]{1,0:T(8,128)(2,1)S(1)}, u32[]{:S(2)}, u32[]{:S(2)}) %collective-permute-start.7) | collective-permute-done | bytes 139296 | tf_op jit(solution)/shard_map/ppermute | solution.py:275
  71.0 1.8 %collective-permute-done.8 = bf16[272,256]{1,0:T(8,128)(2,1)S(1)} collective-permute-done((bf16[272,256]{1,0:T(8,128)(2,1)}, bf16[272,256]{1,0:T(8,128)(2,1)S(1)}, u32[]{:S(2)}, u32[]{:S(2)}) %collective-permute-start.8) | collective-permute-done | bytes 139296 | tf_op jit(solution)/shard_map/ppermute | solution.py:275
  72.8 1.0 add_add_fusion
  73.7 3.6 %collective-permute-start.9 = (f32[272,256]{1,0:T(8,128)S(1)}, f32[272,256]{1,0:T(8,128)S(1)}, u32[]{:S(2)}, u32[]{:S(2)}) collective-permute-start(f32[272,256]{1,0:T(8,128)S(1)} %add_add_fusion), channel_id=1, source_target_pairs={{0,4},{4,0},{1,5},{5,1},{2,6},{6,2},{3,7},{7,3},{8,12},{12,8},{9,1... | collective-permute-start | bytes 835592 | tf_op jit(solution)/shard_map/ppermute | solution.py:275
  77.3 5.9 %collective-permute-done.9 = f32[272,256]{1,0:T(8,128)S(1)} collective-permute-done((f32[272,256]{1,0:T(8,128)S(1)}, f32[272,256]{1,0:T(8,128)S(1)}, u32[]{:S(2)}, u32[]{:S(2)}) %collective-permute-start.9) | collective-permute-done | bytes 278560 | tf_op jit(solution)/shard_map/ppermute | solution.py:275
  83.4 4.4 %collective-permute-start.11 = (bf16[272,256]{1,0:T(8,128)(2,1)S(1)}, bf16[272,256]{1,0:T(8,128)(2,1)S(1)}, u32[]{:S(2)}, u32[]{:S(2)}) collective-permute-start(bf16[272,256]{1,0:T(8,128)(2,1)S(1)} %add_convert_fusion.refs_0_), channel_id=1, source_target_pairs={{0,2},{1,3},{2,0},{3,1},{4,6},{5,7},{6,4},{7,5},{8,10},{9,11},{10,... | collective-permute-start | bytes 417800 | tf_op jit(solution)/shard_map/ppermute | solution.py:275
  87.8 1.4 %collective-permute-start.12 = (bf16[272,256]{1,0:T(8,128)(2,1)S(1)}, bf16[272,256]{1,0:T(8,128)(2,1)S(1)}, u32[]{:S(2)}, u32[]{:S(2)}) collective-permute-start(bf16[272,256]{1,0:T(8,128)(2,1)S(1)} %add_convert_fusion.refs_0_), channel_id=1, source_target_pairs={{0,3},{1,2},{2,1},{3,0},{4,7},{5,6},{6,5},{7,4},{8,11},{9,10},{10,... | collective-permute-start | bytes 417800 | tf_op jit(solution)/shard_map/ppermute | solution.py:275
  89.2 0.7 copy-done.15
  90.0 0.2 copy-done.16
  90.2 5.6 %pass2.3.refs_12_ = bf16[2048,256]{1,0:T(8,128)(2,1)} custom-call(bf16[2048,256]{1,0:T(8,128)(2,1)} %get-tuple-element.33.c_ref, bf16[1024,256]{1,0:T(8,128)(2,1)} %refs_0_.5, bf16[1024,256]{1,0:T(8,128)(2,1)} %copy-done.15, bf16[1024,256]{1,0:T(8,128)(2,1)} %copy-done.14, bf16[1024,256]{1,0:T(8,128)(2,1)} %copy-done.16, ...), custom_call_target="tpu_custom_call" | custom-call | flops 2147483648 | bytes 2097152 | tf_op jit(solution)/shard_map/pass2/pallas_call | solution.py:258
  95.8 5.6 %pass2.4.refs_12_ = bf16[2048,256]{1,0:T(8,128)(2,1)} custom-call(bf16[2048,256]{1,0:T(8,128)(2,1)} %get-tuple-element.33.c_ref, bf16[1024,256]{1,0:T(8,128)(2,1)} %refs_0_.5, bf16[1024,256]{1,0:T(8,128)(2,1)} %copy-done.15, bf16[1024,256]{1,0:T(8,128)(2,1)} %copy-done.14, bf16[1024,256]{1,0:T(8,128)(2,1)} %copy-done.16, ...), custom_call_target="tpu_custom_call", output_to_operand_aliasing={{}: (13, {})} | custom-call | flops 2147483648 | bytes 2097152 | tf_op jit(solution)/shard_map/pass2/pallas_call | solution.py:258
  101.4 8.8 %pass2.5 = bf16[2048,256]{1,0:T(8,128)(2,1)} custom-call(bf16[2048,256]{1,0:T(8,128)(2,1)} %get-tuple-element.33.c_ref, bf16[1024,256]{1,0:T(8,128)(2,1)} %refs_0_.5, bf16[1024,256]{1,0:T(8,128)(2,1)} %copy-done.15, bf16[1024,256]{1,0:T(8,128)(2,1)} %copy-done.14, bf16[1024,256]{1,0:T(8,128)(2,1)} %copy-done.16, ...), custom_call_target="tpu_custom_call", output_to_operand_aliasing={{}: (13, {})} | custom-call | flops 4294967296 | bytes 2097152 | tf_op jit(solution)/shard_map/pass2/pallas_call | solution.py:258
  110.2 0.6 copy-done.7
  110.9 0.7 copy-done.9
  111.5 1.9 %finish.1 = (bf16[1024,256]{1,0:T(8,128)(2,1)}, f32[8,128]{1,0:T(8,128)}) custom-call(f32[8,128]{1,0:T(8,128)} %get-tuple-element.29.lse_ref.refs_4_, bf16[272,256]{1,0:T(8,128)(2,1)} %copy-done.1, bf16[272,256]{1,0:T(8,128)(2,1)} %copy-done.7, bf16[272,256]{1,0:T(8,128)(2,1)} %copy-done.8, bf16[272,256]{1,0:T(8,128)(2,1)} %copy-done.9), custom_call_target="tpu_custom_call" | custom-call | tf_op jit(solution)/shard_map/finish/pallas_call | solution.py:219
  (59 shorter events, 0.8 us)
Async XLA Ops:
  0.6 28.5 %copy-start.2 = (bf16[1024,256]{1,0:T(8,128)(2,1)S(1)}, bf16[1024,256]{1,0:T(8,128)(2,1)}, u32[]{:S(2)}) copy-start(bf16[1024,256]{1,0:T(8,128)(2,1)} %refs_0_.5) | copy-start | bytes 1572868
  17.9 30.5 %copy-start.17 = (bf16[256,256]{1,0:T(8,128)(2,1)S(1)}, bf16[256,256]{1,0:T(8,128)(2,1)}, u32[]{:S(2)}) copy-start(bf16[256,256]{1,0:T(8,128)(2,1)} %get-tuple-element.24) | copy-start | bytes 393220
  17.9 47.5 %copy-start.3 = (bf16[1024,256]{1,0:T(8,128)(2,1)S(1)}, bf16[1024,256]{1,0:T(8,128)(2,1)}, u32[]{:S(2)}) copy-start(bf16[1024,256]{1,0:T(8,128)(2,1)} %refs_0_.5) | copy-start | bytes 1572868
  17.9 59.4 %copy-start.13 = (s32[1024]{0:T(1024)S(1)}, s32[1024]{0:T(1024)}, u32[]{:S(2)}) copy-start(s32[1024]{0:T(1024)} %pos_ref.1) | copy-start | bytes 12292
  17.9 39.3 %all-to-all-start = ((f32[128,8,128]{2,1,0:T(8,128)}), f32[128,8,128]{2,1,0:T(8,128)S(1)}, u32[]{:S(2)}, u32[]{:S(2)}) async-start(f32[128,8,128]{2,1,0:T(8,128)} %get-tuple-element.20), calls=%async_computation | async-start | bytes 1048576 | tf_op jit(solution)/shard_map/all_to_all | solution.py:286
  29.1 36.3 %collective-permute-start.14 = (bf16[1024,256]{1,0:T(8,128)(2,1)S(1)}, bf16[1024,256]{1,0:T(8,128)(2,1)S(1)}, u32[]{:S(2)}, u32[]{:S(2)}) collective-permute-start(bf16[1024,256]{1,0:T(8,128)(2,1)S(1)} %copy-done.2), channel_id=1, source_target_pairs={{0,64},{32,96},{64,0},{96,32},{1,65},{33,97},{65,1},{97,33},{2,66}... | collective-permute-start | bytes 1572872 | tf_op jit(solution)/shard_map/ppermute | solution.py:275
  30.1 15.7 %collective-permute-start = (bf16[256,256]{1,0:T(8,128)(2,1)}, bf16[256,256]{1,0:T(8,128)(2,1)S(1)}, u32[]{:S(2)}, u32[]{:S(2)}) collective-permute-start(bf16[256,256]{1,0:T(8,128)(2,1)} %get-tuple-element.22), channel_id=1, source_target_pairs={{0,1},{1,0},{2,3},{3,2},{4,5},{5,4},{6,7},{7,6},{8,9},{9,8},{10,11... | collective-permute-start | bytes 393224 | tf_op jit(solution)/shard_map/ppermute | solution.py:275
  31.6 16.8 %collective-permute-start.1 = (bf16[256,256]{1,0:T(8,128)(2,1)}, bf16[256,256]{1,0:T(8,128)(2,1)S(1)}, u32[]{:S(2)}, u32[]{:S(2)}) collective-permute-start(bf16[256,256]{1,0:T(8,128)(2,1)} %get-tuple-element.23), channel_id=1, source_target_pairs={{0,2},{1,3},{2,0},{3,1},{4,6},{5,7},{6,4},{7,5},{8,10},{9,11},{10,... | collective-permute-start | bytes 393224 | tf_op jit(solution)/shard_map/ppermute | solution.py:275
  43.7 13.5 %collective-permute-start.3 = (bf16[272,256]{1,0:T(8,128)(2,1)}, bf16[272,256]{1,0:T(8,128)(2,1)S(1)}, u32[]{:S(2)}, u32[]{:S(2)}) collective-permute-start(bf16[272,256]{1,0:T(8,128)(2,1)} %get-tuple-element.26), channel_id=1, source_target_pairs={{0,1},{1,0},{2,3},{3,2},{4,5},{5,4},{6,7},{7,6},{8,9},{9,8},{10,11... | collective-permute-start | bytes 417800 | tf_op jit(solution)/shard_map/ppermute | solution.py:275
  43.9 13.3 %collective-permute-start.4 = (bf16[272,256]{1,0:T(8,128)(2,1)}, bf16[272,256]{1,0:T(8,128)(2,1)S(1)}, u32[]{:S(2)}, u32[]{:S(2)}) collective-permute-start(bf16[272,256]{1,0:T(8,128)(2,1)} %get-tuple-element.27), channel_id=1, source_target_pairs={{0,2},{1,3},{2,0},{3,1},{4,6},{5,7},{6,4},{7,5},{8,10},{9,11},{10,... | collective-permute-start | bytes 417800 | tf_op jit(solution)/shard_map/ppermute | solution.py:275
  45.8 11.4 %copy-start.10 = (bf16[256,256]{1,0:T(8,128)(2,1)}, bf16[256,256]{1,0:T(8,128)(2,1)S(1)}, u32[]{:S(2)}) copy-start(bf16[256,256]{1,0:T(8,128)(2,1)S(1)} %collective-permute-done.refs_1_) | copy-start | bytes 393220
  45.8 11.4 %collective-permute-start.5 = (bf16[272,256]{1,0:T(8,128)(2,1)}, bf16[272,256]{1,0:T(8,128)(2,1)S(1)}, u32[]{:S(2)}, u32[]{:S(2)}) collective-permute-start(bf16[272,256]{1,0:T(8,128)(2,1)} %get-tuple-element.28), channel_id=1, source_target_pairs={{0,3},{1,2},{2,1},{3,0},{4,7},{5,6},{6,5},{7,4},{8,11},{9,10},{10,... | collective-permute-start | bytes 417800 | tf_op jit(solution)/shard_map/ppermute | solution.py:275
  48.4 8.9 %copy-start.11 = (bf16[256,256]{1,0:T(8,128)(2,1)}, bf16[256,256]{1,0:T(8,128)(2,1)S(1)}, u32[]{:S(2)}) copy-start(bf16[256,256]{1,0:T(8,128)(2,1)S(1)} %collective-permute-done.1.refs_2_) | copy-start | bytes 393220
  48.4 8.8 %collective-permute-start.2 = (bf16[256,256]{1,0:T(8,128)(2,1)S(1)}, bf16[256,256]{1,0:T(8,128)(2,1)S(1)}, u32[]{:S(2)}, u32[]{:S(2)}) collective-permute-start(bf16[256,256]{1,0:T(8,128)(2,1)S(1)} %copy-done.17), channel_id=1, source_target_pairs={{0,3},{1,2},{2,1},{3,0},{4,7},{5,6},{6,5},{7,4},{8,11},{9,10},{10,... | collective-permute-start | bytes 393224 | tf_op jit(solution)/shard_map/ppermute | solution.py:275
  60.7 6.7 %collective-permute-start.6 = (bf16[272,256]{1,0:T(8,128)(2,1)}, bf16[272,256]{1,0:T(8,128)(2,1)S(1)}, u32[]{:S(2)}, u32[]{:S(2)}) collective-permute-start(bf16[272,256]{1,0:T(8,128)(2,1)} %get-tuple-element.30), channel_id=1, source_target_pairs={{0,8},{8,0},{16,24},{24,16},{1,9},{9,1},{17,25},{25,17},{2,10},{10... | collective-permute-start | bytes 417800 | tf_op jit(solution)/shard_map/ppermute | solution.py:275
  61.9 9.1 %collective-permute-start.7 = (bf16[272,256]{1,0:T(8,128)(2,1)}, bf16[272,256]{1,0:T(8,128)(2,1)S(1)}, u32[]{:S(2)}, u32[]{:S(2)}) collective-permute-start(bf16[272,256]{1,0:T(8,128)(2,1)} %get-tuple-element.30), channel_id=1, source_target_pairs={{0,16},{8,24},{16,0},{24,8},{1,17},{9,25},{17,1},{25,9},{2,18},{10... | collective-permute-start | bytes 417800 | tf_op jit(solution)/shard_map/ppermute | solution.py:275
  65.1 7.7 %collective-permute-start.8 = (bf16[272,256]{1,0:T(8,128)(2,1)}, bf16[272,256]{1,0:T(8,128)(2,1)S(1)}, u32[]{:S(2)}, u32[]{:S(2)}) collective-permute-start(bf16[272,256]{1,0:T(8,128)(2,1)} %get-tuple-element.30), channel_id=1, source_target_pairs={{0,24},{8,16},{16,8},{24,0},{1,25},{9,17},{17,9},{25,1},{2,26},{10... | collective-permute-start | bytes 417800 | tf_op jit(solution)/shard_map/ppermute | solution.py:275
  65.4 23.8 %collective-permute-start.13 = (bf16[1024,256]{1,0:T(8,128)(2,1)S(1)}, bf16[1024,256]{1,0:T(8,128)(2,1)S(1)}, u32[]{:S(2)}, u32[]{:S(2)}) collective-permute-start(bf16[1024,256]{1,0:T(8,128)(2,1)S(1)} %copy-done.3), channel_id=1, source_target_pairs={{0,32},{32,0},{64,96},{96,64},{1,33},{33,1},{65,97},{97,65},{2,34}... | collective-permute-start | bytes 1572872 | tf_op jit(solution)/shard_map/ppermute | solution.py:275
  65.4 23.8 %copy-start.14 = (bf16[1024,256]{1,0:T(8,128)(2,1)}, bf16[1024,256]{1,0:T(8,128)(2,1)S(1)}, u32[]{:S(2)}) copy-start(bf16[1024,256]{1,0:T(8,128)(2,1)S(1)} %collective-permute-done.14.refs_2_) | copy-start | bytes 1572868
  65.4 23.8 %collective-permute-start.15 = (bf16[1024,256]{1,0:T(8,128)(2,1)S(1)}, bf16[1024,256]{1,0:T(8,128)(2,1)S(1)}, u32[]{:S(2)}, u32[]{:S(2)}) collective-permute-start(bf16[1024,256]{1,0:T(8,128)(2,1)S(1)} %collective-permute-done.14.refs_2_), channel_id=1, source_target_pairs={{0,32},{32,0},{64,96},{96,64},{1,33},{33,1},{65,97},{97,65},{2,34}... | collective-permute-start | bytes 1572872 | tf_op jit(solution)/shard_map/ppermute | solution.py:275
  73.7 9.5 %collective-permute-start.9 = (f32[272,256]{1,0:T(8,128)S(1)}, f32[272,256]{1,0:T(8,128)S(1)}, u32[]{:S(2)}, u32[]{:S(2)}) collective-permute-start(f32[272,256]{1,0:T(8,128)S(1)} %add_add_fusion), channel_id=1, source_target_pairs={{0,4},{4,0},{1,5},{5,1},{2,6},{6,2},{3,7},{7,3},{8,12},{12,8},{9,1... | collective-permute-start | bytes 835592 | tf_op jit(solution)/shard_map/ppermute | solution.py:275
  77.3 6.0 %collective-permute-start.16 = (s32[8,128]{1,0:T(8,128)S(1)}, s32[8,128]{1,0:T(8,128)S(1)}, u32[]{:S(2)}, u32[]{:S(2)}) collective-permute-start(s32[8,128]{1,0:T(8,128)S(1)} %bitcast.5), channel_id=1, source_target_pairs={{0,32},{32,0},{64,96},{96,64},{1,33},{33,1},{65,97},{97,65},{2,34}... | collective-permute-start | bytes 12296 | tf_op jit(solution)/shard_map/ppermute | solution.py:275
  77.3 6.1 %collective-permute-start.17 = (s32[8,128]{1,0:T(8,128)S(1)}, s32[8,128]{1,0:T(8,128)S(1)}, u32[]{:S(2)}, u32[]{:S(2)}) collective-permute-start(s32[8,128]{1,0:T(8,128)S(1)} %bitcast.6), channel_id=1, source_target_pairs={{0,64},{32,96},{64,0},{96,32},{1,65},{33,97},{65,1},{97,33},{2,66}... | collective-permute-start | bytes 12296 | tf_op jit(solution)/shard_map/ppermute | solution.py:275
  83.2 4.6 %collective-permute-start.18 = (s32[8,128]{1,0:T(8,128)S(1)}, s32[8,128]{1,0:T(8,128)S(1)}, u32[]{:S(2)}, u32[]{:S(2)}) collective-permute-start(s32[8,128]{1,0:T(8,128)S(1)} %bitcast.7), channel_id=1, source_target_pairs={{0,96},{32,64},{64,32},{96,0},{1,97},{33,65},{65,33},{97,1},{2,98}... | collective-permute-start | bytes 12296 | tf_op jit(solution)/shard_map/ppermute | solution.py:275
  83.3 18.1 %copy-start.1 = (bf16[272,256]{1,0:T(8,128)(2,1)}, bf16[272,256]{1,0:T(8,128)(2,1)S(1)}, u32[]{:S(2)}) copy-start(bf16[272,256]{1,0:T(8,128)(2,1)S(1)} %add_convert_fusion.refs_0_) | copy-start | bytes 417796
  83.3 5.9 %copy-start.18 = (s32[8,128]{1,0:T(8,128)}, s32[8,128]{1,0:T(8,128)S(1)}, u32[]{:S(2)}) copy-start(s32[8,128]{1,0:T(8,128)S(1)} %collective-permute-done.16.refs_9_) | copy-start | bytes 12292
  83.3 26.9 %collective-permute-start.10 = (bf16[272,256]{1,0:T(8,128)(2,1)S(1)}, bf16[272,256]{1,0:T(8,128)(2,1)S(1)}, u32[]{:S(2)}, u32[]{:S(2)}) collective-permute-start(bf16[272,256]{1,0:T(8,128)(2,1)S(1)} %add_convert_fusion.refs_0_), channel_id=1, source_target_pairs={{0,1},{1,0},{2,3},{3,2},{4,5},{5,4},{6,7},{7,6},{8,9},{9,8},{10,11... | collective-permute-start | bytes 417800 | tf_op jit(solution)/shard_map/ppermute | solution.py:275
  83.4 5.8 %copy-start.19 = (s32[8,128]{1,0:T(8,128)}, s32[8,128]{1,0:T(8,128)S(1)}, u32[]{:S(2)}) copy-start(s32[8,128]{1,0:T(8,128)S(1)} %collective-permute-done.17.refs_10_) | copy-start | bytes 12292
  83.4 26.7 %collective-permute-start.11 = (bf16[272,256]{1,0:T(8,128)(2,1)S(1)}, bf16[272,256]{1,0:T(8,128)(2,1)S(1)}, u32[]{:S(2)}, u32[]{:S(2)}) collective-permute-start(bf16[272,256]{1,0:T(8,128)(2,1)S(1)} %add_convert_fusion.refs_0_), channel_id=1, source_target_pairs={{0,2},{1,3},{2,0},{3,1},{4,6},{5,7},{6,4},{7,5},{8,10},{9,11},{10,... | collective-permute-start | bytes 417800 | tf_op jit(solution)/shard_map/ppermute | solution.py:275
  87.8 1.5 %copy-start.20 = (s32[8,128]{1,0:T(8,128)}, s32[8,128]{1,0:T(8,128)S(1)}, u32[]{:S(2)}) copy-start(s32[8,128]{1,0:T(8,128)S(1)} %collective-permute-done.18.refs_11_) | copy-start | bytes 12292
  87.8 22.4 %collective-permute-start.12 = (bf16[272,256]{1,0:T(8,128)(2,1)S(1)}, bf16[272,256]{1,0:T(8,128)(2,1)S(1)}, u32[]{:S(2)}, u32[]{:S(2)}) collective-permute-start(bf16[272,256]{1,0:T(8,128)(2,1)S(1)} %add_convert_fusion.refs_0_), channel_id=1, source_target_pairs={{0,3},{1,2},{2,1},{3,0},{4,7},{5,6},{6,5},{7,4},{8,11},{9,10},{10,... | collective-permute-start | bytes 417800 | tf_op jit(solution)/shard_map/ppermute | solution.py:275
  89.2 1.0 copy-start.16
  (9 other events, 6.6 us)

commit v4 on v3

--- a/solution.py
+++ b/solution.py
@@ -17,14 +17,24 @@
 VMEM = pl.BlockSpec(memory_space=pltpu.VMEM)
 SMEM = pl.BlockSpec(memory_space=pltpu.SMEM)
 ANY = pl.BlockSpec(memory_space=pl.ANY)
+HBM = pl.BlockSpec(memory_space=pltpu.HBM)
 f32 = jnp.float32
 bf16 = jnp.bfloat16
+MIB = 1 << 20
 
 
 def exp_of(x):
     return jnp.exp2(x * SCALE)
 
 
+def near(xs):
+    return [pltpu.with_memory_space_constraint(x, pltpu.VMEM) for x in xs]
+
+
+def far(x):
+    return pltpu.with_memory_space_constraint(x, pltpu.HBM)
+
+
 def struct(*shape, dtype=f32):
     return jax.ShapeDtypeStruct(shape, dtype)
 
@@ -37,7 +47,7 @@
     return jnp.broadcast_to(row, (128, 128)).T
 
 
-def pass1_kernel(tile, rb, u_ref, cat_ref, *refs):
+def pass1_kernel(tile, rb, u_ref, pos_ref, cat_ref, *refs):
     out_refs, every_ref, (c_ref, acc_ref, m_ref, l_ref, st_ref, sem) = refs[:4], refs[4], refs[5:]
     rows = u_ref.shape[0]
     count, width = cat_ref.shape
@@ -76,6 +86,7 @@
         total = jnp.sum(l_ref[sl], axis=1, keepdims=True)
         acc_ref[sl] = acc_ref[sl] * (1.0 / total)
         st_ref[b : b + 1] = m_ref[sl].T[0:1] + sharpness_divisor * jnp.log(as_row(total))
+    st_ref[rows // 128 :] = pos_ref[...].astype(f32)
     every_ref[...] = jnp.broadcast_to(st_ref[...][None], every_ref.shape)
     x = lax.axis_index("x")
     chunk = rows // 4
@@ -84,55 +95,61 @@
         out_ref[...] = acc_ref[part, :].astype(bf16)
 
 
-def pass1(users, catalog, tile=2048, rb=256):
+def pass1(users, pos, catalog, tile=2048, rb=256):
     rows, width = users.shape
     count = catalog.shape[0]
     return pl.pallas_call(
         functools.partial(pass1_kernel, tile, rb),
-        in_specs=[VMEM, ANY],
+        in_specs=[VMEM, VMEM, HBM],
         out_specs=[VMEM] * 5,
-        out_shape=[struct(rows // 4, width, dtype=bf16)] * 4 + [struct(128, rows // 128, 128)],
+        out_shape=[struct(rows // 4, width, dtype=bf16)] * 4 + [struct(128, rows // 64, 128)],
         scratch_shapes=[
             pltpu.VMEM((count, width), bf16),
             pltpu.VMEM((rows, width), f32),
             pltpu.VMEM((rows, 128), f32),
             pltpu.VMEM((rows, 128), f32),
-            pltpu.VMEM((rows // 128, 128), f32),
+            pltpu.VMEM((rows // 64, 128), f32),
             pltpu.SemaphoreType.DMA((count // tile,)),
         ],
         cost_estimate=pl.CostEstimate(
             flops=4 * rows * count * width, bytes_accessed=2 * count * width, transcendentals=rows * count
         ),
+        compiler_params=pltpu.CompilerParams(vmem_limit_bytes=20 * MIB),
         name="pass1",
-    )(users, catalog)
-
-
-def hits_kernel(pos_ref, u_ref, c_ref, *refs):
-    out_refs, own_ref, hit_ref, sp_ref = refs[:4], refs[4], refs[5], refs[6]
+    )(users, pos, far(catalog))
+
+
+def hits_kernel(pos_ref, u_ref, cat_ref, *refs):
+    out_refs, own_ref, (hit_ref, sp_ref, c_ref, found_ref, sem) = refs[:4], refs[4], refs[5:]
     rows, width = u_ref.shape
-    count = c_ref.shape[0]
+    count = cat_ref.shape[0]
     items = own_ref.shape[0]
     x, member, shard = lax.axis_index("x"), lax.axis_index(USER), lax.axis_index(ITEM)
-    own_ref[...] = c_ref[pl.ds(pl.multiple_of(member * items, items), items), :]
+    mine = pl.ds(pl.multiple_of(member * items, items), items)
+    whole_copy = pltpu.make_async_copy(cat_ref, c_ref, sem.at[0])
+    own_copy = pltpu.make_async_copy(cat_ref.at[mine], own_ref, sem.at[1])
+    whole_copy.start()
+    own_copy.start()
     hit_ref[...] = jnp.zeros_like(hit_ref)
     base = shard * count
-
-    @pl.loop(0, rows // 8)
-    def _(g):
-        here = [pos_ref[g * 8 + j] - base for j in range(8)]
-        mine = [(h >= 0) & (h < count) for h in here]
-
-        @pl.when(functools.reduce(jnp.logical_or, mine))
-        def _():
-            for j in range(8):
-
-                @pl.when(mine[j])
-                def _():
-                    start = pl.multiple_of((here[j] >> 4) << 4, 16)
-                    group = c_ref[pl.ds(start, 16), :].astype(f32)
-                    inside = lax.broadcasted_iota(jnp.int32, group.shape, 0) == (here[j] & 15)
-                    row = jnp.sum(jnp.where(inside, group, 0.0), axis=0, keepdims=True)
-                    hit_ref[pl.ds(g * 8 + j, 1), :] = row
+    bits = count.bit_length() - 1
+
+    def scan(g, n):
+        for j in range(16):
+            found_ref[n] = g * 16 + j
+            n = n + ((pos_ref[g * 16 + j] >> bits) == shard).astype(jnp.int32)
+        return n
+
+    n_found = lax.fori_loop(0, rows // 16, scan, jnp.int32(0))
+    whole_copy.wait()
+
+    @pl.loop(0, n_found)
+    def _(i):
+        user = found_ref[i]
+        here = pos_ref[user] - base
+        group = c_ref[pl.ds(pl.multiple_of((here >> 4) << 4, 16), 16), :].astype(f32)
+        inside = lax.broadcasted_iota(jnp.int32, group.shape, 0) == (here & 15)
+        hit_ref[pl.ds(user, 1), :] = jnp.sum(jnp.where(inside, group, 0.0), axis=0, keepdims=True)
 
     for b in range(rows // 128):
         sl = slice(b * 128, (b + 1) * 128)
@@ -150,6 +167,7 @@
             terms.append(term)
         terms.append(jnp.zeros((13, width), f32))
         out_ref[chunk:] = jnp.concatenate(terms, axis=0).astype(bf16)
+    own_copy.wait()
 
 
 def find_hits(positives, users, catalog):
@@ -157,15 +175,22 @@
     count = catalog.shape[0]
     return pl.pallas_call(
         hits_kernel,
-        in_specs=[SMEM, VMEM, VMEM],
+        in_specs=[SMEM, VMEM, HBM],
         out_specs=[VMEM] * 5,
         out_shape=[struct(rows // 4 + 16, width, dtype=bf16)] * 4 + [struct(count // 4, width, dtype=bf16)],
-        scratch_shapes=[pltpu.VMEM((rows, width), f32), pltpu.VMEM((rows // 128, 128), f32)],
+        scratch_shapes=[
+            pltpu.VMEM((rows, width), f32),
+            pltpu.VMEM((rows // 128, 128), f32),
+            pltpu.VMEM((count, width), bf16),
+            pltpu.SMEM((rows,), jnp.int32),
+            pltpu.SemaphoreType.DMA((2,)),
+        ],
         cost_estimate=pl.CostEstimate(
             flops=rows * count * width // 2, bytes_accessed=2 * count * width, transcendentals=0
         ),
+        compiler_params=pltpu.CompilerParams(vmem_limit_bytes=12 * MIB),
         name="hits",
-    )(positives, users, catalog)
+    )(positives, users, far(catalog))
 
 
 def combine_kernel(all_ref, *refs):
@@ -173,10 +198,13 @@
     x, member, shard = lax.axis_index("x"), lax.axis_index(USER), lax.axis_index(ITEM)
     shards = all_ref.shape[0] // 4
     chunk, width = u_refs[0].shape
+    half = all_ref.shape[1] // 2
     for k, l_ref in enumerate(l_refs):
-        stats = all_ref[pl.ds((member ^ k) * shards, shards)]
+        first = (member ^ k) * shards
+        stats = all_ref[pl.ds(first, shards), 0:half]
         top = jnp.max(stats, axis=0)
-        l_ref[...] = top + sharpness_divisor * jnp.log(jnp.sum(exp_of(stats - top[None]), axis=0))
+        l_ref[0:half] = top + sharpness_divisor * jnp.log(jnp.sum(exp_of(stats - top[None]), axis=0))
+        l_ref[half:] = all_ref[first, half:]
     for h in range(chunk // 128):
         sl = slice(h * 128, (h + 1) * 128)
         row = pl.ds(x * 2 + h, 1)
@@ -197,8 +225,9 @@
         in_specs=[VMEM] * 9,
         out_specs=[VMEM] * 5,
         out_shape=[struct(*every.shape[1:])] * 4 + [struct(rows, width, dtype=bf16)],
+        compiler_params=pltpu.CompilerParams(vmem_limit_bytes=8 * MIB),
         name="combine",
-    )(every, *us, *hs)
+    )(*near([every, *us, *hs]))
 
 
 def finish_kernel(lse_ref, *refs):
@@ -220,36 +249,40 @@
         finish_kernel,
         in_specs=[VMEM] * 5,
         out_specs=[VMEM] * 2,
-        out_shape=[struct(rows, width, dtype=bf16), struct(*lse4.shape)],
+        out_shape=[struct(rows, width, dtype=bf16), struct(rows // 128, 128)],
+        compiler_params=pltpu.CompilerParams(vmem_limit_bytes=6 * MIB),
         name="finish",
-    )(lse4, *parts)
+    )(*near([lse4, *parts]))
 
 
 def pass2_kernel(tile, lead, c_ref, *refs):
-    us, lses, poss, out_ref = refs[:4], refs[4:8], refs[8:12], refs[-1]
+    us, infos, out_ref = refs[:4], refs[4:8], refs[-1]
     member, shard = lax.axis_index(USER), lax.axis_index(ITEM)
     start = (lead + pl.program_id(0)) * tile
     items = c_ref.shape[0]
     c = c_ref[pl.ds(pl.multiple_of(start, tile), tile), :]
     item = lax.broadcasted_iota(jnp.int32, (tile, 128), 0) + (shard * 4 + member) * items + start
+    item = item.astype(f32)
     total = jnp.zeros((tile, c.shape[1]), f32)
-    for u_ref, l_ref, pos_ref in zip(us, lses, poss):
+    for u_ref, info_ref in zip(us, infos):
         u = u_ref[...]
+        blocks = u.shape[0] // 128
         r = lax.dot_general(c, u, NT, preferred_element_type=f32)
         ws = []
-        for j in range(u.shape[0] // 128):
-            w = exp_of(r[:, j * 128 : (j + 1) * 128] - l_ref[j : j + 1])
-            ws.append(jnp.where(pos_ref[j : j + 1] == item, w - 1.0, w).astype(bf16))
+        for j in range(blocks):
+            w = exp_of(r[:, j * 128 : (j + 1) * 128] - info_ref[j : j + 1])
+            hit = info_ref[blocks + j : blocks + j + 1] == item
+            ws.append(jnp.where(hit, w - 1.0, w).astype(bf16))
         total = total + jnp.dot(jnp.concatenate(ws, axis=1), u, preferred_element_type=f32)
     out_ref[...] = (total / sharpness_divisor).astype(out_ref.dtype)
 
 
-def pass2(own, us, lses, poss, start, stop, before, tile=512):
+def pass2(own, us, infos, start, stop, before, tile=512):
     items, width = own.shape
     rows = us[0].shape[0]
     lead = start // tile
-    in_specs = [VMEM] * 13
-    args = [own, *us, *lses, *poss]
+    in_specs = [VMEM] * 9
+    args = [own, *us, *infos]
     aliases = {}
     if before is not None:
         in_specs.append(ANY)
@@ -267,8 +300,9 @@
             bytes_accessed=8 * rows * width,
             transcendentals=4 * rows * (stop - start),
         ),
+        compiler_params=pltpu.CompilerParams(vmem_limit_bytes=14 * MIB),
         name="pass2",
-    )(*args)
+    )(*near(args[:9]), *args[9:])
 
 
 def swap(x, axis, size, k):
@@ -281,24 +315,23 @@
     pos = positives.reshape(rows // 128, 128)
     over = swap(users, USER, 4, 2)
     us = [users, swap(users, USER, 4, 1), over, swap(over, USER, 4, 1)]
-    poss = [pos] + [swap(pos, USER, 4, k) for k in (1, 2, 3)]
-    *pieces, every = pass1(users, catalog)
+    *pieces, every = pass1(users, pos, catalog)
     every = lax.all_to_all(every, USER + ITEM, 0, 0, tiled=True)
     *hits, own = find_hits(positives, users, catalog)
     pieces = [pieces[0]] + [swap(pieces[k], "x", 4, k) for k in (1, 2, 3)]
     hits = [hits[0]] + [swap(hits[k], "x", 4, k) for k in (1, 2, 3)]
-    *lses, value = combine(every, pieces, hits)
+    *infos, value = combine(every, pieces, hits)
 
     a = [value] + [swap(value, "z", 4, k) for k in (1, 2, 3)]
-    item_grad = pass2(own, us, lses, poss, 0, SPLIT[0], None)
+    item_grad = pass2(own, us, infos, 0, SPLIT[0], None)
     a = [v.astype(f32) for v in a]
     value = (a[0] + a[1]) + (a[2] + a[3])
     other = swap(value, "y_hi", 2, 1)
-    item_grad = pass2(own, us, lses, poss, SPLIT[0], SPLIT[1], item_grad)
+    item_grad = pass2(own, us, infos, SPLIT[0], SPLIT[1], item_grad)
     value = (value + other).astype(bf16)
     got = [value] + [swap(value, "x", 4, k) for k in (1, 2, 3)]
-    item_grad = pass2(own, us, lses, poss, SPLIT[1], items, item_grad)
-    user_grad, loss = finish(lses[0], got, rows)
+    item_grad = pass2(own, us, infos, SPLIT[1], items, item_grad)
+    user_grad, loss = finish(infos[0], got, rows)
     return loss.reshape(rows), user_grad, item_grad
 
 

time: 114 us -> 103 us (0.904)
  Pallas kernels: 51.1 us -> 39.5 us
  waiting for transfers between devices: 20.8 us -> 24.2 us
  starting transfers between devices: 36.4 us -> 34 us
    pallas_call x1, Pallas kernels: 9.41 us -> 4.23 us  [find_hits(): pl.pallas_call(hits_kernel, in_specs=[SMEM, VMEM, HBM], out_specs=[VMEM]...]
    ppermute x19 -> x16, waiting for transfers between devices: 20.8 us -> 24.2 us  [swap(): return lax.ppermute(x, axis, [(i, i ^ k) for i in range(size)])]
    ppermute x19 -> x16, starting transfers between devices: 25.3 us -> 22.8 us  [swap(): return lax.ppermute(x, axis, [(i, i ^ k) for i in range(size)])]
    pallas_call x1, Pallas kernels: 2.51 us -> 0.37 us  [combine(): pl.pallas_call(combine_kernel, in_specs=[VMEM] * 9, out_specs=[VMEM] * 5,...]
    pallas_call x3, Pallas kernels: 20 us -> 17.9 us  [pass2(): pl.pallas_call(functools.partial(pass2_kernel, tile, lead), grid=((stop -...]
    unnamed x42 -> x12, local copies, waits for them, and re-layouts: 3.22 us -> 3.96 us
  transfers between devices with their start and end apart: 20 -> 17, of which waited for: 5 -> 8; matrix products, arithmetic and copies ran while one was open for 1% -> 0% of each run, Pallas kernels for 28% -> 22%
where the time goes in v4:
time: 103 us; the launch traced here: 102 us
  Pallas kernels  39.5 us (38%)
  starting transfers between devices  34 us (33%)
  waiting for transfers between devices  24.2 us (23%)
  local copies, waits for them, and re-layouts  3.96 us (4%)
    ppermute x16, waiting for transfers between devices, swap(): return lax.ppermute(x, axis, [(i, i ^ k) for i in range(size)])  24.2 us
    ppermute x16, starting transfers between devices, swap(): return lax.ppermute(x, axis, [(i, i ^ k) for i in range(size)])  22.8 us
    pallas_call x3, Pallas kernels, pass2(): pl.pallas_call(functools.partial(pass2_kernel, tile, lead), grid=((stop -...  17.9 us
    pallas_call x1, Pallas kernels, pass1(): pl.pallas_call(functools.partial(pass1_kernel, tile, rb), in_specs=[VMEM,...  16.2 us
    all_to_all x1, starting transfers between devices, per_device(): every = lax.all_to_all(every, USER + ITEM, 0, 0, tiled=True)  11.2 us
    pallas_call x1, Pallas kernels, find_hits(): pl.pallas_call(hits_kernel, in_specs=[SMEM, VMEM, HBM], out_specs=[VMEM]...  4.23 us
    unnamed x12, local copies, waits for them, and re-layouts  3.96 us
  transfers between devices with their start and end apart: 17, of which 8 were waited for; matrix products, arithmetic and copies ran while one was open for 0% of the time, Pallas kernels for 22%

profile of v4, /device:TPU:0, one launch (start us, length us, event | category | flops | bytes accessed | tf_op | source)
XLA Modules:
  0.0 102.4 jit_solution(13514126599125141080)
XLA Ops:
  0.6 1.0 %copy-done = bf16[1024,256]{1,0:T(8,128)(2,1)S(1)} copy-done((bf16[1024,256]{1,0:T(8,128)(2,1)S(1)}, bf16[1024,256]{1,0:T(8,128)(2,1)}, u32[]{:S(2)}) %copy-start) | copy-done | bytes 524312
  1.7 0.7 copy-done.2
  2.4 16.2 %pass1.1 = (bf16[256,256]{1,0:T(8,128)(2,1)S(1)}, bf16[256,256]{1,0:T(8,128)(2,1)S(1)}, bf16[256,256]{1,0:T(8,128)(2,1)S(1)}, bf16[256,256]{1,0:T(8,128)(2,1)S(1)}, f32[128,16,128]{2,1,0:T(8,128)}) custom-call(bf16[1024,256]{1,0:T(8,128)(2,1)S(1)} %copy-done, s32[8,128]{1,0:T(8,128)S(1)} %bitcast.2, bf16[8192,256]{1,0:T(8,128)(2,1)} %cat_ref.3), custom_call_target="tpu_custom_call" | custom-call | flops 8589934592 | bytes 4194304 | tf_op jit(solution)/shard_map/pass1/pallas_call | solution.py:101
  18.5 11.2 %all-to-all-start = ((f32[128,16,128]{2,1,0:T(8,128)}), f32[128,16,128]{2,1,0:T(8,128)S(1)}, u32[]{:S(2)}, u32[]{:S(2)}) async-start(f32[128,16,128]{2,1,0:T(8,128)} %get-tuple-element.20), calls=%async_computation | async-start | bytes 2097152 | tf_op jit(solution)/shard_map/all_to_all | solution.py:319
  29.7 1.0 %collective-permute-start.14 = (bf16[1024,256]{1,0:T(8,128)(2,1)S(1)}, bf16[1024,256]{1,0:T(8,128)(2,1)S(1)}, u32[]{:S(2)}, u32[]{:S(2)}) collective-permute-start(bf16[1024,256]{1,0:T(8,128)(2,1)S(1)} %copy-done.1), channel_id=1, source_target_pairs={{0,64},{32,96},{64,0},{96,32},{1,65},{33,97},{65,1},{97,33},{2,66}... | collective-permute-start | bytes 1572872 | tf_op jit(solution)/shard_map/ppermute | solution.py:309
  30.8 1.5 %collective-permute-start = (bf16[256,256]{1,0:T(8,128)(2,1)S(1)}, bf16[256,256]{1,0:T(8,128)(2,1)S(1)}, u32[]{:S(2)}, u32[]{:S(2)}) collective-permute-start(bf16[256,256]{1,0:T(8,128)(2,1)S(1)} %get-tuple-element.22), channel_id=1, source_target_pairs={{0,1},{1,0},{2,3},{3,2},{4,5},{5,4},{6,7},{7,6},{8,9},{9,8},{10,11... | collective-permute-start | bytes 393224 | tf_op jit(solution)/shard_map/ppermute | solution.py:309
  32.2 2.7 %collective-permute-start.1 = (bf16[256,256]{1,0:T(8,128)(2,1)S(1)}, bf16[256,256]{1,0:T(8,128)(2,1)S(1)}, u32[]{:S(2)}, u32[]{:S(2)}) collective-permute-start(bf16[256,256]{1,0:T(8,128)(2,1)S(1)} %get-tuple-element.23), channel_id=1, source_target_pairs={{0,2},{1,3},{2,0},{3,1},{4,6},{5,7},{6,4},{7,5},{8,10},{9,11},{10,... | collective-permute-start | bytes 393224 | tf_op jit(solution)/shard_map/ppermute | solution.py:309
  34.9 0.6 collective-permute-start.2
  35.5 4.2 %hits.1 = (bf16[272,256]{1,0:T(8,128)(2,1)S(1)}, bf16[272,256]{1,0:T(8,128)(2,1)S(1)}, bf16[272,256]{1,0:T(8,128)(2,1)S(1)}, bf16[272,256]{1,0:T(8,128)(2,1)S(1)}, bf16[2048,256]{1,0:T(8,128)(2,1)S(1)}) custom-call(s32[1024]{0:T(1024)S(1)} %copy-done.3, bf16[1024,256]{1,0:T(8,128)(2,1)S(1)} %copy-done.1, bf16[8192,256]{1,0:T(8,128)(2,1)} %cat_ref.3), custom_call_target="tpu_custom_call" | custom-call | flops 1073741824 | bytes 4194304 | tf_op jit(solution)/shard_map/hits/pallas_call | solution.py:176
  39.7 1.0 copy-done.4
  40.7 4.9 %collective-permute-done.refs_1_ = bf16[256,256]{1,0:T(8,128)(2,1)S(1)} collective-permute-done((bf16[256,256]{1,0:T(8,128)(2,1)S(1)}, bf16[256,256]{1,0:T(8,128)(2,1)S(1)}, u32[]{:S(2)}, u32[]{:S(2)}) %collective-permute-start) | collective-permute-done | bytes 131104 | tf_op jit(solution)/shard_map/ppermute | solution.py:309
  45.6 0.9 collective-permute-start.3
  46.5 3.4 %collective-permute-done.1.refs_2_ = bf16[256,256]{1,0:T(8,128)(2,1)S(1)} collective-permute-done((bf16[256,256]{1,0:T(8,128)(2,1)S(1)}, bf16[256,256]{1,0:T(8,128)(2,1)S(1)}, u32[]{:S(2)}, u32[]{:S(2)}) %collective-permute-start.1) | collective-permute-done | bytes 131104 | tf_op jit(solution)/shard_map/ppermute | solution.py:309
  49.9 0.6 collective-permute-start.4
  50.5 2.9 %collective-permute-done.14.refs_2_ = bf16[1024,256]{1,0:T(8,128)(2,1)S(1)} collective-permute-done((bf16[1024,256]{1,0:T(8,128)(2,1)S(1)}, bf16[1024,256]{1,0:T(8,128)(2,1)S(1)}, u32[]{:S(2)}, u32[]{:S(2)}) %collective-permute-start.14) | collective-permute-done | bytes 524320 | tf_op jit(solution)/shard_map/ppermute | solution.py:309
  53.5 2.7 %collective-permute-start.5 = (bf16[272,256]{1,0:T(8,128)(2,1)S(1)}, bf16[272,256]{1,0:T(8,128)(2,1)S(1)}, u32[]{:S(2)}, u32[]{:S(2)}) collective-permute-start(bf16[272,256]{1,0:T(8,128)(2,1)S(1)} %get-tuple-element.28), channel_id=1, source_target_pairs={{0,3},{1,2},{2,1},{3,0},{4,7},{5,6},{6,5},{7,4},{8,11},{9,10},{10,... | collective-permute-start | bytes 417800 | tf_op jit(solution)/shard_map/ppermute | solution.py:309
  56.5 4.3 %collective-permute-done.5.refs_7_ = bf16[272,256]{1,0:T(8,128)(2,1)S(1)} collective-permute-done((bf16[272,256]{1,0:T(8,128)(2,1)S(1)}, bf16[272,256]{1,0:T(8,128)(2,1)S(1)}, u32[]{:S(2)}, u32[]{:S(2)}) %collective-permute-start.5) | collective-permute-done | bytes 139296 | tf_op jit(solution)/shard_map/ppermute | solution.py:309
  60.8 0.4 combine.1
  61.1 1.7 %collective-permute-start.6 = (bf16[272,256]{1,0:T(8,128)(2,1)S(1)}, bf16[272,256]{1,0:T(8,128)(2,1)S(1)}, u32[]{:S(2)}, u32[]{:S(2)}) collective-permute-start(bf16[272,256]{1,0:T(8,128)(2,1)S(1)} %get-tuple-element.30), channel_id=1, source_target_pairs={{0,8},{8,0},{16,24},{24,16},{1,9},{9,1},{17,25},{25,17},{2,10},{10... | collective-permute-start | bytes 417800 | tf_op jit(solution)/shard_map/ppermute | solution.py:309
  62.9 3.2 %collective-permute-start.7 = (bf16[272,256]{1,0:T(8,128)(2,1)S(1)}, bf16[272,256]{1,0:T(8,128)(2,1)S(1)}, u32[]{:S(2)}, u32[]{:S(2)}) collective-permute-start(bf16[272,256]{1,0:T(8,128)(2,1)S(1)} %get-tuple-element.30), channel_id=1, source_target_pairs={{0,16},{8,24},{16,0},{24,8},{1,17},{9,25},{17,1},{25,9},{2,18},{10... | collective-permute-start | bytes 417800 | tf_op jit(solution)/shard_map/ppermute | solution.py:309
  66.1 0.8 collective-permute-done.6
  66.9 5.5 %collective-permute-done.7 = bf16[272,256]{1,0:T(8,128)(2,1)S(1)} collective-permute-done((bf16[272,256]{1,0:T(8,128)(2,1)S(1)}, bf16[272,256]{1,0:T(8,128)(2,1)S(1)}, u32[]{:S(2)}, u32[]{:S(2)}) %collective-permute-start.7) | collective-permute-done | bytes 139296 | tf_op jit(solution)/shard_map/ppermute | solution.py:309
  72.4 2.1 %collective-permute-done.8 = bf16[272,256]{1,0:T(8,128)(2,1)S(1)} collective-permute-done((bf16[272,256]{1,0:T(8,128)(2,1)S(1)}, bf16[272,256]{1,0:T(8,128)(2,1)S(1)}, u32[]{:S(2)}, u32[]{:S(2)}) %collective-permute-start.8) | collective-permute-done | bytes 139296 | tf_op jit(solution)/shard_map/ppermute | solution.py:309
  74.5 3.1 %collective-permute-start.9 = (f32[272,256]{1,0:T(8,128)S(1)}, f32[272,256]{1,0:T(8,128)S(1)}, u32[]{:S(2)}, u32[]{:S(2)}) collective-permute-start(f32[272,256]{1,0:T(8,128)S(1)} %add_add_fusion), channel_id=1, source_target_pairs={{0,4},{4,0},{1,5},{5,1},{2,6},{6,2},{3,7},{7,3},{8,12},{12,8},{9,1... | collective-permute-start | bytes 835592 | tf_op jit(solution)/shard_map/ppermute | solution.py:309
  77.6 1.2 %copy-done.5 = bf16[2048,256]{1,0:T(8,128)(2,1)S(1)} copy-done((bf16[2048,256]{1,0:T(8,128)(2,1)S(1)}, bf16[2048,256]{1,0:T(8,128)(2,1)}, u32[]{:S(2)}) %copy-start.5) | copy-done | bytes 1048600
  78.9 4.9 %pass2.3.refs_8_ = bf16[2048,256]{1,0:T(8,128)(2,1)} custom-call(bf16[2048,256]{1,0:T(8,128)(2,1)S(1)} %copy-done.5, bf16[1024,256]{1,0:T(8,128)(2,1)S(1)} %copy-done.1, bf16[1024,256]{1,0:T(8,128)(2,1)} %collective-permute-done.13.refs_1_, bf16[1024,256]{1,0:T(8,128)(2,1)S(1)} %collective-permute-done.14.refs_2_, ...), custom_call_target="tpu_custom_call" | custom-call | flops 2147483648 | bytes 2097152 | tf_op jit(solution)/shard_map/pass2/pallas_call | solution.py:291
  83.8 4.9 %pass2.4.refs_8_ = bf16[2048,256]{1,0:T(8,128)(2,1)} custom-call(bf16[2048,256]{1,0:T(8,128)(2,1)S(1)} %copy-done.5, bf16[1024,256]{1,0:T(8,128)(2,1)S(1)} %copy-done.1, bf16[1024,256]{1,0:T(8,128)(2,1)} %collective-permute-done.13.refs_1_, bf16[1024,256]{1,0:T(8,128)(2,1)S(1)} %collective-permute-done.14.refs_2_, ...), custom_call_target="tpu_custom_call", output_to_operand_aliasing={{}: (9, {})} | custom-call | flops 2147483648 | bytes 2097152 | tf_op jit(solution)/shard_map/pass2/pallas_call | solution.py:291
  88.8 0.3 collective-permute-start.10
  89.1 3.9 %collective-permute-start.11 = (bf16[272,256]{1,0:T(8,128)(2,1)S(1)}, bf16[272,256]{1,0:T(8,128)(2,1)S(1)}, u32[]{:S(2)}, u32[]{:S(2)}) collective-permute-start(bf16[272,256]{1,0:T(8,128)(2,1)S(1)} %add_convert_fusion.refs_0_), channel_id=1, source_target_pairs={{0,2},{1,3},{2,0},{3,1},{4,6},{5,7},{6,4},{7,5},{8,10},{9,11},{10,... | collective-permute-start | bytes 417800 | tf_op jit(solution)/shard_map/ppermute | solution.py:309
  93.1 0.5 collective-permute-start.12
  93.6 8.0 %pass2.5 = bf16[2048,256]{1,0:T(8,128)(2,1)} custom-call(bf16[2048,256]{1,0:T(8,128)(2,1)S(1)} %copy-done.5, bf16[1024,256]{1,0:T(8,128)(2,1)S(1)} %copy-done.1, bf16[1024,256]{1,0:T(8,128)(2,1)} %collective-permute-done.13.refs_1_, bf16[1024,256]{1,0:T(8,128)(2,1)S(1)} %collective-permute-done.14.refs_2_, ...), custom_call_target="tpu_custom_call", output_to_operand_aliasing={{}: (9, {})} | custom-call | flops 4294967296 | bytes 2097152 | tf_op jit(solution)/shard_map/pass2/pallas_call | solution.py:291
  101.6 0.8 finish.1
  (23 shorter events, 0.5 us)
Async XLA Ops:
  0.6 1.0 %copy-start = (bf16[1024,256]{1,0:T(8,128)(2,1)S(1)}, bf16[1024,256]{1,0:T(8,128)(2,1)}, u32[]{:S(2)}) copy-start(bf16[1024,256]{1,0:T(8,128)(2,1)} %refs_0_.5) | copy-start | bytes 1572868
  1.7 0.7 copy-start.2
  2.4 27.4 %copy-start.1 = (bf16[1024,256]{1,0:T(8,128)(2,1)S(1)}, bf16[1024,256]{1,0:T(8,128)(2,1)}, u32[]{:S(2)}) copy-start(bf16[1024,256]{1,0:T(8,128)(2,1)} %refs_0_.5) | copy-start | bytes 1572868
  2.4 33.1 %copy-start.3 = (s32[1024]{0:T(1024)S(1)}, s32[1024]{0:T(1024)}, u32[]{:S(2)}) copy-start(s32[1024]{0:T(1024)} %pos_ref.1) | copy-start | bytes 12292
  18.5 42.2 %all-to-all-start = ((f32[128,16,128]{2,1,0:T(8,128)}), f32[128,16,128]{2,1,0:T(8,128)S(1)}, u32[]{:S(2)}, u32[]{:S(2)}) async-start(f32[128,16,128]{2,1,0:T(8,128)} %get-tuple-element.20), calls=%async_computation | async-start | bytes 2097152 | tf_op jit(solution)/shard_map/all_to_all | solution.py:319
  29.7 23.7 %collective-permute-start.14 = (bf16[1024,256]{1,0:T(8,128)(2,1)S(1)}, bf16[1024,256]{1,0:T(8,128)(2,1)S(1)}, u32[]{:S(2)}, u32[]{:S(2)}) collective-permute-start(bf16[1024,256]{1,0:T(8,128)(2,1)S(1)} %copy-done.1), channel_id=1, source_target_pairs={{0,64},{32,96},{64,0},{96,32},{1,65},{33,97},{65,1},{97,33},{2,66}... | collective-permute-start | bytes 1572872 | tf_op jit(solution)/shard_map/ppermute | solution.py:309
  30.8 14.8 %collective-permute-start = (bf16[256,256]{1,0:T(8,128)(2,1)S(1)}, bf16[256,256]{1,0:T(8,128)(2,1)S(1)}, u32[]{:S(2)}, u32[]{:S(2)}) collective-permute-start(bf16[256,256]{1,0:T(8,128)(2,1)S(1)} %get-tuple-element.22), channel_id=1, source_target_pairs={{0,1},{1,0},{2,3},{3,2},{4,5},{5,4},{6,7},{7,6},{8,9},{9,8},{10,11... | collective-permute-start | bytes 393224 | tf_op jit(solution)/shard_map/ppermute | solution.py:309
  32.2 17.7 %collective-permute-start.1 = (bf16[256,256]{1,0:T(8,128)(2,1)S(1)}, bf16[256,256]{1,0:T(8,128)(2,1)S(1)}, u32[]{:S(2)}, u32[]{:S(2)}) collective-permute-start(bf16[256,256]{1,0:T(8,128)(2,1)S(1)} %get-tuple-element.23), channel_id=1, source_target_pairs={{0,2},{1,3},{2,0},{3,1},{4,6},{5,7},{6,4},{7,5},{8,10},{9,11},{10,... | collective-permute-start | bytes 393224 | tf_op jit(solution)/shard_map/ppermute | solution.py:309
  34.9 18.6 %collective-permute-start.2 = (bf16[256,256]{1,0:T(8,128)(2,1)S(1)}, bf16[256,256]{1,0:T(8,128)(2,1)S(1)}, u32[]{:S(2)}, u32[]{:S(2)}) collective-permute-start(bf16[256,256]{1,0:T(8,128)(2,1)S(1)} %get-tuple-element.24), channel_id=1, source_target_pairs={{0,3},{1,2},{2,1},{3,0},{4,7},{5,6},{6,5},{7,4},{8,11},{9,10},{10,... | collective-permute-start | bytes 393224 | tf_op jit(solution)/shard_map/ppermute | solution.py:309
  35.5 42.2 %collective-permute-start.13 = (bf16[1024,256]{1,0:T(8,128)(2,1)S(1)}, bf16[1024,256]{1,0:T(8,128)(2,1)}, u32[]{:S(2)}, u32[]{:S(2)}) collective-permute-start(bf16[1024,256]{1,0:T(8,128)(2,1)S(1)} %copy-done.1), channel_id=1, source_target_pairs={{0,32},{32,0},{64,96},{96,64},{1,33},{33,1},{65,97},{97,65},{2,34}... | collective-permute-start | bytes 1572872 | tf_op jit(solution)/shard_map/ppermute | solution.py:309
  39.7 1.0 copy-start.4
  45.6 10.6 %collective-permute-start.3 = (bf16[272,256]{1,0:T(8,128)(2,1)S(1)}, bf16[272,256]{1,0:T(8,128)(2,1)S(1)}, u32[]{:S(2)}, u32[]{:S(2)}) collective-permute-start(bf16[272,256]{1,0:T(8,128)(2,1)S(1)} %get-tuple-element.26), channel_id=1, source_target_pairs={{0,1},{1,0},{2,3},{3,2},{4,5},{5,4},{6,7},{7,6},{8,9},{9,8},{10,11... | collective-permute-start | bytes 417800 | tf_op jit(solution)/shard_map/ppermute | solution.py:309
  49.9 6.6 %collective-permute-start.4 = (bf16[272,256]{1,0:T(8,128)(2,1)S(1)}, bf16[272,256]{1,0:T(8,128)(2,1)S(1)}, u32[]{:S(2)}, u32[]{:S(2)}) collective-permute-start(bf16[272,256]{1,0:T(8,128)(2,1)S(1)} %get-tuple-element.27), channel_id=1, source_target_pairs={{0,2},{1,3},{2,0},{3,1},{4,6},{5,7},{6,4},{7,5},{8,10},{9,11},{10,... | collective-permute-start | bytes 417800 | tf_op jit(solution)/shard_map/ppermute | solution.py:309
  53.5 24.2 %collective-permute-start.15 = (bf16[1024,256]{1,0:T(8,128)(2,1)S(1)}, bf16[1024,256]{1,0:T(8,128)(2,1)}, u32[]{:S(2)}, u32[]{:S(2)}) collective-permute-start(bf16[1024,256]{1,0:T(8,128)(2,1)S(1)} %collective-permute-done.14.refs_2_), channel_id=1, source_target_pairs={{0,32},{32,0},{64,96},{96,64},{1,33},{33,1},{65,97},{97,65},{2,34}... | collective-permute-start | bytes 1572872 | tf_op jit(solution)/shard_map/ppermute | solution.py:309
  53.5 7.3 %collective-permute-start.5 = (bf16[272,256]{1,0:T(8,128)(2,1)S(1)}, bf16[272,256]{1,0:T(8,128)(2,1)S(1)}, u32[]{:S(2)}, u32[]{:S(2)}) collective-permute-start(bf16[272,256]{1,0:T(8,128)(2,1)S(1)} %get-tuple-element.28), channel_id=1, source_target_pairs={{0,3},{1,2},{2,1},{3,0},{4,7},{5,6},{6,5},{7,4},{8,11},{9,10},{10,... | collective-permute-start | bytes 417800 | tf_op jit(solution)/shard_map/ppermute | solution.py:309
  61.1 5.7 %collective-permute-start.6 = (bf16[272,256]{1,0:T(8,128)(2,1)S(1)}, bf16[272,256]{1,0:T(8,128)(2,1)S(1)}, u32[]{:S(2)}, u32[]{:S(2)}) collective-permute-start(bf16[272,256]{1,0:T(8,128)(2,1)S(1)} %get-tuple-element.30), channel_id=1, source_target_pairs={{0,8},{8,0},{16,24},{24,16},{1,9},{9,1},{17,25},{25,17},{2,10},{10... | collective-permute-start | bytes 417800 | tf_op jit(solution)/shard_map/ppermute | solution.py:309
  62.9 9.5 %collective-permute-start.7 = (bf16[272,256]{1,0:T(8,128)(2,1)S(1)}, bf16[272,256]{1,0:T(8,128)(2,1)S(1)}, u32[]{:S(2)}, u32[]{:S(2)}) collective-permute-start(bf16[272,256]{1,0:T(8,128)(2,1)S(1)} %get-tuple-element.30), channel_id=1, source_target_pairs={{0,16},{8,24},{16,0},{24,8},{1,17},{9,25},{17,1},{25,9},{2,18},{10... | collective-permute-start | bytes 417800 | tf_op jit(solution)/shard_map/ppermute | solution.py:309
  66.1 8.4 %collective-permute-start.8 = (bf16[272,256]{1,0:T(8,128)(2,1)S(1)}, bf16[272,256]{1,0:T(8,128)(2,1)S(1)}, u32[]{:S(2)}, u32[]{:S(2)}) collective-permute-start(bf16[272,256]{1,0:T(8,128)(2,1)S(1)} %get-tuple-element.30), channel_id=1, source_target_pairs={{0,24},{8,16},{16,8},{24,0},{1,25},{9,17},{17,9},{25,1},{2,26},{10... | collective-permute-start | bytes 417800 | tf_op jit(solution)/shard_map/ppermute | solution.py:309
  74.5 14.2 %collective-permute-start.9 = (f32[272,256]{1,0:T(8,128)S(1)}, f32[272,256]{1,0:T(8,128)S(1)}, u32[]{:S(2)}, u32[]{:S(2)}) collective-permute-start(f32[272,256]{1,0:T(8,128)S(1)} %add_add_fusion), channel_id=1, source_target_pairs={{0,4},{4,0},{1,5},{5,1},{2,6},{6,2},{3,7},{7,3},{8,12},{12,8},{9,1... | collective-permute-start | bytes 835592 | tf_op jit(solution)/shard_map/ppermute | solution.py:309
  77.6 1.2 %copy-start.5 = (bf16[2048,256]{1,0:T(8,128)(2,1)S(1)}, bf16[2048,256]{1,0:T(8,128)(2,1)}, u32[]{:S(2)}) copy-start(bf16[2048,256]{1,0:T(8,128)(2,1)} %copy-done.4) | copy-start | bytes 3145732
  88.8 12.8 %collective-permute-start.10 = (bf16[272,256]{1,0:T(8,128)(2,1)S(1)}, bf16[272,256]{1,0:T(8,128)(2,1)S(1)}, u32[]{:S(2)}, u32[]{:S(2)}) collective-permute-start(bf16[272,256]{1,0:T(8,128)(2,1)S(1)} %add_convert_fusion.refs_0_), channel_id=1, source_target_pairs={{0,1},{1,0},{2,3},{3,2},{4,5},{5,4},{6,7},{7,6},{8,9},{9,8},{10,11... | collective-permute-start | bytes 417800 | tf_op jit(solution)/shard_map/ppermute | solution.py:309
  89.1 12.5 %collective-permute-start.11 = (bf16[272,256]{1,0:T(8,128)(2,1)S(1)}, bf16[272,256]{1,0:T(8,128)(2,1)S(1)}, u32[]{:S(2)}, u32[]{:S(2)}) collective-permute-start(bf16[272,256]{1,0:T(8,128)(2,1)S(1)} %add_convert_fusion.refs_0_), channel_id=1, source_target_pairs={{0,2},{1,3},{2,0},{3,1},{4,6},{5,7},{6,4},{7,5},{8,10},{9,11},{10,... | collective-permute-start | bytes 417800 | tf_op jit(solution)/shard_map/ppermute | solution.py:309
  93.1 8.5 %collective-permute-start.12 = (bf16[272,256]{1,0:T(8,128)(2,1)S(1)}, bf16[272,256]{1,0:T(8,128)(2,1)S(1)}, u32[]{:S(2)}, u32[]{:S(2)}) collective-permute-start(bf16[272,256]{1,0:T(8,128)(2,1)S(1)} %add_convert_fusion.refs_0_), channel_id=1, source_target_pairs={{0,3},{1,2},{2,1},{3,0},{4,7},{5,6},{6,5},{7,4},{8,11},{9,10},{10,... | collective-permute-start | bytes 417800 | tf_op jit(solution)/shard_map/ppermute | solution.py:309

commit v5 on v4

--- a/solution.py
+++ b/solution.py
@@ -47,7 +47,7 @@
     return jnp.broadcast_to(row, (128, 128)).T
 
 
-def pass1_kernel(tile, rb, u_ref, pos_ref, cat_ref, *refs):
+def pass1_kernel(tile, rb, u_ref, cat_ref, *refs):
     out_refs, every_ref, (c_ref, acc_ref, m_ref, l_ref, st_ref, sem) = refs[:4], refs[4], refs[5:]
     rows = u_ref.shape[0]
     count, width = cat_ref.shape
@@ -86,7 +86,6 @@
         total = jnp.sum(l_ref[sl], axis=1, keepdims=True)
         acc_ref[sl] = acc_ref[sl] * (1.0 / total)
         st_ref[b : b + 1] = m_ref[sl].T[0:1] + sharpness_divisor * jnp.log(as_row(total))
-    st_ref[rows // 128 :] = pos_ref[...].astype(f32)
     every_ref[...] = jnp.broadcast_to(st_ref[...][None], every_ref.shape)
     x = lax.axis_index("x")
     chunk = rows // 4
@@ -95,20 +94,20 @@
         out_ref[...] = acc_ref[part, :].astype(bf16)
 
 
-def pass1(users, pos, catalog, tile=2048, rb=256):
+def pass1(users, catalog, tile=2048, rb=256):
     rows, width = users.shape
     count = catalog.shape[0]
     return pl.pallas_call(
         functools.partial(pass1_kernel, tile, rb),
-        in_specs=[VMEM, VMEM, HBM],
+        in_specs=[VMEM, HBM],
         out_specs=[VMEM] * 5,
-        out_shape=[struct(rows // 4, width, dtype=bf16)] * 4 + [struct(128, rows // 64, 128)],
+        out_shape=[struct(rows // 4, width, dtype=bf16)] * 4 + [struct(128, rows // 128, 128)],
         scratch_shapes=[
             pltpu.VMEM((count, width), bf16),
             pltpu.VMEM((rows, width), f32),
             pltpu.VMEM((rows, 128), f32),
             pltpu.VMEM((rows, 128), f32),
-            pltpu.VMEM((rows // 64, 128), f32),
+            pltpu.VMEM((rows // 128, 128), f32),
             pltpu.SemaphoreType.DMA((count // tile,)),
         ],
         cost_estimate=pl.CostEstimate(
@@ -116,20 +115,16 @@
         ),
         compiler_params=pltpu.CompilerParams(vmem_limit_bytes=20 * MIB),
         name="pass1",
-    )(users, pos, far(catalog))
+    )(users, far(catalog))
 
 
 def hits_kernel(pos_ref, u_ref, cat_ref, *refs):
-    out_refs, own_ref, (hit_ref, sp_ref, c_ref, found_ref, sem) = refs[:4], refs[4], refs[5:]
+    out_refs, (hit_ref, sp_ref, c_ref, found_ref, sem) = refs[:4], refs[4:]
     rows, width = u_ref.shape
     count = cat_ref.shape[0]
-    items = own_ref.shape[0]
-    x, member, shard = lax.axis_index("x"), lax.axis_index(USER), lax.axis_index(ITEM)
-    mine = pl.ds(pl.multiple_of(member * items, items), items)
-    whole_copy = pltpu.make_async_copy(cat_ref, c_ref, sem.at[0])
-    own_copy = pltpu.make_async_copy(cat_ref.at[mine], own_ref, sem.at[1])
+    x, shard = lax.axis_index("x"), lax.axis_index(ITEM)
+    whole_copy = pltpu.make_async_copy(cat_ref, c_ref, sem)
     whole_copy.start()
-    own_copy.start()
     hit_ref[...] = jnp.zeros_like(hit_ref)
     base = shard * count
     bits = count.bit_length() - 1
@@ -167,7 +162,6 @@
             terms.append(term)
         terms.append(jnp.zeros((13, width), f32))
         out_ref[chunk:] = jnp.concatenate(terms, axis=0).astype(bf16)
-    own_copy.wait()
 
 
 def find_hits(positives, users, catalog):
@@ -176,14 +170,14 @@
     return pl.pallas_call(
         hits_kernel,
         in_specs=[SMEM, VMEM, HBM],
-        out_specs=[VMEM] * 5,
-        out_shape=[struct(rows // 4 + 16, width, dtype=bf16)] * 4 + [struct(count // 4, width, dtype=bf16)],
+        out_specs=[VMEM] * 4,
+        out_shape=[struct(rows // 4 + 16, width, dtype=bf16)] * 4,
         scratch_shapes=[
             pltpu.VMEM((rows, width), f32),
             pltpu.VMEM((rows // 128, 128), f32),
             pltpu.VMEM((count, width), bf16),
             pltpu.SMEM((rows,), jnp.int32),
-            pltpu.SemaphoreType.DMA((2,)),
+            pltpu.SemaphoreType.DMA(()),
         ],
         cost_estimate=pl.CostEstimate(
             flops=rows * count * width // 2, bytes_accessed=2 * count * width, transcendentals=0
@@ -198,13 +192,10 @@
     x, member, shard = lax.axis_index("x"), lax.axis_index(USER), lax.axis_index(ITEM)
     shards = all_ref.shape[0] // 4
     chunk, width = u_refs[0].shape
-    half = all_ref.shape[1] // 2
     for k, l_ref in enumerate(l_refs):
-        first = (member ^ k) * shards
-        stats = all_ref[pl.ds(first, shards), 0:half]
+        stats = all_ref[pl.ds((member ^ k) * shards, shards)]
         top = jnp.max(stats, axis=0)
-        l_ref[0:half] = top + sharpness_divisor * jnp.log(jnp.sum(exp_of(stats - top[None]), axis=0))
-        l_ref[half:] = all_ref[first, half:]
+        l_ref[...] = top + sharpness_divisor * jnp.log(jnp.sum(exp_of(stats - top[None]), axis=0))
     for h in range(chunk // 128):
         sl = slice(h * 128, (h + 1) * 128)
         row = pl.ds(x * 2 + h, 1)
@@ -255,41 +246,39 @@
     )(*near([lse4, *parts]))
 
 
-def pass2_kernel(tile, lead, c_ref, *refs):
-    us, infos, out_ref = refs[:4], refs[4:8], refs[-1]
+def pass2_kernel(tile, items, lead, c_ref, *refs):
+    us, infos, poss, out_ref = refs[:4], refs[4:8], refs[8:12], refs[-1]
     member, shard = lax.axis_index(USER), lax.axis_index(ITEM)
     start = (lead + pl.program_id(0)) * tile
-    items = c_ref.shape[0]
-    c = c_ref[pl.ds(pl.multiple_of(start, tile), tile), :]
+    c = c_ref[...]
     item = lax.broadcasted_iota(jnp.int32, (tile, 128), 0) + (shard * 4 + member) * items + start
-    item = item.astype(f32)
     total = jnp.zeros((tile, c.shape[1]), f32)
-    for u_ref, info_ref in zip(us, infos):
+    for u_ref, info_ref, pos_ref in zip(us, infos, poss):
         u = u_ref[...]
         blocks = u.shape[0] // 128
         r = lax.dot_general(c, u, NT, preferred_element_type=f32)
         ws = []
         for j in range(blocks):
             w = exp_of(r[:, j * 128 : (j + 1) * 128] - info_ref[j : j + 1])
-            hit = info_ref[blocks + j : blocks + j + 1] == item
-            ws.append(jnp.where(hit, w - 1.0, w).astype(bf16))
+            ws.append(jnp.where(pos_ref[j : j + 1] == item, w - 1.0, w).astype(bf16))
         total = total + jnp.dot(jnp.concatenate(ws, axis=1), u, preferred_element_type=f32)
     out_ref[...] = (total / sharpness_divisor).astype(out_ref.dtype)
 
 
-def pass2(own, us, infos, start, stop, before, tile=512):
-    items, width = own.shape
+def pass2(catalog, us, infos, poss, start, stop, before, tile=512):
+    items, width = catalog.shape[0] // 4, catalog.shape[1]
     rows = us[0].shape[0]
     lead = start // tile
-    in_specs = [VMEM] * 9
-    args = [own, *us, *infos]
+    mine = lambda i: (lax.axis_index(USER) * (items // tile) + lead + i, 0)
+    in_specs = [pl.BlockSpec((tile, width), mine)] + [VMEM] * 12
+    args = [far(catalog), *near([*us, *infos, *poss])]
     aliases = {}
     if before is not None:
         in_specs.append(ANY)
         aliases = {len(args): 0}
         args.append(before)
     return pl.pallas_call(
-        functools.partial(pass2_kernel, tile, lead),
+        functools.partial(pass2_kernel, tile, items, lead),
         grid=((stop - start) // tile,),
         in_specs=in_specs,
         out_specs=pl.BlockSpec((tile, width), lambda i: (lead + i, 0)),
@@ -302,7 +291,7 @@
         ),
         compiler_params=pltpu.CompilerParams(vmem_limit_bytes=14 * MIB),
         name="pass2",
-    )(*near(args[:9]), *args[9:])
+    )(*args)
 
 
 def swap(x, axis, size, k):
@@ -315,22 +304,23 @@
     pos = positives.reshape(rows // 128, 128)
     over = swap(users, USER, 4, 2)
     us = [users, swap(users, USER, 4, 1), over, swap(over, USER, 4, 1)]
-    *pieces, every = pass1(users, pos, catalog)
+    poss = [pos] + [swap(pos, USER, 4, k) for k in (1, 2, 3)]
+    *pieces, every = pass1(users, catalog)
     every = lax.all_to_all(every, USER + ITEM, 0, 0, tiled=True)
-    *hits, own = find_hits(positives, users, catalog)
+    hits = find_hits(positives, users, catalog)
     pieces = [pieces[0]] + [swap(pieces[k], "x", 4, k) for k in (1, 2, 3)]
     hits = [hits[0]] + [swap(hits[k], "x", 4, k) for k in (1, 2, 3)]
     *infos, value = combine(every, pieces, hits)
 
     a = [value] + [swap(value, "z", 4, k) for k in (1, 2, 3)]
-    item_grad = pass2(own, us, infos, 0, SPLIT[0], None)
+    item_grad = pass2(catalog, us, infos, poss, 0, SPLIT[0], None)
     a = [v.astype(f32) for v in a]
     value = (a[0] + a[1]) + (a[2] + a[3])
     other = swap(value, "y_hi", 2, 1)
-    item_grad = pass2(own, us, infos, SPLIT[0], SPLIT[1], item_grad)
+    item_grad = pass2(catalog, us, infos, poss, SPLIT[0], SPLIT[1], item_grad)
     value = (value + other).astype(bf16)
     got = [value] + [swap(value, "x", 4, k) for k in (1, 2, 3)]
-    item_grad = pass2(own, us, infos, SPLIT[1], items, item_grad)
+    item_grad = pass2(catalog, us, infos, poss, SPLIT[1], items, item_grad)
     user_grad, loss = finish(infos[0], got, rows)
     return loss.reshape(rows), user_grad, item_grad
 

time: 103 us -> 100 us (0.971)
  the two profiles are of different devices: /device:TPU:0 before, /device:TPU:1 now
where the time goes in v5:
time: 100 us
  starting transfers between devices  41.1 us (41%)
  Pallas kernels  38.6 us (39%)
  waiting for transfers between devices  18.5 us (18%)
  local copies, waits for them, and re-layouts  1.04 us (1%)
    ppermute x19, starting transfers between devices, swap(): return lax.ppermute(x, axis, [(i, i ^ k) for i in range(size)])  29.6 us
    ppermute x19, waiting for transfers between devices, swap(): return lax.ppermute(x, axis, [(i, i ^ k) for i in range(size)])  18.5 us
    pallas_call x3, Pallas kernels, pass2(): pl.pallas_call(functools.partial(pass2_kernel, tile, items, lead), grid=(...  17.2 us
    pallas_call x1, Pallas kernels, pass1(): pl.pallas_call(functools.partial(pass1_kernel, tile, rb), in_specs=[VMEM,...  15.9 us
    all_to_all x1, starting transfers between devices, per_device(): every = lax.all_to_all(every, USER + ITEM, 0, 0, tiled=True)  11.5 us
    pallas_call x1, Pallas kernels, find_hits(): pl.pallas_call(hits_kernel, in_specs=[SMEM, VMEM, HBM], out_specs=[VMEM]...  4.18 us
  transfers between devices with their start and end apart: 20, of which 6 were waited for; matrix products, arithmetic and copies ran while one was open for 0% of the time, Pallas kernels for 22%

profile of v5, /device:TPU:1, one launch (start us, length us, event | category | flops | bytes accessed | tf_op | source)
XLA Modules:
  0.0 100.1 jit_solution(17492580516053916771)
XLA Ops:
  0.6 1.0 %copy-done = bf16[1024,256]{1,0:T(8,128)(2,1)S(1)} copy-done((bf16[1024,256]{1,0:T(8,128)(2,1)S(1)}, bf16[1024,256]{1,0:T(8,128)(2,1)}, u32[]{:S(2)}) %copy-start) | copy-done | bytes 524312
  1.7 15.9 %pass1.1 = (bf16[256,256]{1,0:T(8,128)(2,1)S(1)}, bf16[256,256]{1,0:T(8,128)(2,1)S(1)}, bf16[256,256]{1,0:T(8,128)(2,1)S(1)}, bf16[256,256]{1,0:T(8,128)(2,1)S(1)}, f32[128,8,128]{2,1,0:T(8,128)}) custom-call(bf16[1024,256]{1,0:T(8,128)(2,1)S(1)} %copy-done, bf16[8192,256]{1,0:T(8,128)(2,1)} %c_ref.5), custom_call_target="tpu_custom_call" | custom-call | flops 8589934592 | bytes 4194304 | tf_op jit(solution)/shard_map/pass1/pallas_call | solution.py:100
  17.6 11.5 %all-to-all-start = ((f32[128,8,128]{2,1,0:T(8,128)}), f32[128,8,128]{2,1,0:T(8,128)S(1)}, u32[]{:S(2)}, u32[]{:S(2)}) async-start(f32[128,8,128]{2,1,0:T(8,128)} %get-tuple-element.19), calls=%async_computation | async-start | bytes 1048576 | tf_op jit(solution)/shard_map/all_to_all | solution.py:309
  29.1 1.4 %collective-permute-start.14 = (bf16[1024,256]{1,0:T(8,128)(2,1)S(1)}, bf16[1024,256]{1,0:T(8,128)(2,1)S(1)}, u32[]{:S(2)}, u32[]{:S(2)}) collective-permute-start(bf16[1024,256]{1,0:T(8,128)(2,1)S(1)} %copy-done.1), channel_id=1, source_target_pairs={{0,64},{32,96},{64,0},{96,32},{1,65},{33,97},{65,1},{97,33},{2,66}... | collective-permute-start | bytes 1572872 | tf_op jit(solution)/shard_map/ppermute | solution.py:298
  30.6 1.2 %collective-permute-start = (bf16[256,256]{1,0:T(8,128)(2,1)S(1)}, bf16[256,256]{1,0:T(8,128)(2,1)S(1)}, u32[]{:S(2)}, u32[]{:S(2)}) collective-permute-start(bf16[256,256]{1,0:T(8,128)(2,1)S(1)} %get-tuple-element.21), channel_id=1, source_target_pairs={{0,1},{1,0},{2,3},{3,2},{4,5},{5,4},{6,7},{7,6},{8,9},{9,8},{10,11... | collective-permute-start | bytes 393224 | tf_op jit(solution)/shard_map/ppermute | solution.py:298
  31.8 2.4 %collective-permute-start.1 = (bf16[256,256]{1,0:T(8,128)(2,1)S(1)}, bf16[256,256]{1,0:T(8,128)(2,1)S(1)}, u32[]{:S(2)}, u32[]{:S(2)}) collective-permute-start(bf16[256,256]{1,0:T(8,128)(2,1)S(1)} %get-tuple-element.22), channel_id=1, source_target_pairs={{0,2},{1,3},{2,0},{3,1},{4,6},{5,7},{6,4},{7,5},{8,10},{9,11},{10,... | collective-permute-start | bytes 393224 | tf_op jit(solution)/shard_map/ppermute | solution.py:298
  34.2 4.2 %hits.1 = (bf16[272,256]{1,0:T(8,128)(2,1)S(1)}, bf16[272,256]{1,0:T(8,128)(2,1)S(1)}, bf16[272,256]{1,0:T(8,128)(2,1)S(1)}, bf16[272,256]{1,0:T(8,128)(2,1)S(1)}) custom-call(s32[1024]{0:T(1024)S(1)} %copy-done.2, bf16[1024,256]{1,0:T(8,128)(2,1)S(1)} %copy-done.1, bf16[8192,256]{1,0:T(8,128)(2,1)} %c_ref.5), custom_call_target="tpu_custom_call" | custom-call | flops 1073741824 | bytes 4194304 | tf_op jit(solution)/shard_map/hits/pallas_call | solution.py:170
  38.3 0.1 collective-permute-start.3
  38.4 1.7 %collective-permute-start.4 = (bf16[272,256]{1,0:T(8,128)(2,1)S(1)}, bf16[272,256]{1,0:T(8,128)(2,1)S(1)}, u32[]{:S(2)}, u32[]{:S(2)}) collective-permute-start(bf16[272,256]{1,0:T(8,128)(2,1)S(1)} %get-tuple-element.26), channel_id=1, source_target_pairs={{0,2},{1,3},{2,0},{3,1},{4,6},{5,7},{6,4},{7,5},{8,10},{9,11},{10,... | collective-permute-start | bytes 417800 | tf_op jit(solution)/shard_map/ppermute | solution.py:298
  40.2 2.1 %collective-permute-start.5 = (bf16[272,256]{1,0:T(8,128)(2,1)S(1)}, bf16[272,256]{1,0:T(8,128)(2,1)S(1)}, u32[]{:S(2)}, u32[]{:S(2)}) collective-permute-start(bf16[272,256]{1,0:T(8,128)(2,1)S(1)} %get-tuple-element.27), channel_id=1, source_target_pairs={{0,3},{1,2},{2,1},{3,0},{4,7},{5,6},{6,5},{7,4},{8,11},{9,10},{10,... | collective-permute-start | bytes 417800 | tf_op jit(solution)/shard_map/ppermute | solution.py:298
  42.3 0.9 collective-permute-done.1.refs_2_
  43.2 0.9 collective-permute-start.2
  44.1 8.4 %collective-permute-done.2.refs_3_ = bf16[256,256]{1,0:T(8,128)(2,1)S(1)} collective-permute-done((bf16[256,256]{1,0:T(8,128)(2,1)S(1)}, bf16[256,256]{1,0:T(8,128)(2,1)S(1)}, u32[]{:S(2)}, u32[]{:S(2)}) %collective-permute-start.2) | collective-permute-done | bytes 131104 | tf_op jit(solution)/shard_map/ppermute | solution.py:298
  52.5 0.4 combine.1
  52.9 1.4 %collective-permute-start.6 = (bf16[272,256]{1,0:T(8,128)(2,1)S(1)}, bf16[272,256]{1,0:T(8,128)(2,1)S(1)}, u32[]{:S(2)}, u32[]{:S(2)}) collective-permute-start(bf16[272,256]{1,0:T(8,128)(2,1)S(1)} %get-tuple-element.29), channel_id=1, source_target_pairs={{0,8},{8,0},{16,24},{24,16},{1,9},{9,1},{17,25},{25,17},{2,10},{10... | collective-permute-start | bytes 417800 | tf_op jit(solution)/shard_map/ppermute | solution.py:298
  54.3 2.9 %collective-permute-start.7 = (bf16[272,256]{1,0:T(8,128)(2,1)S(1)}, bf16[272,256]{1,0:T(8,128)(2,1)S(1)}, u32[]{:S(2)}, u32[]{:S(2)}) collective-permute-start(bf16[272,256]{1,0:T(8,128)(2,1)S(1)} %get-tuple-element.29), channel_id=1, source_target_pairs={{0,16},{8,24},{16,0},{24,8},{1,17},{9,25},{17,1},{25,9},{2,18},{10... | collective-permute-start | bytes 417800 | tf_op jit(solution)/shard_map/ppermute | solution.py:298
  57.3 2.0 %collective-permute-start.13 = (bf16[1024,256]{1,0:T(8,128)(2,1)S(1)}, bf16[1024,256]{1,0:T(8,128)(2,1)S(1)}, u32[]{:S(2)}, u32[]{:S(2)}) collective-permute-start(bf16[1024,256]{1,0:T(8,128)(2,1)S(1)} %copy-done.1), channel_id=1, source_target_pairs={{0,32},{32,0},{64,96},{96,64},{1,33},{33,1},{65,97},{97,65},{2,34}... | collective-permute-start | bytes 1572872 | tf_op jit(solution)/shard_map/ppermute | solution.py:298
  59.3 2.9 %collective-permute-done.7 = bf16[272,256]{1,0:T(8,128)(2,1)S(1)} collective-permute-done((bf16[272,256]{1,0:T(8,128)(2,1)S(1)}, bf16[272,256]{1,0:T(8,128)(2,1)S(1)}, u32[]{:S(2)}, u32[]{:S(2)}) %collective-permute-start.7) | collective-permute-done | bytes 139296 | tf_op jit(solution)/shard_map/ppermute | solution.py:298
  62.3 2.9 %collective-permute-done.8 = bf16[272,256]{1,0:T(8,128)(2,1)S(1)} collective-permute-done((bf16[272,256]{1,0:T(8,128)(2,1)S(1)}, bf16[272,256]{1,0:T(8,128)(2,1)S(1)}, u32[]{:S(2)}, u32[]{:S(2)}) %collective-permute-start.8) | collective-permute-done | bytes 139296 | tf_op jit(solution)/shard_map/ppermute | solution.py:298
  65.2 3.3 %collective-permute-start.9 = (f32[272,256]{1,0:T(8,128)S(1)}, f32[272,256]{1,0:T(8,128)S(1)}, u32[]{:S(2)}, u32[]{:S(2)}) collective-permute-start(f32[272,256]{1,0:T(8,128)S(1)} %add_add_fusion), channel_id=1, source_target_pairs={{0,4},{4,0},{1,5},{5,1},{2,6},{6,2},{3,7},{7,3},{8,12},{12,8},{9,1... | collective-permute-start | bytes 835592 | tf_op jit(solution)/shard_map/ppermute | solution.py:298
  68.5 1.7 %collective-permute-start.16 = (s32[8,128]{1,0:T(8,128)S(1)}, s32[8,128]{1,0:T(8,128)S(1)}, u32[]{:S(2)}, u32[]{:S(2)}) collective-permute-start(s32[8,128]{1,0:T(8,128)S(1)} %bitcast.2), channel_id=1, source_target_pairs={{0,32},{32,0},{64,96},{96,64},{1,33},{33,1},{65,97},{97,65},{2,34}... | collective-permute-start | bytes 12296 | tf_op jit(solution)/shard_map/ppermute | solution.py:298
  70.2 0.6 collective-permute-start.17
  70.8 3.2 %collective-permute-done.9 = f32[272,256]{1,0:T(8,128)S(1)} collective-permute-done((f32[272,256]{1,0:T(8,128)S(1)}, f32[272,256]{1,0:T(8,128)S(1)}, u32[]{:S(2)}, u32[]{:S(2)}) %collective-permute-start.9) | collective-permute-done | bytes 278560 | tf_op jit(solution)/shard_map/ppermute | solution.py:298
  74.0 4.0 %collective-permute-start.18 = (s32[8,128]{1,0:T(8,128)S(1)}, s32[8,128]{1,0:T(8,128)S(1)}, u32[]{:S(2)}, u32[]{:S(2)}) collective-permute-start(s32[8,128]{1,0:T(8,128)S(1)} %bitcast.4), channel_id=1, source_target_pairs={{0,96},{32,64},{64,32},{96,0},{1,97},{33,65},{65,33},{97,1},{2,98}... | collective-permute-start | bytes 12296 | tf_op jit(solution)/shard_map/ppermute | solution.py:298
  78.0 0.2 collective-permute-start.10
  78.2 0.9 collective-permute-start.11
  79.1 0.2 collective-permute-done.18.refs_11_
  79.3 2.7 %collective-permute-start.12 = (bf16[272,256]{1,0:T(8,128)(2,1)S(1)}, bf16[272,256]{1,0:T(8,128)(2,1)S(1)}, u32[]{:S(2)}, u32[]{:S(2)}) collective-permute-start(bf16[272,256]{1,0:T(8,128)(2,1)S(1)} %add_convert_fusion.refs_0_), channel_id=1, source_target_pairs={{0,3},{1,2},{2,1},{3,0},{4,7},{5,6},{6,5},{7,4},{8,11},{9,10},{10,... | collective-permute-start | bytes 417800 | tf_op jit(solution)/shard_map/ppermute | solution.py:298
  82.0 4.7 %pass2.3.refs_12_ = bf16[2048,256]{1,0:T(8,128)(2,1)} custom-call(bf16[8192,256]{1,0:T(8,128)(2,1)} %c_ref.5, bf16[1024,256]{1,0:T(8,128)(2,1)S(1)} %copy-done.1, bf16[1024,256]{1,0:T(8,128)(2,1)S(1)} %collective-permute-done.13.refs_1_, bf16[1024,256]{1,0:T(8,128)(2,1)S(1)} %collective-permute-done.14.refs_2_, ...), custom_call_target="tpu_custom_call" | custom-call | flops 2147483648 | bytes 2097152 | tf_op jit(solution)/shard_map/pass2/pallas_call | solution.py:280
  86.7 4.7 %pass2.4.refs_12_ = bf16[2048,256]{1,0:T(8,128)(2,1)} custom-call(bf16[8192,256]{1,0:T(8,128)(2,1)} %c_ref.5, bf16[1024,256]{1,0:T(8,128)(2,1)S(1)} %copy-done.1, bf16[1024,256]{1,0:T(8,128)(2,1)S(1)} %collective-permute-done.13.refs_1_, bf16[1024,256]{1,0:T(8,128)(2,1)S(1)} %collective-permute-done.14.refs_2_, ...), custom_call_target="tpu_custom_call", output_to_operand_aliasing={{}: (13, {})} | custom-call | flops 2147483648 | bytes 2097152 | tf_op jit(solution)/shard_map/pass2/pallas_call | solution.py:280
  91.4 7.8 %pass2.5 = bf16[2048,256]{1,0:T(8,128)(2,1)} custom-call(bf16[8192,256]{1,0:T(8,128)(2,1)} %c_ref.5, bf16[1024,256]{1,0:T(8,128)(2,1)S(1)} %copy-done.1, bf16[1024,256]{1,0:T(8,128)(2,1)S(1)} %collective-permute-done.13.refs_1_, bf16[1024,256]{1,0:T(8,128)(2,1)S(1)} %collective-permute-done.14.refs_2_, ...), custom_call_target="tpu_custom_call", output_to_operand_aliasing={{}: (13, {})} | custom-call | flops 4294967296 | bytes 2097152 | tf_op jit(solution)/shard_map/pass2/pallas_call | solution.py:280
  99.2 0.8 finish.1
  (23 shorter events, 0.2 us)
Async XLA Ops:
  0.6 1.0 %copy-start = (bf16[1024,256]{1,0:T(8,128)(2,1)S(1)}, bf16[1024,256]{1,0:T(8,128)(2,1)}, u32[]{:S(2)}) copy-start(bf16[1024,256]{1,0:T(8,128)(2,1)} %refs_0_.5) | copy-start | bytes 1572868
  1.7 27.5 %copy-start.1 = (bf16[1024,256]{1,0:T(8,128)(2,1)S(1)}, bf16[1024,256]{1,0:T(8,128)(2,1)}, u32[]{:S(2)}) copy-start(bf16[1024,256]{1,0:T(8,128)(2,1)} %refs_0_.5) | copy-start | bytes 1572868
  1.7 32.5 %copy-start.2 = (s32[1024]{0:T(1024)S(1)}, s32[1024]{0:T(1024)}, u32[]{:S(2)}) copy-start(s32[1024]{0:T(1024)} %pos_ref.1) | copy-start | bytes 12292
  17.6 34.9 %all-to-all-start = ((f32[128,8,128]{2,1,0:T(8,128)}), f32[128,8,128]{2,1,0:T(8,128)S(1)}, u32[]{:S(2)}, u32[]{:S(2)}) async-start(f32[128,8,128]{2,1,0:T(8,128)} %get-tuple-element.19), calls=%async_computation | async-start | bytes 1048576 | tf_op jit(solution)/shard_map/all_to_all | solution.py:309
  29.1 30.1 %collective-permute-start.14 = (bf16[1024,256]{1,0:T(8,128)(2,1)S(1)}, bf16[1024,256]{1,0:T(8,128)(2,1)S(1)}, u32[]{:S(2)}, u32[]{:S(2)}) collective-permute-start(bf16[1024,256]{1,0:T(8,128)(2,1)S(1)} %copy-done.1), channel_id=1, source_target_pairs={{0,64},{32,96},{64,0},{96,32},{1,65},{33,97},{65,1},{97,33},{2,66}... | collective-permute-start | bytes 1572872 | tf_op jit(solution)/shard_map/ppermute | solution.py:298
  30.6 9.6 %collective-permute-start = (bf16[256,256]{1,0:T(8,128)(2,1)S(1)}, bf16[256,256]{1,0:T(8,128)(2,1)S(1)}, u32[]{:S(2)}, u32[]{:S(2)}) collective-permute-start(bf16[256,256]{1,0:T(8,128)(2,1)S(1)} %get-tuple-element.21), channel_id=1, source_target_pairs={{0,1},{1,0},{2,3},{3,2},{4,5},{5,4},{6,7},{7,6},{8,9},{9,8},{10,11... | collective-permute-start | bytes 393224 | tf_op jit(solution)/shard_map/ppermute | solution.py:298
  31.8 11.5 %collective-permute-start.1 = (bf16[256,256]{1,0:T(8,128)(2,1)S(1)}, bf16[256,256]{1,0:T(8,128)(2,1)S(1)}, u32[]{:S(2)}, u32[]{:S(2)}) collective-permute-start(bf16[256,256]{1,0:T(8,128)(2,1)S(1)} %get-tuple-element.22), channel_id=1, source_target_pairs={{0,2},{1,3},{2,0},{3,1},{4,6},{5,7},{6,4},{7,5},{8,10},{9,11},{10,... | collective-permute-start | bytes 393224 | tf_op jit(solution)/shard_map/ppermute | solution.py:298
  38.3 14.1 %collective-permute-start.3 = (bf16[272,256]{1,0:T(8,128)(2,1)S(1)}, bf16[272,256]{1,0:T(8,128)(2,1)S(1)}, u32[]{:S(2)}, u32[]{:S(2)}) collective-permute-start(bf16[272,256]{1,0:T(8,128)(2,1)S(1)} %get-tuple-element.25), channel_id=1, source_target_pairs={{0,1},{1,0},{2,3},{3,2},{4,5},{5,4},{6,7},{7,6},{8,9},{9,8},{10,11... | collective-permute-start | bytes 417800 | tf_op jit(solution)/shard_map/ppermute | solution.py:298
  38.4 14.0 %collective-permute-start.4 = (bf16[272,256]{1,0:T(8,128)(2,1)S(1)}, bf16[272,256]{1,0:T(8,128)(2,1)S(1)}, u32[]{:S(2)}, u32[]{:S(2)}) collective-permute-start(bf16[272,256]{1,0:T(8,128)(2,1)S(1)} %get-tuple-element.26), channel_id=1, source_target_pairs={{0,2},{1,3},{2,0},{3,1},{4,6},{5,7},{6,4},{7,5},{8,10},{9,11},{10,... | collective-permute-start | bytes 417800 | tf_op jit(solution)/shard_map/ppermute | solution.py:298
  40.2 12.3 %collective-permute-start.5 = (bf16[272,256]{1,0:T(8,128)(2,1)S(1)}, bf16[272,256]{1,0:T(8,128)(2,1)S(1)}, u32[]{:S(2)}, u32[]{:S(2)}) collective-permute-start(bf16[272,256]{1,0:T(8,128)(2,1)S(1)} %get-tuple-element.27), channel_id=1, source_target_pairs={{0,3},{1,2},{2,1},{3,0},{4,7},{5,6},{6,5},{7,4},{8,11},{9,10},{10,... | collective-permute-start | bytes 417800 | tf_op jit(solution)/shard_map/ppermute | solution.py:298
  43.2 9.2 %collective-permute-start.2 = (bf16[256,256]{1,0:T(8,128)(2,1)S(1)}, bf16[256,256]{1,0:T(8,128)(2,1)S(1)}, u32[]{:S(2)}, u32[]{:S(2)}) collective-permute-start(bf16[256,256]{1,0:T(8,128)(2,1)S(1)} %get-tuple-element.23), channel_id=1, source_target_pairs={{0,3},{1,2},{2,1},{3,0},{4,7},{5,6},{6,5},{7,4},{8,11},{9,10},{10,... | collective-permute-start | bytes 393224 | tf_op jit(solution)/shard_map/ppermute | solution.py:298
  52.9 6.5 %collective-permute-start.6 = (bf16[272,256]{1,0:T(8,128)(2,1)S(1)}, bf16[272,256]{1,0:T(8,128)(2,1)S(1)}, u32[]{:S(2)}, u32[]{:S(2)}) collective-permute-start(bf16[272,256]{1,0:T(8,128)(2,1)S(1)} %get-tuple-element.29), channel_id=1, source_target_pairs={{0,8},{8,0},{16,24},{24,16},{1,9},{9,1},{17,25},{25,17},{2,10},{10... | collective-permute-start | bytes 417800 | tf_op jit(solution)/shard_map/ppermute | solution.py:298
  54.3 8.0 %collective-permute-start.7 = (bf16[272,256]{1,0:T(8,128)(2,1)S(1)}, bf16[272,256]{1,0:T(8,128)(2,1)S(1)}, u32[]{:S(2)}, u32[]{:S(2)}) collective-permute-start(bf16[272,256]{1,0:T(8,128)(2,1)S(1)} %get-tuple-element.29), channel_id=1, source_target_pairs={{0,16},{8,24},{16,0},{24,8},{1,17},{9,25},{17,1},{25,9},{2,18},{10... | collective-permute-start | bytes 417800 | tf_op jit(solution)/shard_map/ppermute | solution.py:298
  57.2 7.9 %collective-permute-start.8 = (bf16[272,256]{1,0:T(8,128)(2,1)S(1)}, bf16[272,256]{1,0:T(8,128)(2,1)S(1)}, u32[]{:S(2)}, u32[]{:S(2)}) collective-permute-start(bf16[272,256]{1,0:T(8,128)(2,1)S(1)} %get-tuple-element.29), channel_id=1, source_target_pairs={{0,24},{8,16},{16,8},{24,0},{1,25},{9,17},{17,9},{25,1},{2,26},{10... | collective-permute-start | bytes 417800 | tf_op jit(solution)/shard_map/ppermute | solution.py:298
  57.3 24.7 %collective-permute-start.13 = (bf16[1024,256]{1,0:T(8,128)(2,1)S(1)}, bf16[1024,256]{1,0:T(8,128)(2,1)S(1)}, u32[]{:S(2)}, u32[]{:S(2)}) collective-permute-start(bf16[1024,256]{1,0:T(8,128)(2,1)S(1)} %copy-done.1), channel_id=1, source_target_pairs={{0,32},{32,0},{64,96},{96,64},{1,33},{33,1},{65,97},{97,65},{2,34}... | collective-permute-start | bytes 1572872 | tf_op jit(solution)/shard_map/ppermute | solution.py:298
  59.2 22.7 %collective-permute-start.15 = (bf16[1024,256]{1,0:T(8,128)(2,1)S(1)}, bf16[1024,256]{1,0:T(8,128)(2,1)S(1)}, u32[]{:S(2)}, u32[]{:S(2)}) collective-permute-start(bf16[1024,256]{1,0:T(8,128)(2,1)S(1)} %collective-permute-done.14.refs_2_), channel_id=1, source_target_pairs={{0,32},{32,0},{64,96},{96,64},{1,33},{33,1},{65,97},{97,65},{2,34}... | collective-permute-start | bytes 1572872 | tf_op jit(solution)/shard_map/ppermute | solution.py:298
  65.2 8.7 %collective-permute-start.9 = (f32[272,256]{1,0:T(8,128)S(1)}, f32[272,256]{1,0:T(8,128)S(1)}, u32[]{:S(2)}, u32[]{:S(2)}) collective-permute-start(f32[272,256]{1,0:T(8,128)S(1)} %add_add_fusion), channel_id=1, source_target_pairs={{0,4},{4,0},{1,5},{5,1},{2,6},{6,2},{3,7},{7,3},{8,12},{12,8},{9,1... | collective-permute-start | bytes 835592 | tf_op jit(solution)/shard_map/ppermute | solution.py:298
  68.5 9.5 %collective-permute-start.16 = (s32[8,128]{1,0:T(8,128)S(1)}, s32[8,128]{1,0:T(8,128)S(1)}, u32[]{:S(2)}, u32[]{:S(2)}) collective-permute-start(s32[8,128]{1,0:T(8,128)S(1)} %bitcast.2), channel_id=1, source_target_pairs={{0,32},{32,0},{64,96},{96,64},{1,33},{33,1},{65,97},{97,65},{2,34}... | collective-permute-start | bytes 12296 | tf_op jit(solution)/shard_map/ppermute | solution.py:298
  70.2 8.0 %collective-permute-start.17 = (s32[8,128]{1,0:T(8,128)S(1)}, s32[8,128]{1,0:T(8,128)S(1)}, u32[]{:S(2)}, u32[]{:S(2)}) collective-permute-start(s32[8,128]{1,0:T(8,128)S(1)} %bitcast.3), channel_id=1, source_target_pairs={{0,64},{32,96},{64,0},{96,32},{1,65},{33,97},{65,1},{97,33},{2,66}... | collective-permute-start | bytes 12296 | tf_op jit(solution)/shard_map/ppermute | solution.py:298
  74.0 5.3 %collective-permute-start.18 = (s32[8,128]{1,0:T(8,128)S(1)}, s32[8,128]{1,0:T(8,128)S(1)}, u32[]{:S(2)}, u32[]{:S(2)}) collective-permute-start(s32[8,128]{1,0:T(8,128)S(1)} %bitcast.4), channel_id=1, source_target_pairs={{0,96},{32,64},{64,32},{96,0},{1,97},{33,65},{65,33},{97,1},{2,98}... | collective-permute-start | bytes 12296 | tf_op jit(solution)/shard_map/ppermute | solution.py:298
  78.0 21.2 %collective-permute-start.10 = (bf16[272,256]{1,0:T(8,128)(2,1)S(1)}, bf16[272,256]{1,0:T(8,128)(2,1)S(1)}, u32[]{:S(2)}, u32[]{:S(2)}) collective-permute-start(bf16[272,256]{1,0:T(8,128)(2,1)S(1)} %add_convert_fusion.refs_0_), channel_id=1, source_target_pairs={{0,1},{1,0},{2,3},{3,2},{4,5},{5,4},{6,7},{7,6},{8,9},{9,8},{10,11... | collective-permute-start | bytes 417800 | tf_op jit(solution)/shard_map/ppermute | solution.py:298
  78.2 21.0 %collective-permute-start.11 = (bf16[272,256]{1,0:T(8,128)(2,1)S(1)}, bf16[272,256]{1,0:T(8,128)(2,1)S(1)}, u32[]{:S(2)}, u32[]{:S(2)}) collective-permute-start(bf16[272,256]{1,0:T(8,128)(2,1)S(1)} %add_convert_fusion.refs_0_), channel_id=1, source_target_pairs={{0,2},{1,3},{2,0},{3,1},{4,6},{5,7},{6,4},{7,5},{8,10},{9,11},{10,... | collective-permute-start | bytes 417800 | tf_op jit(solution)/shard_map/ppermute | solution.py:298
  79.3 19.9 %collective-permute-start.12 = (bf16[272,256]{1,0:T(8,128)(2,1)S(1)}, bf16[272,256]{1,0:T(8,128)(2,1)S(1)}, u32[]{:S(2)}, u32[]{:S(2)}) collective-permute-start(bf16[272,256]{1,0:T(8,128)(2,1)S(1)} %add_convert_fusion.refs_0_), channel_id=1, source_target_pairs={{0,3},{1,2},{2,1},{3,0},{4,7},{5,6},{6,5},{7,4},{8,11},{9,10},{10,... | collective-permute-start | bytes 417800 | tf_op jit(solution)/shard_map/ppermute | solution.py:298

commit v6 on v5

--- a/solution.py
+++ b/solution.py
@@ -23,6 +23,16 @@
 MIB = 1 << 20
 
 
+NEAR = (0, 1, 8, 9)
+REST = (0, 3, 24, 27)
+ACROSS = 4
+
+
+def chunk_id():
+    x, z = lax.axis_index("x"), lax.axis_index("z")
+    return ((x ^ (x >> 1)) & 1) + 2 * ((z ^ (z >> 1)) & 1)
+
+
 def exp_of(x):
     return jnp.exp2(x * SCALE)
 
@@ -47,9 +57,11 @@
     return jnp.broadcast_to(row, (128, 128)).T
 
 
-def pass1_kernel(tile, rb, u_ref, cat_ref, *refs):
-    out_refs, every_ref, (c_ref, acc_ref, m_ref, l_ref, st_ref, sem) = refs[:4], refs[4], refs[5:]
+def pass1_kernel(tile, rb, users_ref, cat_ref, *refs):
+    out_refs, every_ref, (u_ref, c_ref, acc_ref, m_ref, l_ref, st_ref, sem, u_sem) = refs[:4], refs[4], refs[5:]
     rows = u_ref.shape[0]
+    u_copy = pltpu.make_async_copy(users_ref, u_ref, u_sem)
+    u_copy.start()
     count, width = cat_ref.shape
     n = count // tile
     copies = []
@@ -60,6 +72,7 @@
     acc_ref[...] = jnp.zeros_like(acc_ref)
     m_ref[...] = jnp.full_like(m_ref, -1e38)
     l_ref[...] = jnp.zeros_like(l_ref)
+    u_copy.wait()
     for i in range(n):
         copies[i].wait()
         c = c_ref[i * tile : (i + 1) * tile]
@@ -87,7 +100,7 @@
         acc_ref[sl] = acc_ref[sl] * (1.0 / total)
         st_ref[b : b + 1] = m_ref[sl].T[0:1] + sharpness_divisor * jnp.log(as_row(total))
     every_ref[...] = jnp.broadcast_to(st_ref[...][None], every_ref.shape)
-    x = lax.axis_index("x")
+    x = chunk_id()
     chunk = rows // 4
     for k, out_ref in enumerate(out_refs):
         part = pl.ds(pl.multiple_of((x ^ k) * chunk, chunk), chunk)
@@ -99,32 +112,38 @@
     count = catalog.shape[0]
     return pl.pallas_call(
         functools.partial(pass1_kernel, tile, rb),
-        in_specs=[VMEM, HBM],
+        in_specs=[HBM, HBM],
         out_specs=[VMEM] * 5,
         out_shape=[struct(rows // 4, width, dtype=bf16)] * 4 + [struct(128, rows // 128, 128)],
         scratch_shapes=[
+            pltpu.VMEM((rows, width), bf16),
             pltpu.VMEM((count, width), bf16),
             pltpu.VMEM((rows, width), f32),
             pltpu.VMEM((rows, 128), f32),
             pltpu.VMEM((rows, 128), f32),
             pltpu.VMEM((rows // 128, 128), f32),
             pltpu.SemaphoreType.DMA((count // tile,)),
+            pltpu.SemaphoreType.DMA(()),
         ],
         cost_estimate=pl.CostEstimate(
             flops=4 * rows * count * width, bytes_accessed=2 * count * width, transcendentals=rows * count
         ),
         compiler_params=pltpu.CompilerParams(vmem_limit_bytes=20 * MIB),
         name="pass1",
-    )(users, far(catalog))
+    )(far(users), far(catalog))
 
 
 def hits_kernel(pos_ref, u_ref, cat_ref, *refs):
-    out_refs, (hit_ref, sp_ref, c_ref, found_ref, sem) = refs[:4], refs[4:]
+    out_refs, own_ref, (hit_ref, sp_ref, c_ref, found_ref, sem) = refs[:4], refs[4], refs[5:]
+    items = own_ref.shape[0]
     rows, width = u_ref.shape
     count = cat_ref.shape[0]
-    x, shard = lax.axis_index("x"), lax.axis_index(ITEM)
-    whole_copy = pltpu.make_async_copy(cat_ref, c_ref, sem)
+    x, shard = chunk_id(), lax.axis_index(ITEM)
+    whole_copy = pltpu.make_async_copy(cat_ref, c_ref, sem.at[0])
     whole_copy.start()
+    mine = pl.ds(pl.multiple_of(lax.axis_index(USER) * items, items), items)
+    own_copy = pltpu.make_async_copy(cat_ref.at[mine], own_ref, sem.at[1])
+    own_copy.start()
     hit_ref[...] = jnp.zeros_like(hit_ref)
     base = shard * count
     bits = count.bit_length() - 1
@@ -162,6 +181,7 @@
             terms.append(term)
         terms.append(jnp.zeros((13, width), f32))
         out_ref[chunk:] = jnp.concatenate(terms, axis=0).astype(bf16)
+    own_copy.wait()
 
 
 def find_hits(positives, users, catalog):
@@ -170,14 +190,14 @@
     return pl.pallas_call(
         hits_kernel,
         in_specs=[SMEM, VMEM, HBM],
-        out_specs=[VMEM] * 4,
-        out_shape=[struct(rows // 4 + 16, width, dtype=bf16)] * 4,
+        out_specs=[VMEM] * 5,
+        out_shape=[struct(rows // 4 + 16, width, dtype=bf16)] * 4 + [struct(count // 4, width, dtype=bf16)],
         scratch_shapes=[
             pltpu.VMEM((rows, width), f32),
             pltpu.VMEM((rows // 128, 128), f32),
             pltpu.VMEM((count, width), bf16),
             pltpu.SMEM((rows,), jnp.int32),
-            pltpu.SemaphoreType.DMA(()),
+            pltpu.SemaphoreType.DMA((2,)),
         ],
         cost_estimate=pl.CostEstimate(
             flops=rows * count * width // 2, bytes_accessed=2 * count * width, transcendentals=0
@@ -189,7 +209,7 @@
 
 def combine_kernel(all_ref, *refs):
     u_refs, h_refs, l_refs, out_ref = refs[:4], refs[4:8], refs[8:12], refs[12]
-    x, member, shard = lax.axis_index("x"), lax.axis_index(USER), lax.axis_index(ITEM)
+    x, member, shard = chunk_id(), lax.axis_index(USER), lax.axis_index(ITEM)
     shards = all_ref.shape[0] // 4
     chunk, width = u_refs[0].shape
     for k, l_ref in enumerate(l_refs):
@@ -201,7 +221,7 @@
         row = pl.ds(x * 2 + h, 1)
         total = jnp.zeros((128, width), f32)
         for k in range(4):
-            weight = exp_of(all_ref[member * shards + (shard ^ k), row, :] - l_refs[0][row, :])
+            weight = exp_of(all_ref[member * shards + (shard ^ NEAR[k]), row, :] - l_refs[0][row, :])
             wide = jnp.concatenate([as_column(weight)] * (width // 128), axis=1)
             total = total + wide * u_refs[k][sl].astype(f32) - h_refs[k][sl].astype(f32)
         out_ref[sl] = (total / sharpness_divisor).astype(bf16)
@@ -223,7 +243,7 @@
 
 def finish_kernel(lse_ref, *refs):
     parts, out_ref, loss_ref = refs[:4], refs[4], refs[5]
-    x = lax.axis_index("x")
+    x = chunk_id()
     chunk = out_ref.shape[0] // 4
     for k, part in enumerate(parts):
         out_ref[pl.ds(pl.multiple_of((x ^ k) * chunk, chunk), chunk), :] = part[0:chunk]
@@ -246,43 +266,48 @@
     )(*near([lse4, *parts]))
 
 
-def pass2_kernel(tile, items, lead, c_ref, *refs):
-    us, infos, poss, out_ref = refs[:4], refs[4:8], refs[8:12], refs[-1]
+def pass2_kernel(tile, lead, n, c_ref, *refs):
+    us, infos, poss, (out_ref, tile_ref, sem) = refs[:4], refs[4:8], refs[8:12], refs[-3:]
     member, shard = lax.axis_index(USER), lax.axis_index(ITEM)
-    start = (lead + pl.program_id(0)) * tile
-    c = c_ref[...]
-    item = lax.broadcasted_iota(jnp.int32, (tile, 128), 0) + (shard * 4 + member) * items + start
-    total = jnp.zeros((tile, c.shape[1]), f32)
-    for u_ref, info_ref, pos_ref in zip(us, infos, poss):
-        u = u_ref[...]
-        blocks = u.shape[0] // 128
-        r = lax.dot_general(c, u, NT, preferred_element_type=f32)
-        ws = []
-        for j in range(blocks):
-            w = exp_of(r[:, j * 128 : (j + 1) * 128] - info_ref[j : j + 1])
-            ws.append(jnp.where(pos_ref[j : j + 1] == item, w - 1.0, w).astype(bf16))
-        total = total + jnp.dot(jnp.concatenate(ws, axis=1), u, preferred_element_type=f32)
-    out_ref[...] = (total / sharpness_divisor).astype(out_ref.dtype)
-
-
-def pass2(catalog, us, infos, poss, start, stop, before, tile=512):
-    items, width = catalog.shape[0] // 4, catalog.shape[1]
+    items = c_ref.shape[0]
+    copies = []
+    for i in range(n):
+        start = (lead + i) * tile
+        c = c_ref[start : start + tile]
+        item = lax.broadcasted_iota(jnp.int32, (tile, 128), 0) + (shard * 4 + member) * items + start
+        total = jnp.zeros((tile, c.shape[1]), f32)
+        for u_ref, info_ref, pos_ref in zip(us, infos, poss):
+            u = u_ref[...]
+            r = lax.dot_general(c, u, NT, preferred_element_type=f32)
+            ws = []
+            for j in range(u.shape[0] // 128):
+                w = exp_of(r[:, j * 128 : (j + 1) * 128] - info_ref[j : j + 1])
+                ws.append(jnp.where(pos_ref[j : j + 1] == item, w - 1.0, w).astype(bf16))
+            total = total + jnp.dot(jnp.concatenate(ws, axis=1), u, preferred_element_type=f32)
+        tile_ref[i] = (total / sharpness_divisor).astype(bf16)
+        copies.append(pltpu.make_async_copy(tile_ref.at[i], out_ref.at[pl.ds(start, tile)], sem.at[i]))
+        copies[-1].start()
+    for copy in copies:
+        copy.wait()
+
+
+def pass2(own, us, infos, poss, start, stop, before, tile=512):
+    items, width = own.shape
     rows = us[0].shape[0]
-    lead = start // tile
-    mine = lambda i: (lax.axis_index(USER) * (items // tile) + lead + i, 0)
-    in_specs = [pl.BlockSpec((tile, width), mine)] + [VMEM] * 12
-    args = [far(catalog), *near([*us, *infos, *poss])]
+    n = (stop - start) // tile
+    in_specs = [VMEM] * 13
+    args = near([own, *us, *infos, *poss])
     aliases = {}
     if before is not None:
-        in_specs.append(ANY)
+        in_specs.append(HBM)
         aliases = {len(args): 0}
         args.append(before)
     return pl.pallas_call(
-        functools.partial(pass2_kernel, tile, items, lead),
-        grid=((stop - start) // tile,),
+        functools.partial(pass2_kernel, tile, start // tile, n),
         in_specs=in_specs,
-        out_specs=pl.BlockSpec((tile, width), lambda i: (lead + i, 0)),
+        out_specs=HBM,
         out_shape=struct(items, width, dtype=bf16),
+        scratch_shapes=[pltpu.VMEM((n, tile, width), bf16), pltpu.SemaphoreType.DMA((n,))],
         input_output_aliases=aliases,
         cost_estimate=pl.CostEstimate(
             flops=16 * rows * (stop - start) * width,
@@ -294,8 +319,29 @@
     )(*args)
 
 
-def swap(x, axis, size, k):
-    return lax.ppermute(x, axis, [(i, i ^ k) for i in range(size)])
+def swap(x, axis, size, k, mask=None):
+    return lax.ppermute(x, axis, [(i, i ^ (k if mask is None else mask)) for i in range(size)])
+
+
+def exchange(xs, masks):
+    return [xs[0]] + [swap(xs[k], ITEM, 32, k, masks[k]) for k in (1, 2, 3)]
+
+
+def add_kernel(*refs):
+    a, out_ref = [ref[...].astype(f32) for ref in refs[:-1]], refs[-1]
+    total = (a[0] + a[1]) + (a[2] + a[3]) if len(a) == 4 else a[0] + a[1]
+    out_ref[...] = total.astype(out_ref.dtype)
+
+
+def add(parts, dtype):
+    return pl.pallas_call(
+        add_kernel,
+        in_specs=[VMEM] * len(parts),
+        out_specs=VMEM,
+        out_shape=struct(*parts[0].shape, dtype=dtype),
+        compiler_params=pltpu.CompilerParams(vmem_limit_bytes=4 * MIB),
+        name="add",
+    )(*near(parts))
 
 
 def per_device(users, catalog, positives):
@@ -307,20 +353,19 @@
     poss = [pos] + [swap(pos, USER, 4, k) for k in (1, 2, 3)]
     *pieces, every = pass1(users, catalog)
     every = lax.all_to_all(every, USER + ITEM, 0, 0, tiled=True)
-    hits = find_hits(positives, users, catalog)
-    pieces = [pieces[0]] + [swap(pieces[k], "x", 4, k) for k in (1, 2, 3)]
-    hits = [hits[0]] + [swap(hits[k], "x", 4, k) for k in (1, 2, 3)]
+    *hits, own = find_hits(positives, users, catalog)
+    pieces = exchange(pieces, NEAR)
+    hits = exchange(hits, NEAR)
     *infos, value = combine(every, pieces, hits)
 
-    a = [value] + [swap(value, "z", 4, k) for k in (1, 2, 3)]
-    item_grad = pass2(catalog, us, infos, poss, 0, SPLIT[0], None)
-    a = [v.astype(f32) for v in a]
-    value = (a[0] + a[1]) + (a[2] + a[3])
-    other = swap(value, "y_hi", 2, 1)
-    item_grad = pass2(catalog, us, infos, poss, SPLIT[0], SPLIT[1], item_grad)
-    value = (value + other).astype(bf16)
-    got = [value] + [swap(value, "x", 4, k) for k in (1, 2, 3)]
-    item_grad = pass2(catalog, us, infos, poss, SPLIT[1], items, item_grad)
+    a = exchange([value] * 4, REST)
+    item_grad = pass2(own, us, infos, poss, 0, SPLIT[0], None)
+    value = add(a, f32)
+    other = swap(value, ITEM, 32, 1, ACROSS)
+    item_grad = pass2(own, us, infos, poss, SPLIT[0], SPLIT[1], item_grad)
+    value = add([value, other], bf16)
+    got = exchange([value] * 4, NEAR)
+    item_grad = pass2(own, us, infos, poss, SPLIT[1], items, item_grad)
     user_grad, loss = finish(infos[0], got, rows)
     return loss.reshape(rows), user_grad, item_grad
 

time: 100 us -> 95.2 us (0.952)
  the two profiles are of different devices: /device:TPU:1 before, /device:TPU:0 now
where the time goes in v6:
time: 95.2 us; the launch traced here: 94.4 us
  Pallas kernels  40 us (42%)
  starting transfers between devices  29.6 us (31%)
  waiting for transfers between devices  24 us (25%)
    ppermute x19, waiting for transfers between devices, swap(): lax.ppermute(x, axis, [(i, i ^ (k if mask is None else mask)) for i in ra...  23.9 us
    ppermute x19, starting transfers between devices, swap(): lax.ppermute(x, axis, [(i, i ^ (k if mask is None else mask)) for i in ra...  18.9 us
    pallas_call x3, Pallas kernels, pass2(): pl.pallas_call(functools.partial(pass2_kernel, tile, start // tile, n), i...  17.7 us
    pallas_call x1, Pallas kernels, pass1(): pl.pallas_call(functools.partial(pass1_kernel, tile, rb), in_specs=[HBM,...  16.7 us
    all_to_all x1, starting transfers between devices, per_device(): every = lax.all_to_all(every, USER + ITEM, 0, 0, tiled=True)  10.8 us
    pallas_call x1, Pallas kernels, find_hits(): pl.pallas_call(hits_kernel, in_specs=[SMEM, VMEM, HBM], out_specs=[VMEM]...  4.23 us
  transfers between devices with their start and end apart: 20, of which 9 were waited for; matrix products, arithmetic and copies ran while one was open for 0% of the time, Pallas kernels for 41%

profile of v6, /device:TPU:0, one launch (start us, length us, event | category | flops | bytes accessed | tf_op | source)
XLA Modules:
  0.0 94.4 jit_solution(14691726777667461793)
XLA Ops:
  0.6 1.8 %collective-permute-start.14 = (bf16[1024,256]{1,0:T(8,128)(2,1)}, bf16[1024,256]{1,0:T(8,128)(2,1)}, u32[]{:S(2)}, u32[]{:S(2)}) collective-permute-start(bf16[1024,256]{1,0:T(8,128)(2,1)} %refs_0_.5), channel_id=1, source_target_pairs={{0,64},{32,96},{64,0},{96,32},{1,65},{33,97},{65,1},{97,33},{2,66}... | collective-permute-start | bytes 1572872 | tf_op jit(solution)/shard_map/ppermute | solution.py:323
  2.4 16.7 %pass1.1 = (bf16[256,256]{1,0:T(8,128)(2,1)S(1)}, bf16[256,256]{1,0:T(8,128)(2,1)S(1)}, bf16[256,256]{1,0:T(8,128)(2,1)S(1)}, bf16[256,256]{1,0:T(8,128)(2,1)S(1)}, f32[128,8,128]{2,1,0:T(8,128)}) custom-call(bf16[1024,256]{1,0:T(8,128)(2,1)} %refs_0_.5, bf16[8192,256]{1,0:T(8,128)(2,1)} %cat_ref.3), custom_call_target="tpu_custom_call" | custom-call | flops 8589934592 | bytes 4194304 | tf_op jit(solution)/shard_map/pass1/pallas_call | solution.py:113
  19.1 10.8 %all-to-all-start = ((f32[128,8,128]{2,1,0:T(8,128)}), f32[128,8,128]{2,1,0:T(8,128)S(1)}, u32[]{:S(2)}, u32[]{:S(2)}) async-start(f32[128,8,128]{2,1,0:T(8,128)} %get-tuple-element.20), calls=%async_computation | async-start | bytes 1048576 | tf_op jit(solution)/shard_map/all_to_all | solution.py:355
  29.9 1.0 %collective-permute-start = (bf16[256,256]{1,0:T(8,128)(2,1)S(1)}, bf16[256,256]{1,0:T(8,128)(2,1)S(1)}, u32[]{:S(2)}, u32[]{:S(2)}) collective-permute-start(bf16[256,256]{1,0:T(8,128)(2,1)S(1)} %get-tuple-element.22), channel_id=1, source_target_pairs={{0,1},{1,0},{2,3},{3,2},{4,5},{5,4},{6,7},{7,6},{8,9},{9,8},{10,11... | collective-permute-start | bytes 393224 | tf_op jit(solution)/shard_map/ppermute | solution.py:323
  30.9 1.6 %collective-permute-start.1 = (bf16[256,256]{1,0:T(8,128)(2,1)S(1)}, bf16[256,256]{1,0:T(8,128)(2,1)S(1)}, u32[]{:S(2)}, u32[]{:S(2)}) collective-permute-start(bf16[256,256]{1,0:T(8,128)(2,1)S(1)} %get-tuple-element.23), channel_id=1, source_target_pairs={{0,8},{1,9},{2,10},{3,11},{4,12},{5,13},{6,14},{7,15},{8,0},{9,1},... | collective-permute-start | bytes 393224 | tf_op jit(solution)/shard_map/ppermute | solution.py:323
  32.5 0.9 collective-permute-start.2
  33.5 4.2 %hits.1 = (bf16[272,256]{1,0:T(8,128)(2,1)S(1)}, bf16[272,256]{1,0:T(8,128)(2,1)S(1)}, bf16[272,256]{1,0:T(8,128)(2,1)S(1)}, bf16[272,256]{1,0:T(8,128)(2,1)S(1)}, bf16[2048,256]{1,0:T(8,128)(2,1)S(1)}) custom-call(s32[1024]{0:T(1024)S(1)} %copy-done.1, bf16[1024,256]{1,0:T(8,128)(2,1)S(1)} %copy-done, bf16[8192,256]{1,0:T(8,128)(2,1)} %cat_ref.3), custom_call_target="tpu_custom_call" | custom-call | flops 1073741824 | bytes 4194304 | tf_op jit(solution)/shard_map/hits/pallas_call | solution.py:190
  37.7 1.0 %collective-permute-start.3 = (bf16[272,256]{1,0:T(8,128)(2,1)S(1)}, bf16[272,256]{1,0:T(8,128)(2,1)S(1)}, u32[]{:S(2)}, u32[]{:S(2)}) collective-permute-start(bf16[272,256]{1,0:T(8,128)(2,1)S(1)} %get-tuple-element.26), channel_id=1, source_target_pairs={{0,1},{1,0},{2,3},{3,2},{4,5},{5,4},{6,7},{7,6},{8,9},{9,8},{10,11... | collective-permute-start | bytes 417800 | tf_op jit(solution)/shard_map/ppermute | solution.py:323
  38.7 1.4 %collective-permute-done.refs_1_ = bf16[256,256]{1,0:T(8,128)(2,1)S(1)} collective-permute-done((bf16[256,256]{1,0:T(8,128)(2,1)S(1)}, bf16[256,256]{1,0:T(8,128)(2,1)S(1)}, u32[]{:S(2)}, u32[]{:S(2)}) %collective-permute-start) | collective-permute-done | bytes 131104 | tf_op jit(solution)/shard_map/ppermute | solution.py:323
  40.1 1.6 %collective-permute-start.4 = (bf16[272,256]{1,0:T(8,128)(2,1)S(1)}, bf16[272,256]{1,0:T(8,128)(2,1)S(1)}, u32[]{:S(2)}, u32[]{:S(2)}) collective-permute-start(bf16[272,256]{1,0:T(8,128)(2,1)S(1)} %get-tuple-element.27), channel_id=1, source_target_pairs={{0,8},{1,9},{2,10},{3,11},{4,12},{5,13},{6,14},{7,15},{8,0},{9,1},... | collective-permute-start | bytes 417800 | tf_op jit(solution)/shard_map/ppermute | solution.py:323
  41.7 2.5 %collective-permute-done.1.refs_2_ = bf16[256,256]{1,0:T(8,128)(2,1)S(1)} collective-permute-done((bf16[256,256]{1,0:T(8,128)(2,1)S(1)}, bf16[256,256]{1,0:T(8,128)(2,1)S(1)}, u32[]{:S(2)}, u32[]{:S(2)}) %collective-permute-start.1) | collective-permute-done | bytes 131104 | tf_op jit(solution)/shard_map/ppermute | solution.py:323
  44.3 1.0 %collective-permute-start.5 = (bf16[272,256]{1,0:T(8,128)(2,1)S(1)}, bf16[272,256]{1,0:T(8,128)(2,1)S(1)}, u32[]{:S(2)}, u32[]{:S(2)}) collective-permute-start(bf16[272,256]{1,0:T(8,128)(2,1)S(1)} %get-tuple-element.28), channel_id=1, source_target_pairs={{0,9},{1,8},{2,11},{3,10},{4,13},{5,12},{6,15},{7,14},{8,1},{9,0},... | collective-permute-start | bytes 417800 | tf_op jit(solution)/shard_map/ppermute | solution.py:323
  45.3 0.5 collective-permute-start.15
  45.8 2.6 %collective-permute-done.4.refs_6_ = bf16[272,256]{1,0:T(8,128)(2,1)S(1)} collective-permute-done((bf16[272,256]{1,0:T(8,128)(2,1)S(1)}, bf16[272,256]{1,0:T(8,128)(2,1)S(1)}, u32[]{:S(2)}, u32[]{:S(2)}) %collective-permute-start.4) | collective-permute-done | bytes 139296 | tf_op jit(solution)/shard_map/ppermute | solution.py:323
  48.4 1.9 %collective-permute-done.5.refs_7_ = bf16[272,256]{1,0:T(8,128)(2,1)S(1)} collective-permute-done((bf16[272,256]{1,0:T(8,128)(2,1)S(1)}, bf16[272,256]{1,0:T(8,128)(2,1)S(1)}, u32[]{:S(2)}, u32[]{:S(2)}) %collective-permute-start.5) | collective-permute-done | bytes 139296 | tf_op jit(solution)/shard_map/ppermute | solution.py:323
  50.3 0.4 combine.1
  50.6 2.0 %collective-permute-start.6 = (bf16[272,256]{1,0:T(8,128)(2,1)S(1)}, bf16[272,256]{1,0:T(8,128)(2,1)S(1)}, u32[]{:S(2)}, u32[]{:S(2)}) collective-permute-start(bf16[272,256]{1,0:T(8,128)(2,1)S(1)} %get-tuple-element.30.refs_0_), channel_id=1, source_target_pairs={{0,3},{1,2},{2,1},{3,0},{4,7},{5,6},{6,5},{7,4},{8,11},{9,10},{10,... | collective-permute-start | bytes 417800 | tf_op jit(solution)/shard_map/ppermute | solution.py:323
  52.7 2.8 %collective-permute-start.7 = (bf16[272,256]{1,0:T(8,128)(2,1)S(1)}, bf16[272,256]{1,0:T(8,128)(2,1)S(1)}, u32[]{:S(2)}, u32[]{:S(2)}) collective-permute-start(bf16[272,256]{1,0:T(8,128)(2,1)S(1)} %get-tuple-element.30.refs_0_), channel_id=1, source_target_pairs={{0,24},{1,25},{2,26},{3,27},{4,28},{5,29},{6,30},{7,31},{8,16},{9,... | collective-permute-start | bytes 417800 | tf_op jit(solution)/shard_map/ppermute | solution.py:323
  55.4 1.2 %collective-permute-start.8 = (bf16[272,256]{1,0:T(8,128)(2,1)S(1)}, bf16[272,256]{1,0:T(8,128)(2,1)S(1)}, u32[]{:S(2)}, u32[]{:S(2)}) collective-permute-start(bf16[272,256]{1,0:T(8,128)(2,1)S(1)} %get-tuple-element.30.refs_0_), channel_id=1, source_target_pairs={{0,27},{1,26},{2,25},{3,24},{4,31},{5,30},{6,29},{7,28},{8,19},{9,... | collective-permute-start | bytes 417800 | tf_op jit(solution)/shard_map/ppermute | solution.py:323
  56.6 0.4 collective-permute-done.6.refs_1_
  57.0 2.1 %collective-permute-done.7.refs_2_ = bf16[272,256]{1,0:T(8,128)(2,1)S(1)} collective-permute-done((bf16[272,256]{1,0:T(8,128)(2,1)S(1)}, bf16[272,256]{1,0:T(8,128)(2,1)S(1)}, u32[]{:S(2)}, u32[]{:S(2)}) %collective-permute-start.7) | collective-permute-done | bytes 139296 | tf_op jit(solution)/shard_map/ppermute | solution.py:323
  59.1 4.7 %collective-permute-done.8.refs_3_ = bf16[272,256]{1,0:T(8,128)(2,1)S(1)} collective-permute-done((bf16[272,256]{1,0:T(8,128)(2,1)S(1)}, bf16[272,256]{1,0:T(8,128)(2,1)S(1)}, u32[]{:S(2)}, u32[]{:S(2)}) %collective-permute-start.8) | collective-permute-done | bytes 139296 | tf_op jit(solution)/shard_map/ppermute | solution.py:323
  63.9 2.0 %collective-permute-start.9 = (f32[272,256]{1,0:T(8,128)S(1)}, f32[272,256]{1,0:T(8,128)S(1)}, u32[]{:S(2)}, u32[]{:S(2)}) collective-permute-start(f32[272,256]{1,0:T(8,128)S(1)} %add.2.refs_0_), channel_id=1, source_target_pairs={{0,4},{1,5},{2,6},{3,7},{4,0},{5,1},{6,2},{7,3},{8,12},{9,13},{10,... | collective-permute-start | bytes 835592 | tf_op jit(solution)/shard_map/ppermute | solution.py:323
  65.9 0.6 collective-permute-start.17
  66.5 5.5 %collective-permute-done.9.refs_1_ = f32[272,256]{1,0:T(8,128)S(1)} collective-permute-done((f32[272,256]{1,0:T(8,128)S(1)}, f32[272,256]{1,0:T(8,128)S(1)}, u32[]{:S(2)}, u32[]{:S(2)}) %collective-permute-start.9) | collective-permute-done | bytes 278560 | tf_op jit(solution)/shard_map/ppermute | solution.py:323
  72.2 0.1 collective-permute-start.11
  72.3 2.8 %collective-permute-done.18.refs_11_ = s32[8,128]{1,0:T(8,128)S(1)} collective-permute-done((s32[8,128]{1,0:T(8,128)S(1)}, s32[8,128]{1,0:T(8,128)S(1)}, u32[]{:S(2)}, u32[]{:S(2)}) %collective-permute-start.18) | collective-permute-done | bytes 4128 | tf_op jit(solution)/shard_map/ppermute | solution.py:323
  75.1 0.6 collective-permute-start.12
  75.7 5.1 %pass2.3.refs_12_ = bf16[2048,256]{1,0:T(8,128)(2,1)} custom-call(bf16[2048,256]{1,0:T(8,128)(2,1)S(1)} %get-tuple-element.33.c_ref, bf16[1024,256]{1,0:T(8,128)(2,1)S(1)} %copy-done, bf16[1024,256]{1,0:T(8,128)(2,1)} %collective-permute-done.13.refs_1_, bf16[1024,256]{1,0:T(8,128)(2,1)} %collective-permute-done.14.refs_2_, ...), custom_call_target="tpu_custom_call" | custom-call | flops 2147483648 | bytes 2097152 | tf_op jit(solution)/shard_map/pass2/pallas_call | solution.py:305
  80.9 5.2 %pass2.4.refs_12_ = bf16[2048,256]{1,0:T(8,128)(2,1)} custom-call(bf16[2048,256]{1,0:T(8,128)(2,1)S(1)} %get-tuple-element.33.c_ref, bf16[1024,256]{1,0:T(8,128)(2,1)S(1)} %copy-done, bf16[1024,256]{1,0:T(8,128)(2,1)} %collective-permute-done.13.refs_1_, bf16[1024,256]{1,0:T(8,128)(2,1)} %collective-permute-done.14.refs_2_, ...), custom_call_target="tpu_custom_call", output_to_operand_aliasing={{}: (13, {})} | custom-call | flops 2147483648 | bytes 2097152 | tf_op jit(solution)/shard_map/pass2/pallas_call | solution.py:305
  86.0 7.4 %pass2.5 = bf16[2048,256]{1,0:T(8,128)(2,1)} custom-call(bf16[2048,256]{1,0:T(8,128)(2,1)S(1)} %get-tuple-element.33.c_ref, bf16[1024,256]{1,0:T(8,128)(2,1)S(1)} %copy-done, bf16[1024,256]{1,0:T(8,128)(2,1)} %collective-permute-done.13.refs_1_, bf16[1024,256]{1,0:T(8,128)(2,1)} %collective-permute-done.14.refs_2_, ...), custom_call_target="tpu_custom_call", output_to_operand_aliasing={{}: (13, {})} | custom-call | flops 4294967296 | bytes 2097152 | tf_op jit(solution)/shard_map/pass2/pallas_call | solution.py:305
  93.5 0.9 finish.1
  (21 shorter events, 0.2 us)
Async XLA Ops:
  0.6 32.8 %copy-start = (bf16[1024,256]{1,0:T(8,128)(2,1)S(1)}, bf16[1024,256]{1,0:T(8,128)(2,1)}, u32[]{:S(2)}) copy-start(bf16[1024,256]{1,0:T(8,128)(2,1)} %refs_0_.5) | copy-start | bytes 1572868
  0.6 32.8 %copy-start.1 = (s32[1024]{0:T(1024)S(1)}, s32[1024]{0:T(1024)}, u32[]{:S(2)}) copy-start(s32[1024]{0:T(1024)} %pos_ref.1) | copy-start | bytes 12292
  0.6 44.6 %collective-permute-start.14 = (bf16[1024,256]{1,0:T(8,128)(2,1)}, bf16[1024,256]{1,0:T(8,128)(2,1)}, u32[]{:S(2)}, u32[]{:S(2)}) collective-permute-start(bf16[1024,256]{1,0:T(8,128)(2,1)} %refs_0_.5), channel_id=1, source_target_pairs={{0,64},{32,96},{64,0},{96,32},{1,65},{33,97},{65,1},{97,33},{2,66}... | collective-permute-start | bytes 1572872 | tf_op jit(solution)/shard_map/ppermute | solution.py:323
  19.1 31.2 %all-to-all-start = ((f32[128,8,128]{2,1,0:T(8,128)}), f32[128,8,128]{2,1,0:T(8,128)S(1)}, u32[]{:S(2)}, u32[]{:S(2)}) async-start(f32[128,8,128]{2,1,0:T(8,128)} %get-tuple-element.20), calls=%async_computation | async-start | bytes 1048576 | tf_op jit(solution)/shard_map/all_to_all | solution.py:355
  29.9 10.3 %collective-permute-start = (bf16[256,256]{1,0:T(8,128)(2,1)S(1)}, bf16[256,256]{1,0:T(8,128)(2,1)S(1)}, u32[]{:S(2)}, u32[]{:S(2)}) collective-permute-start(bf16[256,256]{1,0:T(8,128)(2,1)S(1)} %get-tuple-element.22), channel_id=1, source_target_pairs={{0,1},{1,0},{2,3},{3,2},{4,5},{5,4},{6,7},{7,6},{8,9},{9,8},{10,11... | collective-permute-start | bytes 393224 | tf_op jit(solution)/shard_map/ppermute | solution.py:323
  30.9 13.4 %collective-permute-start.1 = (bf16[256,256]{1,0:T(8,128)(2,1)S(1)}, bf16[256,256]{1,0:T(8,128)(2,1)S(1)}, u32[]{:S(2)}, u32[]{:S(2)}) collective-permute-start(bf16[256,256]{1,0:T(8,128)(2,1)S(1)} %get-tuple-element.23), channel_id=1, source_target_pairs={{0,8},{1,9},{2,10},{3,11},{4,12},{5,13},{6,14},{7,15},{8,0},{9,1},... | collective-permute-start | bytes 393224 | tf_op jit(solution)/shard_map/ppermute | solution.py:323
  32.5 12.8 %collective-permute-start.2 = (bf16[256,256]{1,0:T(8,128)(2,1)S(1)}, bf16[256,256]{1,0:T(8,128)(2,1)S(1)}, u32[]{:S(2)}, u32[]{:S(2)}) collective-permute-start(bf16[256,256]{1,0:T(8,128)(2,1)S(1)} %get-tuple-element.24), channel_id=1, source_target_pairs={{0,9},{1,8},{2,11},{3,10},{4,13},{5,12},{6,15},{7,14},{8,1},{9,0},... | collective-permute-start | bytes 393224 | tf_op jit(solution)/shard_map/ppermute | solution.py:323
  37.7 8.1 %collective-permute-start.3 = (bf16[272,256]{1,0:T(8,128)(2,1)S(1)}, bf16[272,256]{1,0:T(8,128)(2,1)S(1)}, u32[]{:S(2)}, u32[]{:S(2)}) collective-permute-start(bf16[272,256]{1,0:T(8,128)(2,1)S(1)} %get-tuple-element.26), channel_id=1, source_target_pairs={{0,1},{1,0},{2,3},{3,2},{4,5},{5,4},{6,7},{7,6},{8,9},{9,8},{10,11... | collective-permute-start | bytes 417800 | tf_op jit(solution)/shard_map/ppermute | solution.py:323
  40.1 8.2 %collective-permute-start.4 = (bf16[272,256]{1,0:T(8,128)(2,1)S(1)}, bf16[272,256]{1,0:T(8,128)(2,1)S(1)}, u32[]{:S(2)}, u32[]{:S(2)}) collective-permute-start(bf16[272,256]{1,0:T(8,128)(2,1)S(1)} %get-tuple-element.27), channel_id=1, source_target_pairs={{0,8},{1,9},{2,10},{3,11},{4,12},{5,13},{6,14},{7,15},{8,0},{9,1},... | collective-permute-start | bytes 417800 | tf_op jit(solution)/shard_map/ppermute | solution.py:323
  44.3 6.0 %collective-permute-start.5 = (bf16[272,256]{1,0:T(8,128)(2,1)S(1)}, bf16[272,256]{1,0:T(8,128)(2,1)S(1)}, u32[]{:S(2)}, u32[]{:S(2)}) collective-permute-start(bf16[272,256]{1,0:T(8,128)(2,1)S(1)} %get-tuple-element.28), channel_id=1, source_target_pairs={{0,9},{1,8},{2,11},{3,10},{4,13},{5,12},{6,15},{7,14},{8,1},{9,0},... | collective-permute-start | bytes 417800 | tf_op jit(solution)/shard_map/ppermute | solution.py:323
  45.3 30.4 %collective-permute-start.13 = (bf16[1024,256]{1,0:T(8,128)(2,1)S(1)}, bf16[1024,256]{1,0:T(8,128)(2,1)}, u32[]{:S(2)}, u32[]{:S(2)}) collective-permute-start(bf16[1024,256]{1,0:T(8,128)(2,1)S(1)} %copy-done), channel_id=1, source_target_pairs={{0,32},{32,0},{64,96},{96,64},{1,33},{33,1},{65,97},{97,65},{2,34}... | collective-permute-start | bytes 1572872 | tf_op jit(solution)/shard_map/ppermute | solution.py:323
  45.3 30.4 %collective-permute-start.15 = (bf16[1024,256]{1,0:T(8,128)(2,1)}, bf16[1024,256]{1,0:T(8,128)(2,1)}, u32[]{:S(2)}, u32[]{:S(2)}) collective-permute-start(bf16[1024,256]{1,0:T(8,128)(2,1)} %collective-permute-done.14.refs_2_), channel_id=1, source_target_pairs={{0,32},{32,0},{64,96},{96,64},{1,33},{33,1},{65,97},{97,65},{2,34}... | collective-permute-start | bytes 1572872 | tf_op jit(solution)/shard_map/ppermute | solution.py:323
  50.6 6.3 %collective-permute-start.6 = (bf16[272,256]{1,0:T(8,128)(2,1)S(1)}, bf16[272,256]{1,0:T(8,128)(2,1)S(1)}, u32[]{:S(2)}, u32[]{:S(2)}) collective-permute-start(bf16[272,256]{1,0:T(8,128)(2,1)S(1)} %get-tuple-element.30.refs_0_), channel_id=1, source_target_pairs={{0,3},{1,2},{2,1},{3,0},{4,7},{5,6},{6,5},{7,4},{8,11},{9,10},{10,... | collective-permute-start | bytes 417800 | tf_op jit(solution)/shard_map/ppermute | solution.py:323
  52.7 6.4 %collective-permute-start.7 = (bf16[272,256]{1,0:T(8,128)(2,1)S(1)}, bf16[272,256]{1,0:T(8,128)(2,1)S(1)}, u32[]{:S(2)}, u32[]{:S(2)}) collective-permute-start(bf16[272,256]{1,0:T(8,128)(2,1)S(1)} %get-tuple-element.30.refs_0_), channel_id=1, source_target_pairs={{0,24},{1,25},{2,26},{3,27},{4,28},{5,29},{6,30},{7,31},{8,16},{9,... | collective-permute-start | bytes 417800 | tf_op jit(solution)/shard_map/ppermute | solution.py:323
  55.4 8.4 %collective-permute-start.8 = (bf16[272,256]{1,0:T(8,128)(2,1)S(1)}, bf16[272,256]{1,0:T(8,128)(2,1)S(1)}, u32[]{:S(2)}, u32[]{:S(2)}) collective-permute-start(bf16[272,256]{1,0:T(8,128)(2,1)S(1)} %get-tuple-element.30.refs_0_), channel_id=1, source_target_pairs={{0,27},{1,26},{2,25},{3,24},{4,31},{5,30},{6,29},{7,28},{8,19},{9,... | collective-permute-start | bytes 417800 | tf_op jit(solution)/shard_map/ppermute | solution.py:323
  63.9 8.2 %collective-permute-start.9 = (f32[272,256]{1,0:T(8,128)S(1)}, f32[272,256]{1,0:T(8,128)S(1)}, u32[]{:S(2)}, u32[]{:S(2)}) collective-permute-start(f32[272,256]{1,0:T(8,128)S(1)} %add.2.refs_0_), channel_id=1, source_target_pairs={{0,4},{1,5},{2,6},{3,7},{4,0},{5,1},{6,2},{7,3},{8,12},{9,13},{10,... | collective-permute-start | bytes 835592 | tf_op jit(solution)/shard_map/ppermute | solution.py:323
  65.9 6.2 %collective-permute-start.16 = (s32[8,128]{1,0:T(8,128)S(1)}, s32[8,128]{1,0:T(8,128)S(1)}, u32[]{:S(2)}, u32[]{:S(2)}) collective-permute-start(s32[8,128]{1,0:T(8,128)S(1)} %bitcast.2), channel_id=1, source_target_pairs={{0,32},{32,0},{64,96},{96,64},{1,33},{33,1},{65,97},{97,65},{2,34}... | collective-permute-start | bytes 12296 | tf_op jit(solution)/shard_map/ppermute | solution.py:323
  65.9 6.3 %collective-permute-start.17 = (s32[8,128]{1,0:T(8,128)S(1)}, s32[8,128]{1,0:T(8,128)S(1)}, u32[]{:S(2)}, u32[]{:S(2)}) collective-permute-start(s32[8,128]{1,0:T(8,128)S(1)} %bitcast.3), channel_id=1, source_target_pairs={{0,64},{32,96},{64,0},{96,32},{1,65},{33,97},{65,1},{97,33},{2,66}... | collective-permute-start | bytes 12296 | tf_op jit(solution)/shard_map/ppermute | solution.py:323
  72.1 3.0 %collective-permute-start.18 = (s32[8,128]{1,0:T(8,128)S(1)}, s32[8,128]{1,0:T(8,128)S(1)}, u32[]{:S(2)}, u32[]{:S(2)}) collective-permute-start(s32[8,128]{1,0:T(8,128)S(1)} %bitcast.4), channel_id=1, source_target_pairs={{0,96},{32,64},{64,32},{96,0},{1,97},{33,65},{65,33},{97,1},{2,98}... | collective-permute-start | bytes 12296 | tf_op jit(solution)/shard_map/ppermute | solution.py:323
  72.1 21.4 %collective-permute-start.10 = (bf16[272,256]{1,0:T(8,128)(2,1)S(1)}, bf16[272,256]{1,0:T(8,128)(2,1)S(1)}, u32[]{:S(2)}, u32[]{:S(2)}) collective-permute-start(bf16[272,256]{1,0:T(8,128)(2,1)S(1)} %add.3.refs_0_), channel_id=1, source_target_pairs={{0,1},{1,0},{2,3},{3,2},{4,5},{5,4},{6,7},{7,6},{8,9},{9,8},{10,11... | collective-permute-start | bytes 417800 | tf_op jit(solution)/shard_map/ppermute | solution.py:323
  72.2 21.3 %collective-permute-start.11 = (bf16[272,256]{1,0:T(8,128)(2,1)S(1)}, bf16[272,256]{1,0:T(8,128)(2,1)S(1)}, u32[]{:S(2)}, u32[]{:S(2)}) collective-permute-start(bf16[272,256]{1,0:T(8,128)(2,1)S(1)} %add.3.refs_0_), channel_id=1, source_target_pairs={{0,8},{1,9},{2,10},{3,11},{4,12},{5,13},{6,14},{7,15},{8,0},{9,1},... | collective-permute-start | bytes 417800 | tf_op jit(solution)/shard_map/ppermute | solution.py:323
  75.1 18.4 %collective-permute-start.12 = (bf16[272,256]{1,0:T(8,128)(2,1)S(1)}, bf16[272,256]{1,0:T(8,128)(2,1)S(1)}, u32[]{:S(2)}, u32[]{:S(2)}) collective-permute-start(bf16[272,256]{1,0:T(8,128)(2,1)S(1)} %add.3.refs_0_), channel_id=1, source_target_pairs={{0,9},{1,8},{2,11},{3,10},{4,13},{5,12},{6,15},{7,14},{8,1},{9,0},... | collective-permute-start | bytes 417800 | tf_op jit(solution)/shard_map/ppermute | solution.py:323

commit v7 on v6

--- a/solution.py
+++ b/solution.py
@@ -23,14 +23,14 @@
 MIB = 1 << 20
 
 
-NEAR = (0, 1, 8, 9)
-REST = (0, 3, 24, 27)
+NEAR = (0, 8, 1, 9)
+REST = (0, 24, 3, 27)
 ACROSS = 4
 
 
 def chunk_id():
     x, z = lax.axis_index("x"), lax.axis_index("z")
-    return ((x ^ (x >> 1)) & 1) + 2 * ((z ^ (z >> 1)) & 1)
+    return ((z ^ (z >> 1)) & 1) + 2 * ((x ^ (x >> 1)) & 1)
 
 
 def exp_of(x):

time: 95.2 us -> 96.7 us (1.016)
  waiting for transfers between devices: 24 us -> 25.4 us
    ppermute x19, waiting for transfers between devices: 23.9 us -> 25.4 us  [swap(): lax.ppermute(x, axis, [(i, i ^ (k if mask is None else mask)) for i in ra...]
  transfers between devices with their start and end apart: 20 -> 20, of which waited for: 9 -> 8; matrix products, arithmetic and copies ran while one was open for 0% -> 0% of each run, Pallas kernels for 41% -> 41%
where the time goes in v7:
time: 96.7 us; the launch traced here: 95.7 us
  Pallas kernels  40 us (41%)
  starting transfers between devices  29.5 us (31%)
  waiting for transfers between devices  25.4 us (26%)
    ppermute x19, waiting for transfers between devices, swap(): lax.ppermute(x, axis, [(i, i ^ (k if mask is None else mask)) for i in ra...  25.4 us
    ppermute x19, starting transfers between devices, swap(): lax.ppermute(x, axis, [(i, i ^ (k if mask is None else mask)) for i in ra...  18.8 us
    pallas_call x3, Pallas kernels, pass2(): pl.pallas_call(functools.partial(pass2_kernel, tile, start // tile, n), i...  17.7 us
    pallas_call x1, Pallas kernels, pass1(): pl.pallas_call(functools.partial(pass1_kernel, tile, rb), in_specs=[HBM,...  16.7 us
    all_to_all x1, starting transfers between devices, per_device(): every = lax.all_to_all(every, USER + ITEM, 0, 0, tiled=True)  10.8 us
    pallas_call x1, Pallas kernels, find_hits(): pl.pallas_call(hits_kernel, in_specs=[SMEM, VMEM, HBM], out_specs=[VMEM]...  4.23 us
  transfers between devices with their start and end apart: 20, of which 8 were waited for; matrix products, arithmetic and copies ran while one was open for 0% of the time, Pallas kernels for 41%

profile of v7, /device:TPU:0, one launch (start us, length us, event | category | flops | bytes accessed | tf_op | source)
XLA Modules:
  0.0 95.7 jit_solution(15923349665947554889)
XLA Ops:
  0.6 1.8 %collective-permute-start.14 = (bf16[1024,256]{1,0:T(8,128)(2,1)}, bf16[1024,256]{1,0:T(8,128)(2,1)}, u32[]{:S(2)}, u32[]{:S(2)}) collective-permute-start(bf16[1024,256]{1,0:T(8,128)(2,1)} %refs_0_.5), channel_id=1, source_target_pairs={{0,64},{32,96},{64,0},{96,32},{1,65},{33,97},{65,1},{97,33},{2,66}... | collective-permute-start | bytes 1572872 | tf_op jit(solution)/shard_map/ppermute | solution.py:323
  2.4 16.7 %pass1.1 = (bf16[256,256]{1,0:T(8,128)(2,1)S(1)}, bf16[256,256]{1,0:T(8,128)(2,1)S(1)}, bf16[256,256]{1,0:T(8,128)(2,1)S(1)}, bf16[256,256]{1,0:T(8,128)(2,1)S(1)}, f32[128,8,128]{2,1,0:T(8,128)}) custom-call(bf16[1024,256]{1,0:T(8,128)(2,1)} %refs_0_.5, bf16[8192,256]{1,0:T(8,128)(2,1)} %cat_ref.3), custom_call_target="tpu_custom_call" | custom-call | flops 8589934592 | bytes 4194304 | tf_op jit(solution)/shard_map/pass1/pallas_call | solution.py:113
  19.1 10.8 %all-to-all-start = ((f32[128,8,128]{2,1,0:T(8,128)}), f32[128,8,128]{2,1,0:T(8,128)S(1)}, u32[]{:S(2)}, u32[]{:S(2)}) async-start(f32[128,8,128]{2,1,0:T(8,128)} %get-tuple-element.20), calls=%async_computation | async-start | bytes 1048576 | tf_op jit(solution)/shard_map/all_to_all | solution.py:355
  29.9 1.2 %collective-permute-start = (bf16[256,256]{1,0:T(8,128)(2,1)S(1)}, bf16[256,256]{1,0:T(8,128)(2,1)S(1)}, u32[]{:S(2)}, u32[]{:S(2)}) collective-permute-start(bf16[256,256]{1,0:T(8,128)(2,1)S(1)} %get-tuple-element.22), channel_id=1, source_target_pairs={{0,8},{1,9},{2,10},{3,11},{4,12},{5,13},{6,14},{7,15},{8,0},{9,1},... | collective-permute-start | bytes 393224 | tf_op jit(solution)/shard_map/ppermute | solution.py:323
  31.0 1.5 %collective-permute-start.1 = (bf16[256,256]{1,0:T(8,128)(2,1)S(1)}, bf16[256,256]{1,0:T(8,128)(2,1)S(1)}, u32[]{:S(2)}, u32[]{:S(2)}) collective-permute-start(bf16[256,256]{1,0:T(8,128)(2,1)S(1)} %get-tuple-element.23), channel_id=1, source_target_pairs={{0,1},{1,0},{2,3},{3,2},{4,5},{5,4},{6,7},{7,6},{8,9},{9,8},{10,11... | collective-permute-start | bytes 393224 | tf_op jit(solution)/shard_map/ppermute | solution.py:323
  32.5 0.9 collective-permute-start.2
  33.5 4.2 %hits.1 = (bf16[272,256]{1,0:T(8,128)(2,1)S(1)}, bf16[272,256]{1,0:T(8,128)(2,1)S(1)}, bf16[272,256]{1,0:T(8,128)(2,1)S(1)}, bf16[272,256]{1,0:T(8,128)(2,1)S(1)}, bf16[2048,256]{1,0:T(8,128)(2,1)S(1)}) custom-call(s32[1024]{0:T(1024)S(1)} %copy-done.1, bf16[1024,256]{1,0:T(8,128)(2,1)S(1)} %copy-done, bf16[8192,256]{1,0:T(8,128)(2,1)} %cat_ref.3), custom_call_target="tpu_custom_call" | custom-call | flops 1073741824 | bytes 4194304 | tf_op jit(solution)/shard_map/hits/pallas_call | solution.py:190
  37.7 1.4 %collective-permute-start.3 = (bf16[272,256]{1,0:T(8,128)(2,1)S(1)}, bf16[272,256]{1,0:T(8,128)(2,1)S(1)}, u32[]{:S(2)}, u32[]{:S(2)}) collective-permute-start(bf16[272,256]{1,0:T(8,128)(2,1)S(1)} %get-tuple-element.26), channel_id=1, source_target_pairs={{0,8},{1,9},{2,10},{3,11},{4,12},{5,13},{6,14},{7,15},{8,0},{9,1},... | collective-permute-start | bytes 417800 | tf_op jit(solution)/shard_map/ppermute | solution.py:323
  39.0 4.5 %collective-permute-done.refs_1_ = bf16[256,256]{1,0:T(8,128)(2,1)S(1)} collective-permute-done((bf16[256,256]{1,0:T(8,128)(2,1)S(1)}, bf16[256,256]{1,0:T(8,128)(2,1)S(1)}, u32[]{:S(2)}, u32[]{:S(2)}) %collective-permute-start) | collective-permute-done | bytes 131104 | tf_op jit(solution)/shard_map/ppermute | solution.py:323
  43.5 1.3 %collective-permute-start.4 = (bf16[272,256]{1,0:T(8,128)(2,1)S(1)}, bf16[272,256]{1,0:T(8,128)(2,1)S(1)}, u32[]{:S(2)}, u32[]{:S(2)}) collective-permute-start(bf16[272,256]{1,0:T(8,128)(2,1)S(1)} %get-tuple-element.27), channel_id=1, source_target_pairs={{0,1},{1,0},{2,3},{3,2},{4,5},{5,4},{6,7},{7,6},{8,9},{9,8},{10,11... | collective-permute-start | bytes 417800 | tf_op jit(solution)/shard_map/ppermute | solution.py:323
  44.8 1.3 %collective-permute-start.5 = (bf16[272,256]{1,0:T(8,128)(2,1)S(1)}, bf16[272,256]{1,0:T(8,128)(2,1)S(1)}, u32[]{:S(2)}, u32[]{:S(2)}) collective-permute-start(bf16[272,256]{1,0:T(8,128)(2,1)S(1)} %get-tuple-element.28), channel_id=1, source_target_pairs={{0,9},{1,8},{2,11},{3,10},{4,13},{5,12},{6,15},{7,14},{8,1},{9,0},... | collective-permute-start | bytes 417800 | tf_op jit(solution)/shard_map/ppermute | solution.py:323
  46.1 0.5 collective-permute-start.15
  46.6 3.3 %collective-permute-done.4.refs_6_ = bf16[272,256]{1,0:T(8,128)(2,1)S(1)} collective-permute-done((bf16[272,256]{1,0:T(8,128)(2,1)S(1)}, bf16[272,256]{1,0:T(8,128)(2,1)S(1)}, u32[]{:S(2)}, u32[]{:S(2)}) %collective-permute-start.4) | collective-permute-done | bytes 139296 | tf_op jit(solution)/shard_map/ppermute | solution.py:323
  49.9 2.3 %collective-permute-done.5.refs_7_ = bf16[272,256]{1,0:T(8,128)(2,1)S(1)} collective-permute-done((bf16[272,256]{1,0:T(8,128)(2,1)S(1)}, bf16[272,256]{1,0:T(8,128)(2,1)S(1)}, u32[]{:S(2)}, u32[]{:S(2)}) %collective-permute-start.5) | collective-permute-done | bytes 139296 | tf_op jit(solution)/shard_map/ppermute | solution.py:323
  52.2 0.4 combine.1
  52.6 2.6 %collective-permute-start.6 = (bf16[272,256]{1,0:T(8,128)(2,1)S(1)}, bf16[272,256]{1,0:T(8,128)(2,1)S(1)}, u32[]{:S(2)}, u32[]{:S(2)}) collective-permute-start(bf16[272,256]{1,0:T(8,128)(2,1)S(1)} %get-tuple-element.30.refs_0_), channel_id=1, source_target_pairs={{0,24},{1,25},{2,26},{3,27},{4,28},{5,29},{6,30},{7,31},{8,16},{9,... | collective-permute-start | bytes 417800 | tf_op jit(solution)/shard_map/ppermute | solution.py:323
  55.2 1.5 %collective-permute-start.7 = (bf16[272,256]{1,0:T(8,128)(2,1)S(1)}, bf16[272,256]{1,0:T(8,128)(2,1)S(1)}, u32[]{:S(2)}, u32[]{:S(2)}) collective-permute-start(bf16[272,256]{1,0:T(8,128)(2,1)S(1)} %get-tuple-element.30.refs_0_), channel_id=1, source_target_pairs={{0,3},{1,2},{2,1},{3,0},{4,7},{5,6},{6,5},{7,4},{8,11},{9,10},{10,... | collective-permute-start | bytes 417800 | tf_op jit(solution)/shard_map/ppermute | solution.py:323
  56.7 1.9 %collective-permute-start.8 = (bf16[272,256]{1,0:T(8,128)(2,1)S(1)}, bf16[272,256]{1,0:T(8,128)(2,1)S(1)}, u32[]{:S(2)}, u32[]{:S(2)}) collective-permute-start(bf16[272,256]{1,0:T(8,128)(2,1)S(1)} %get-tuple-element.30.refs_0_), channel_id=1, source_target_pairs={{0,27},{1,26},{2,25},{3,24},{4,31},{5,30},{6,29},{7,28},{8,19},{9,... | collective-permute-start | bytes 417800 | tf_op jit(solution)/shard_map/ppermute | solution.py:323
  58.6 0.4 collective-permute-done.6.refs_1_
  59.0 3.9 %collective-permute-done.7.refs_2_ = bf16[272,256]{1,0:T(8,128)(2,1)S(1)} collective-permute-done((bf16[272,256]{1,0:T(8,128)(2,1)S(1)}, bf16[272,256]{1,0:T(8,128)(2,1)S(1)}, u32[]{:S(2)}, u32[]{:S(2)}) %collective-permute-start.7) | collective-permute-done | bytes 139296 | tf_op jit(solution)/shard_map/ppermute | solution.py:323
  62.8 2.3 %collective-permute-done.8.refs_3_ = bf16[272,256]{1,0:T(8,128)(2,1)S(1)} collective-permute-done((bf16[272,256]{1,0:T(8,128)(2,1)S(1)}, bf16[272,256]{1,0:T(8,128)(2,1)S(1)}, u32[]{:S(2)}, u32[]{:S(2)}) %collective-permute-start.8) | collective-permute-done | bytes 139296 | tf_op jit(solution)/shard_map/ppermute | solution.py:323
  65.1 0.1 add.2.refs_0_
  65.2 1.5 %collective-permute-start.9 = (f32[272,256]{1,0:T(8,128)S(1)}, f32[272,256]{1,0:T(8,128)S(1)}, u32[]{:S(2)}, u32[]{:S(2)}) collective-permute-start(f32[272,256]{1,0:T(8,128)S(1)} %add.2.refs_0_), channel_id=1, source_target_pairs={{0,4},{1,5},{2,6},{3,7},{4,0},{5,1},{6,2},{7,3},{8,12},{9,13},{10,... | collective-permute-start | bytes 835592 | tf_op jit(solution)/shard_map/ppermute | solution.py:323
  66.6 0.7 collective-permute-start.17
  67.3 6.0 %collective-permute-done.9.refs_1_ = f32[272,256]{1,0:T(8,128)S(1)} collective-permute-done((f32[272,256]{1,0:T(8,128)S(1)}, f32[272,256]{1,0:T(8,128)S(1)}, u32[]{:S(2)}, u32[]{:S(2)}) %collective-permute-start.9) | collective-permute-done | bytes 278560 | tf_op jit(solution)/shard_map/ppermute | solution.py:323
  73.4 0.3 collective-permute-start.10
  73.7 2.7 %collective-permute-done.18.refs_11_ = s32[8,128]{1,0:T(8,128)S(1)} collective-permute-done((s32[8,128]{1,0:T(8,128)S(1)}, s32[8,128]{1,0:T(8,128)S(1)}, u32[]{:S(2)}, u32[]{:S(2)}) %collective-permute-start.18) | collective-permute-done | bytes 4128 | tf_op jit(solution)/shard_map/ppermute | solution.py:323
  76.4 0.6 collective-permute-start.12
  77.0 5.1 %pass2.3.refs_12_ = bf16[2048,256]{1,0:T(8,128)(2,1)} custom-call(bf16[2048,256]{1,0:T(8,128)(2,1)S(1)} %get-tuple-element.33.c_ref, bf16[1024,256]{1,0:T(8,128)(2,1)S(1)} %copy-done, bf16[1024,256]{1,0:T(8,128)(2,1)} %collective-permute-done.13.refs_1_, bf16[1024,256]{1,0:T(8,128)(2,1)} %collective-permute-done.14.refs_2_, ...), custom_call_target="tpu_custom_call" | custom-call | flops 2147483648 | bytes 2097152 | tf_op jit(solution)/shard_map/pass2/pallas_call | solution.py:305
  82.2 5.2 %pass2.4.refs_12_ = bf16[2048,256]{1,0:T(8,128)(2,1)} custom-call(bf16[2048,256]{1,0:T(8,128)(2,1)S(1)} %get-tuple-element.33.c_ref, bf16[1024,256]{1,0:T(8,128)(2,1)S(1)} %copy-done, bf16[1024,256]{1,0:T(8,128)(2,1)} %collective-permute-done.13.refs_1_, bf16[1024,256]{1,0:T(8,128)(2,1)} %collective-permute-done.14.refs_2_, ...), custom_call_target="tpu_custom_call", output_to_operand_aliasing={{}: (13, {})} | custom-call | flops 2147483648 | bytes 2097152 | tf_op jit(solution)/shard_map/pass2/pallas_call | solution.py:305
  87.3 7.4 %pass2.5 = bf16[2048,256]{1,0:T(8,128)(2,1)} custom-call(bf16[2048,256]{1,0:T(8,128)(2,1)S(1)} %get-tuple-element.33.c_ref, bf16[1024,256]{1,0:T(8,128)(2,1)S(1)} %copy-done, bf16[1024,256]{1,0:T(8,128)(2,1)} %collective-permute-done.13.refs_1_, bf16[1024,256]{1,0:T(8,128)(2,1)} %collective-permute-done.14.refs_2_, ...), custom_call_target="tpu_custom_call", output_to_operand_aliasing={{}: (13, {})} | custom-call | flops 4294967296 | bytes 2097152 | tf_op jit(solution)/shard_map/pass2/pallas_call | solution.py:305
  94.8 0.8 finish.1
  (21 shorter events, 0.1 us)
Async XLA Ops:
  0.6 32.8 %copy-start = (bf16[1024,256]{1,0:T(8,128)(2,1)S(1)}, bf16[1024,256]{1,0:T(8,128)(2,1)}, u32[]{:S(2)}) copy-start(bf16[1024,256]{1,0:T(8,128)(2,1)} %refs_0_.5) | copy-start | bytes 1572868
  0.6 32.8 %copy-start.1 = (s32[1024]{0:T(1024)S(1)}, s32[1024]{0:T(1024)}, u32[]{:S(2)}) copy-start(s32[1024]{0:T(1024)} %pos_ref.1) | copy-start | bytes 12292
  0.6 45.5 %collective-permute-start.14 = (bf16[1024,256]{1,0:T(8,128)(2,1)}, bf16[1024,256]{1,0:T(8,128)(2,1)}, u32[]{:S(2)}, u32[]{:S(2)}) collective-permute-start(bf16[1024,256]{1,0:T(8,128)(2,1)} %refs_0_.5), channel_id=1, source_target_pairs={{0,64},{32,96},{64,0},{96,32},{1,65},{33,97},{65,1},{97,33},{2,66}... | collective-permute-start | bytes 1572872 | tf_op jit(solution)/shard_map/ppermute | solution.py:323
  19.1 33.1 %all-to-all-start = ((f32[128,8,128]{2,1,0:T(8,128)}), f32[128,8,128]{2,1,0:T(8,128)S(1)}, u32[]{:S(2)}, u32[]{:S(2)}) async-start(f32[128,8,128]{2,1,0:T(8,128)} %get-tuple-element.20), calls=%async_computation | async-start | bytes 1048576 | tf_op jit(solution)/shard_map/all_to_all | solution.py:355
  29.9 13.6 %collective-permute-start = (bf16[256,256]{1,0:T(8,128)(2,1)S(1)}, bf16[256,256]{1,0:T(8,128)(2,1)S(1)}, u32[]{:S(2)}, u32[]{:S(2)}) collective-permute-start(bf16[256,256]{1,0:T(8,128)(2,1)S(1)} %get-tuple-element.22), channel_id=1, source_target_pairs={{0,8},{1,9},{2,10},{3,11},{4,12},{5,13},{6,14},{7,15},{8,0},{9,1},... | collective-permute-start | bytes 393224 | tf_op jit(solution)/shard_map/ppermute | solution.py:323
  31.0 13.8 %collective-permute-start.1 = (bf16[256,256]{1,0:T(8,128)(2,1)S(1)}, bf16[256,256]{1,0:T(8,128)(2,1)S(1)}, u32[]{:S(2)}, u32[]{:S(2)}) collective-permute-start(bf16[256,256]{1,0:T(8,128)(2,1)S(1)} %get-tuple-element.23), channel_id=1, source_target_pairs={{0,1},{1,0},{2,3},{3,2},{4,5},{5,4},{6,7},{7,6},{8,9},{9,8},{10,11... | collective-permute-start | bytes 393224 | tf_op jit(solution)/shard_map/ppermute | solution.py:323
  32.5 13.6 %collective-permute-start.2 = (bf16[256,256]{1,0:T(8,128)(2,1)S(1)}, bf16[256,256]{1,0:T(8,128)(2,1)S(1)}, u32[]{:S(2)}, u32[]{:S(2)}) collective-permute-start(bf16[256,256]{1,0:T(8,128)(2,1)S(1)} %get-tuple-element.24), channel_id=1, source_target_pairs={{0,9},{1,8},{2,11},{3,10},{4,13},{5,12},{6,15},{7,14},{8,1},{9,0},... | collective-permute-start | bytes 393224 | tf_op jit(solution)/shard_map/ppermute | solution.py:323
  37.7 8.9 %collective-permute-start.3 = (bf16[272,256]{1,0:T(8,128)(2,1)S(1)}, bf16[272,256]{1,0:T(8,128)(2,1)S(1)}, u32[]{:S(2)}, u32[]{:S(2)}) collective-permute-start(bf16[272,256]{1,0:T(8,128)(2,1)S(1)} %get-tuple-element.26), channel_id=1, source_target_pairs={{0,8},{1,9},{2,10},{3,11},{4,12},{5,13},{6,14},{7,15},{8,0},{9,1},... | collective-permute-start | bytes 417800 | tf_op jit(solution)/shard_map/ppermute | solution.py:323
  43.5 6.4 %collective-permute-start.4 = (bf16[272,256]{1,0:T(8,128)(2,1)S(1)}, bf16[272,256]{1,0:T(8,128)(2,1)S(1)}, u32[]{:S(2)}, u32[]{:S(2)}) collective-permute-start(bf16[272,256]{1,0:T(8,128)(2,1)S(1)} %get-tuple-element.27), channel_id=1, source_target_pairs={{0,1},{1,0},{2,3},{3,2},{4,5},{5,4},{6,7},{7,6},{8,9},{9,8},{10,11... | collective-permute-start | bytes 417800 | tf_op jit(solution)/shard_map/ppermute | solution.py:323
  44.8 7.4 %collective-permute-start.5 = (bf16[272,256]{1,0:T(8,128)(2,1)S(1)}, bf16[272,256]{1,0:T(8,128)(2,1)S(1)}, u32[]{:S(2)}, u32[]{:S(2)}) collective-permute-start(bf16[272,256]{1,0:T(8,128)(2,1)S(1)} %get-tuple-element.28), channel_id=1, source_target_pairs={{0,9},{1,8},{2,11},{3,10},{4,13},{5,12},{6,15},{7,14},{8,1},{9,0},... | collective-permute-start | bytes 417800 | tf_op jit(solution)/shard_map/ppermute | solution.py:323
  46.1 30.9 %collective-permute-start.13 = (bf16[1024,256]{1,0:T(8,128)(2,1)S(1)}, bf16[1024,256]{1,0:T(8,128)(2,1)}, u32[]{:S(2)}, u32[]{:S(2)}) collective-permute-start(bf16[1024,256]{1,0:T(8,128)(2,1)S(1)} %copy-done), channel_id=1, source_target_pairs={{0,32},{32,0},{64,96},{96,64},{1,33},{33,1},{65,97},{97,65},{2,34}... | collective-permute-start | bytes 1572872 | tf_op jit(solution)/shard_map/ppermute | solution.py:323
  46.1 30.9 %collective-permute-start.15 = (bf16[1024,256]{1,0:T(8,128)(2,1)}, bf16[1024,256]{1,0:T(8,128)(2,1)}, u32[]{:S(2)}, u32[]{:S(2)}) collective-permute-start(bf16[1024,256]{1,0:T(8,128)(2,1)} %collective-permute-done.14.refs_2_), channel_id=1, source_target_pairs={{0,32},{32,0},{64,96},{96,64},{1,33},{33,1},{65,97},{97,65},{2,34}... | collective-permute-start | bytes 1572872 | tf_op jit(solution)/shard_map/ppermute | solution.py:323
  52.6 6.3 %collective-permute-start.6 = (bf16[272,256]{1,0:T(8,128)(2,1)S(1)}, bf16[272,256]{1,0:T(8,128)(2,1)S(1)}, u32[]{:S(2)}, u32[]{:S(2)}) collective-permute-start(bf16[272,256]{1,0:T(8,128)(2,1)S(1)} %get-tuple-element.30.refs_0_), channel_id=1, source_target_pairs={{0,24},{1,25},{2,26},{3,27},{4,28},{5,29},{6,30},{7,31},{8,16},{9,... | collective-permute-start | bytes 417800 | tf_op jit(solution)/shard_map/ppermute | solution.py:323
  55.2 7.6 %collective-permute-start.7 = (bf16[272,256]{1,0:T(8,128)(2,1)S(1)}, bf16[272,256]{1,0:T(8,128)(2,1)S(1)}, u32[]{:S(2)}, u32[]{:S(2)}) collective-permute-start(bf16[272,256]{1,0:T(8,128)(2,1)S(1)} %get-tuple-element.30.refs_0_), channel_id=1, source_target_pairs={{0,3},{1,2},{2,1},{3,0},{4,7},{5,6},{6,5},{7,4},{8,11},{9,10},{10,... | collective-permute-start | bytes 417800 | tf_op jit(solution)/shard_map/ppermute | solution.py:323
  56.7 8.4 %collective-permute-start.8 = (bf16[272,256]{1,0:T(8,128)(2,1)S(1)}, bf16[272,256]{1,0:T(8,128)(2,1)S(1)}, u32[]{:S(2)}, u32[]{:S(2)}) collective-permute-start(bf16[272,256]{1,0:T(8,128)(2,1)S(1)} %get-tuple-element.30.refs_0_), channel_id=1, source_target_pairs={{0,27},{1,26},{2,25},{3,24},{4,31},{5,30},{6,29},{7,28},{8,19},{9,... | collective-permute-start | bytes 417800 | tf_op jit(solution)/shard_map/ppermute | solution.py:323
  65.2 8.2 %collective-permute-start.9 = (f32[272,256]{1,0:T(8,128)S(1)}, f32[272,256]{1,0:T(8,128)S(1)}, u32[]{:S(2)}, u32[]{:S(2)}) collective-permute-start(f32[272,256]{1,0:T(8,128)S(1)} %add.2.refs_0_), channel_id=1, source_target_pairs={{0,4},{1,5},{2,6},{3,7},{4,0},{5,1},{6,2},{7,3},{8,12},{9,13},{10,... | collective-permute-start | bytes 835592 | tf_op jit(solution)/shard_map/ppermute | solution.py:323
  66.6 6.8 %collective-permute-start.16 = (s32[8,128]{1,0:T(8,128)S(1)}, s32[8,128]{1,0:T(8,128)S(1)}, u32[]{:S(2)}, u32[]{:S(2)}) collective-permute-start(s32[8,128]{1,0:T(8,128)S(1)} %bitcast.2), channel_id=1, source_target_pairs={{0,32},{32,0},{64,96},{96,64},{1,33},{33,1},{65,97},{97,65},{2,34}... | collective-permute-start | bytes 12296 | tf_op jit(solution)/shard_map/ppermute | solution.py:323
  66.6 7.1 %collective-permute-start.17 = (s32[8,128]{1,0:T(8,128)S(1)}, s32[8,128]{1,0:T(8,128)S(1)}, u32[]{:S(2)}, u32[]{:S(2)}) collective-permute-start(s32[8,128]{1,0:T(8,128)S(1)} %bitcast.3), channel_id=1, source_target_pairs={{0,64},{32,96},{64,0},{96,32},{1,65},{33,97},{65,1},{97,33},{2,66}... | collective-permute-start | bytes 12296 | tf_op jit(solution)/shard_map/ppermute | solution.py:323
  73.4 3.0 %collective-permute-start.18 = (s32[8,128]{1,0:T(8,128)S(1)}, s32[8,128]{1,0:T(8,128)S(1)}, u32[]{:S(2)}, u32[]{:S(2)}) collective-permute-start(s32[8,128]{1,0:T(8,128)S(1)} %bitcast.4), channel_id=1, source_target_pairs={{0,96},{32,64},{64,32},{96,0},{1,97},{33,65},{65,33},{97,1},{2,98}... | collective-permute-start | bytes 12296 | tf_op jit(solution)/shard_map/ppermute | solution.py:323
  73.4 21.4 %collective-permute-start.10 = (bf16[272,256]{1,0:T(8,128)(2,1)S(1)}, bf16[272,256]{1,0:T(8,128)(2,1)S(1)}, u32[]{:S(2)}, u32[]{:S(2)}) collective-permute-start(bf16[272,256]{1,0:T(8,128)(2,1)S(1)} %add.3.refs_0_), channel_id=1, source_target_pairs={{0,8},{1,9},{2,10},{3,11},{4,12},{5,13},{6,14},{7,15},{8,0},{9,1},... | collective-permute-start | bytes 417800 | tf_op jit(solution)/shard_map/ppermute | solution.py:323
  73.7 21.1 %collective-permute-start.11 = (bf16[272,256]{1,0:T(8,128)(2,1)S(1)}, bf16[272,256]{1,0:T(8,128)(2,1)S(1)}, u32[]{:S(2)}, u32[]{:S(2)}) collective-permute-start(bf16[272,256]{1,0:T(8,128)(2,1)S(1)} %add.3.refs_0_), channel_id=1, source_target_pairs={{0,1},{1,0},{2,3},{3,2},{4,5},{5,4},{6,7},{7,6},{8,9},{9,8},{10,11... | collective-permute-start | bytes 417800 | tf_op jit(solution)/shard_map/ppermute | solution.py:323
  76.4 18.4 %collective-permute-start.12 = (bf16[272,256]{1,0:T(8,128)(2,1)S(1)}, bf16[272,256]{1,0:T(8,128)(2,1)S(1)}, u32[]{:S(2)}, u32[]{:S(2)}) collective-permute-start(bf16[272,256]{1,0:T(8,128)(2,1)S(1)} %add.3.refs_0_), channel_id=1, source_target_pairs={{0,9},{1,8},{2,11},{3,10},{4,13},{5,12},{6,15},{7,14},{8,1},{9,0},... | collective-permute-start | bytes 417800 | tf_op jit(solution)/shard_map/ppermute | solution.py:323

commit v8 on v7

--- a/solution.py
+++ b/solution.py
@@ -134,16 +134,12 @@
 
 
 def hits_kernel(pos_ref, u_ref, cat_ref, *refs):
-    out_refs, own_ref, (hit_ref, sp_ref, c_ref, found_ref, sem) = refs[:4], refs[4], refs[5:]
-    items = own_ref.shape[0]
+    out_refs, (hit_ref, sp_ref, c_ref, found_ref, sem) = refs[:4], refs[4:]
     rows, width = u_ref.shape
     count = cat_ref.shape[0]
     x, shard = chunk_id(), lax.axis_index(ITEM)
-    whole_copy = pltpu.make_async_copy(cat_ref, c_ref, sem.at[0])
+    whole_copy = pltpu.make_async_copy(cat_ref, c_ref, sem)
     whole_copy.start()
-    mine = pl.ds(pl.multiple_of(lax.axis_index(USER) * items, items), items)
-    own_copy = pltpu.make_async_copy(cat_ref.at[mine], own_ref, sem.at[1])
-    own_copy.start()
     hit_ref[...] = jnp.zeros_like(hit_ref)
     base = shard * count
     bits = count.bit_length() - 1
@@ -181,7 +177,6 @@
             terms.append(term)
         terms.append(jnp.zeros((13, width), f32))
         out_ref[chunk:] = jnp.concatenate(terms, axis=0).astype(bf16)
-    own_copy.wait()
 
 
 def find_hits(positives, users, catalog):
@@ -190,14 +185,14 @@
     return pl.pallas_call(
         hits_kernel,
         in_specs=[SMEM, VMEM, HBM],
-        out_specs=[VMEM] * 5,
-        out_shape=[struct(rows // 4 + 16, width, dtype=bf16)] * 4 + [struct(count // 4, width, dtype=bf16)],
+        out_specs=[VMEM] * 4,
+        out_shape=[struct(rows // 4 + 16, width, dtype=bf16)] * 4,
         scratch_shapes=[
             pltpu.VMEM((rows, width), f32),
             pltpu.VMEM((rows // 128, 128), f32),
             pltpu.VMEM((count, width), bf16),
             pltpu.SMEM((rows,), jnp.int32),
-            pltpu.SemaphoreType.DMA((2,)),
+            pltpu.SemaphoreType.DMA(()),
         ],
         cost_estimate=pl.CostEstimate(
             flops=rows * count * width // 2, bytes_accessed=2 * count * width, transcendentals=0
@@ -319,6 +314,29 @@
     )(*args)
 
 
+def hold_kernel(u0, u1, u2, cat_ref, v0, v1, v2, own_ref, sem):
+    items = own_ref.shape[0]
+    mine = pl.ds(pl.multiple_of(lax.axis_index(USER) * items, items), items)
+    own_copy = pltpu.make_async_copy(cat_ref.at[mine], own_ref, sem)
+    own_copy.start()
+    for u_ref, v_ref in ((u0, v0), (u1, v1), (u2, v2)):
+        v_ref[...] = u_ref[...]
+    own_copy.wait()
+
+
+def hold(us, catalog):
+    count, width = catalog.shape
+    return pl.pallas_call(
+        hold_kernel,
+        in_specs=[VMEM] * 3 + [HBM],
+        out_specs=[VMEM] * 4,
+        out_shape=[struct(*u.shape, dtype=u.dtype) for u in us] + [struct(count // 4, width, dtype=bf16)],
+        scratch_shapes=[pltpu.SemaphoreType.DMA(())],
+        compiler_params=pltpu.CompilerParams(vmem_limit_bytes=6 * MIB),
+        name="hold",
+    )(*us, far(catalog))
+
+
 def swap(x, axis, size, k, mask=None):
     return lax.ppermute(x, axis, [(i, i ^ (k if mask is None else mask)) for i in range(size)])
 
@@ -353,12 +371,14 @@
     poss = [pos] + [swap(pos, USER, 4, k) for k in (1, 2, 3)]
     *pieces, every = pass1(users, catalog)
     every = lax.all_to_all(every, USER + ITEM, 0, 0, tiled=True)
-    *hits, own = find_hits(positives, users, catalog)
+    hits = find_hits(positives, users, catalog)
     pieces = exchange(pieces, NEAR)
     hits = exchange(hits, NEAR)
     *infos, value = combine(every, pieces, hits)
 
     a = exchange([value] * 4, REST)
+    *held, own = hold(us[1:], catalog)
+    us = [users, *held]
     item_grad = pass2(own, us, infos, poss, 0, SPLIT[0], None)
     value = add(a, f32)
     other = swap(value, ITEM, 32, 1, ACROSS)

time: 96.7 us -> 96.2 us (level)
  local copies, waits for them, and re-layouts: 0.01 us -> 3.12 us
  Pallas kernels: 40 us -> 37.3 us
  waiting for transfers between devices: 25.4 us -> 22.7 us
  starting transfers between devices: 29.5 us -> 31.9 us
    pallas_call x3, Pallas kernels: 17.7 us -> 13.9 us  [pass2(): pl.pallas_call(functools.partial(pass2_kernel, tile, start // tile, n), i...]
    unnamed x4 -> x12, local copies, waits for them, and re-layouts: 0.01 us -> 3.12 us
    ppermute x19, waiting for transfers between devices: 25.4 us -> 22.7 us  [swap(): lax.ppermute(x, axis, [(i, i ^ (k if mask is None else mask)) for i in ra...]
    ppermute x19, starting transfers between devices: 18.8 us -> 21.1 us  [swap(): lax.ppermute(x, axis, [(i, i ^ (k if mask is None else mask)) for i in ra...]
    pallas_call x0 -> x1, Pallas kernels: none -> 1.25 us  [hold(): pl.pallas_call(hold_kernel, in_specs=[VMEM] * 3 + [HBM], out_specs=[VMEM]...]
  transfers between devices with their start and end apart: 20 -> 20, of which waited for: 8 -> 7; matrix products, arithmetic and copies ran while one was open for 0% -> 0% of each run, Pallas kernels for 41% -> 38%
where the time goes in v8:
time: 96.2 us; the launch traced here: 95.8 us
  Pallas kernels  37.3 us (39%)
  starting transfers between devices  31.9 us (33%)
  waiting for transfers between devices  22.7 us (24%)
  local copies, waits for them, and re-layouts  3.12 us (3%)
    ppermute x19, waiting for transfers between devices, swap(): lax.ppermute(x, axis, [(i, i ^ (k if mask is None else mask)) for i in ra...  22.7 us
    ppermute x19, starting transfers between devices, swap(): lax.ppermute(x, axis, [(i, i ^ (k if mask is None else mask)) for i in ra...  21.1 us
    pallas_call x1, Pallas kernels, pass1(): pl.pallas_call(functools.partial(pass1_kernel, tile, rb), in_specs=[HBM,...  16.7 us
    pallas_call x3, Pallas kernels, pass2(): pl.pallas_call(functools.partial(pass2_kernel, tile, start // tile, n), i...  13.9 us
    all_to_all x1, starting transfers between devices, per_device(): every = lax.all_to_all(every, USER + ITEM, 0, 0, tiled=True)  10.8 us
    pallas_call x1, Pallas kernels, find_hits(): pl.pallas_call(hits_kernel, in_specs=[SMEM, VMEM, HBM], out_specs=[VMEM]...  4.22 us
    unnamed x12, local copies, waits for them, and re-layouts  3.12 us
  transfers between devices with their start and end apart: 20, of which 7 were waited for; matrix products, arithmetic and copies ran while one was open for 0% of the time, Pallas kernels for 38%

profile of v8, /device:TPU:0, one launch (start us, length us, event | category | flops | bytes accessed | tf_op | source)
XLA Modules:
  0.0 95.8 jit_solution(11776154930241752387)
XLA Ops:
  0.6 1.8 %collective-permute-start.14 = (bf16[1024,256]{1,0:T(8,128)(2,1)}, bf16[1024,256]{1,0:T(8,128)(2,1)S(1)}, u32[]{:S(2)}, u32[]{:S(2)}) collective-permute-start(bf16[1024,256]{1,0:T(8,128)(2,1)} %refs_0_.5), channel_id=1, source_target_pairs={{0,64},{32,96},{64,0},{96,32},{1,65},{33,97},{65,1},{97,33},{2,66}... | collective-permute-start | bytes 1572872 | tf_op jit(solution)/shard_map/ppermute | solution.py:341
  2.4 16.7 %pass1.1 = (bf16[256,256]{1,0:T(8,128)(2,1)S(1)}, bf16[256,256]{1,0:T(8,128)(2,1)S(1)}, bf16[256,256]{1,0:T(8,128)(2,1)S(1)}, bf16[256,256]{1,0:T(8,128)(2,1)S(1)}, f32[128,8,128]{2,1,0:T(8,128)}) custom-call(bf16[1024,256]{1,0:T(8,128)(2,1)} %refs_0_.5, bf16[8192,256]{1,0:T(8,128)(2,1)} %cat_ref.5), custom_call_target="tpu_custom_call" | custom-call | flops 8589934592 | bytes 4194304 | tf_op jit(solution)/shard_map/pass1/pallas_call | solution.py:113
  19.1 10.8 %all-to-all-start = ((f32[128,8,128]{2,1,0:T(8,128)}), f32[128,8,128]{2,1,0:T(8,128)S(1)}, u32[]{:S(2)}, u32[]{:S(2)}) async-start(f32[128,8,128]{2,1,0:T(8,128)} %get-tuple-element.23), calls=%async_computation | async-start | bytes 1048576 | tf_op jit(solution)/shard_map/all_to_all | solution.py:373
  29.9 1.2 %collective-permute-start = (bf16[256,256]{1,0:T(8,128)(2,1)S(1)}, bf16[256,256]{1,0:T(8,128)(2,1)S(1)}, u32[]{:S(2)}, u32[]{:S(2)}) collective-permute-start(bf16[256,256]{1,0:T(8,128)(2,1)S(1)} %get-tuple-element.25), channel_id=1, source_target_pairs={{0,8},{1,9},{2,10},{3,11},{4,12},{5,13},{6,14},{7,15},{8,0},{9,1},... | collective-permute-start | bytes 393224 | tf_op jit(solution)/shard_map/ppermute | solution.py:341
  31.0 1.5 %collective-permute-start.1 = (bf16[256,256]{1,0:T(8,128)(2,1)S(1)}, bf16[256,256]{1,0:T(8,128)(2,1)S(1)}, u32[]{:S(2)}, u32[]{:S(2)}) collective-permute-start(bf16[256,256]{1,0:T(8,128)(2,1)S(1)} %get-tuple-element.26), channel_id=1, source_target_pairs={{0,1},{1,0},{2,3},{3,2},{4,5},{5,4},{6,7},{7,6},{8,9},{9,8},{10,11... | collective-permute-start | bytes 393224 | tf_op jit(solution)/shard_map/ppermute | solution.py:341
  32.5 0.9 collective-permute-start.2
  33.4 4.2 %hits.1 = (bf16[272,256]{1,0:T(8,128)(2,1)S(1)}, bf16[272,256]{1,0:T(8,128)(2,1)S(1)}, bf16[272,256]{1,0:T(8,128)(2,1)S(1)}, bf16[272,256]{1,0:T(8,128)(2,1)S(1)}) custom-call(s32[1024]{0:T(1024)S(1)} %copy-done.5, bf16[1024,256]{1,0:T(8,128)(2,1)S(1)} %copy-done, bf16[8192,256]{1,0:T(8,128)(2,1)} %cat_ref.5), custom_call_target="tpu_custom_call" | custom-call | flops 1073741824 | bytes 4194304 | tf_op jit(solution)/shard_map/hits/pallas_call | solution.py:185
  37.7 1.4 %collective-permute-start.3 = (bf16[272,256]{1,0:T(8,128)(2,1)S(1)}, bf16[272,256]{1,0:T(8,128)(2,1)S(1)}, u32[]{:S(2)}, u32[]{:S(2)}) collective-permute-start(bf16[272,256]{1,0:T(8,128)(2,1)S(1)} %get-tuple-element.29), channel_id=1, source_target_pairs={{0,8},{1,9},{2,10},{3,11},{4,12},{5,13},{6,14},{7,15},{8,0},{9,1},... | collective-permute-start | bytes 417800 | tf_op jit(solution)/shard_map/ppermute | solution.py:341
  39.0 4.5 %collective-permute-done.refs_1_ = bf16[256,256]{1,0:T(8,128)(2,1)S(1)} collective-permute-done((bf16[256,256]{1,0:T(8,128)(2,1)S(1)}, bf16[256,256]{1,0:T(8,128)(2,1)S(1)}, u32[]{:S(2)}, u32[]{:S(2)}) %collective-permute-start) | collective-permute-done | bytes 131104 | tf_op jit(solution)/shard_map/ppermute | solution.py:341
  43.5 1.3 %collective-permute-start.4 = (bf16[272,256]{1,0:T(8,128)(2,1)S(1)}, bf16[272,256]{1,0:T(8,128)(2,1)S(1)}, u32[]{:S(2)}, u32[]{:S(2)}) collective-permute-start(bf16[272,256]{1,0:T(8,128)(2,1)S(1)} %get-tuple-element.30), channel_id=1, source_target_pairs={{0,1},{1,0},{2,3},{3,2},{4,5},{5,4},{6,7},{7,6},{8,9},{9,8},{10,11... | collective-permute-start | bytes 417800 | tf_op jit(solution)/shard_map/ppermute | solution.py:341
  44.8 0.7 copy-done.1
  45.5 1.3 %collective-permute-start.5 = (bf16[272,256]{1,0:T(8,128)(2,1)S(1)}, bf16[272,256]{1,0:T(8,128)(2,1)S(1)}, u32[]{:S(2)}, u32[]{:S(2)}) collective-permute-start(bf16[272,256]{1,0:T(8,128)(2,1)S(1)} %get-tuple-element.31), channel_id=1, source_target_pairs={{0,9},{1,8},{2,11},{3,10},{4,13},{5,12},{6,15},{7,14},{8,1},{9,0},... | collective-permute-start | bytes 417800 | tf_op jit(solution)/shard_map/ppermute | solution.py:341
  46.7 0.7 copy-done.3
  47.4 0.5 collective-permute-start.15
  47.9 1.3 %collective-permute-done.4.refs_6_ = bf16[272,256]{1,0:T(8,128)(2,1)S(1)} collective-permute-done((bf16[272,256]{1,0:T(8,128)(2,1)S(1)}, bf16[272,256]{1,0:T(8,128)(2,1)S(1)}, u32[]{:S(2)}, u32[]{:S(2)}) %collective-permute-start.4) | collective-permute-done | bytes 139296 | tf_op jit(solution)/shard_map/ppermute | solution.py:341
  49.2 3.0 %collective-permute-done.5.refs_7_ = bf16[272,256]{1,0:T(8,128)(2,1)S(1)} collective-permute-done((bf16[272,256]{1,0:T(8,128)(2,1)S(1)}, bf16[272,256]{1,0:T(8,128)(2,1)S(1)}, u32[]{:S(2)}, u32[]{:S(2)}) %collective-permute-start.5) | collective-permute-done | bytes 139296 | tf_op jit(solution)/shard_map/ppermute | solution.py:341
  52.2 0.9 copy-done.2
  53.1 0.9 copy-done.4
  54.4 2.6 %collective-permute-start.6 = (bf16[272,256]{1,0:T(8,128)(2,1)S(1)}, bf16[272,256]{1,0:T(8,128)(2,1)S(1)}, u32[]{:S(2)}, u32[]{:S(2)}) collective-permute-start(bf16[272,256]{1,0:T(8,128)(2,1)S(1)} %get-tuple-element.33.refs_0_), channel_id=1, source_target_pairs={{0,24},{1,25},{2,26},{3,27},{4,28},{5,29},{6,30},{7,31},{8,16},{9,... | collective-permute-start | bytes 417800 | tf_op jit(solution)/shard_map/ppermute | solution.py:341
  57.0 2.2 %collective-permute-start.7 = (bf16[272,256]{1,0:T(8,128)(2,1)S(1)}, bf16[272,256]{1,0:T(8,128)(2,1)S(1)}, u32[]{:S(2)}, u32[]{:S(2)}) collective-permute-start(bf16[272,256]{1,0:T(8,128)(2,1)S(1)} %get-tuple-element.33.refs_0_), channel_id=1, source_target_pairs={{0,3},{1,2},{2,1},{3,0},{4,7},{5,6},{6,5},{7,4},{8,11},{9,10},{10,... | collective-permute-start | bytes 417800 | tf_op jit(solution)/shard_map/ppermute | solution.py:341
  59.2 1.2 %collective-permute-start.8 = (bf16[272,256]{1,0:T(8,128)(2,1)S(1)}, bf16[272,256]{1,0:T(8,128)(2,1)S(1)}, u32[]{:S(2)}, u32[]{:S(2)}) collective-permute-start(bf16[272,256]{1,0:T(8,128)(2,1)S(1)} %get-tuple-element.33.refs_0_), channel_id=1, source_target_pairs={{0,27},{1,26},{2,25},{3,24},{4,31},{5,30},{6,29},{7,28},{8,19},{9,... | collective-permute-start | bytes 417800 | tf_op jit(solution)/shard_map/ppermute | solution.py:341
  60.8 3.9 %collective-permute-done.7.refs_2_ = bf16[272,256]{1,0:T(8,128)(2,1)S(1)} collective-permute-done((bf16[272,256]{1,0:T(8,128)(2,1)S(1)}, bf16[272,256]{1,0:T(8,128)(2,1)S(1)}, u32[]{:S(2)}, u32[]{:S(2)}) %collective-permute-start.7) | collective-permute-done | bytes 139296 | tf_op jit(solution)/shard_map/ppermute | solution.py:341
  64.6 3.0 %collective-permute-done.8.refs_3_ = bf16[272,256]{1,0:T(8,128)(2,1)S(1)} collective-permute-done((bf16[272,256]{1,0:T(8,128)(2,1)S(1)}, bf16[272,256]{1,0:T(8,128)(2,1)S(1)}, u32[]{:S(2)}, u32[]{:S(2)}) %collective-permute-start.8) | collective-permute-done | bytes 139296 | tf_op jit(solution)/shard_map/ppermute | solution.py:341
  67.6 0.8 collective-permute-start.9
  68.5 0.7 collective-permute-start.17
  69.1 6.7 %collective-permute-done.9.refs_1_ = f32[272,256]{1,0:T(8,128)S(1)} collective-permute-done((f32[272,256]{1,0:T(8,128)S(1)}, f32[272,256]{1,0:T(8,128)S(1)}, u32[]{:S(2)}, u32[]{:S(2)}) %collective-permute-start.9) | collective-permute-done | bytes 278560 | tf_op jit(solution)/shard_map/ppermute | solution.py:341
  76.1 1.2 %hold.1 = (bf16[1024,256]{1,0:T(8,128)(2,1)S(1)}, bf16[1024,256]{1,0:T(8,128)(2,1)S(1)}, bf16[1024,256]{1,0:T(8,128)(2,1)S(1)}, bf16[2048,256]{1,0:T(8,128)(2,1)S(1)}) custom-call(bf16[1024,256]{1,0:T(8,128)(2,1)S(1)} %collective-permute-done.13.u0, bf16[1024,256]{1,0:T(8,128)(2,1)S(1)} %collective-permute-done.14.u1, ...), custom_call_target="tpu_custom_call" | custom-call | tf_op jit(solution)/shard_map/hold/pallas_call | solution.py:329
  77.3 3.7 %collective-permute-start.12 = (bf16[272,256]{1,0:T(8,128)(2,1)S(1)}, bf16[272,256]{1,0:T(8,128)(2,1)S(1)}, u32[]{:S(2)}, u32[]{:S(2)}) collective-permute-start(bf16[272,256]{1,0:T(8,128)(2,1)S(1)} %add.3.refs_0_), channel_id=1, source_target_pairs={{0,9},{1,8},{2,11},{3,10},{4,13},{5,12},{6,15},{7,14},{8,1},{9,0},... | collective-permute-start | bytes 417800 | tf_op jit(solution)/shard_map/ppermute | solution.py:341
  81.0 3.8 %pass2.3.refs_12_ = bf16[2048,256]{1,0:T(8,128)(2,1)} custom-call(bf16[2048,256]{1,0:T(8,128)(2,1)S(1)} %get-tuple-element.36.c_ref, bf16[1024,256]{1,0:T(8,128)(2,1)S(1)} %copy-done, bf16[1024,256]{1,0:T(8,128)(2,1)S(1)} %get-tuple-element.37.refs_1_, bf16[1024,256]{1,0:T(8,128)(2,1)S(1)} %get-tuple-element.38.refs_2_, ...), custom_call_target="tpu_custom_call" | custom-call | flops 2147483648 | bytes 2097152 | tf_op jit(solution)/shard_map/pass2/pallas_call | solution.py:300
  84.9 3.8 %pass2.4.refs_12_ = bf16[2048,256]{1,0:T(8,128)(2,1)} custom-call(bf16[2048,256]{1,0:T(8,128)(2,1)S(1)} %get-tuple-element.36.c_ref, bf16[1024,256]{1,0:T(8,128)(2,1)S(1)} %copy-done, bf16[1024,256]{1,0:T(8,128)(2,1)S(1)} %get-tuple-element.37.refs_1_, bf16[1024,256]{1,0:T(8,128)(2,1)S(1)} %get-tuple-element.38.refs_2_, ...), custom_call_target="tpu_custom_call", output_to_operand_aliasing={{}: (13, {})} | custom-call | flops 2147483648 | bytes 2097152 | tf_op jit(solution)/shard_map/pass2/pallas_call | solution.py:300
  88.7 6.2 %pass2.5 = bf16[2048,256]{1,0:T(8,128)(2,1)} custom-call(bf16[2048,256]{1,0:T(8,128)(2,1)S(1)} %get-tuple-element.36.c_ref, bf16[1024,256]{1,0:T(8,128)(2,1)S(1)} %copy-done, bf16[1024,256]{1,0:T(8,128)(2,1)S(1)} %get-tuple-element.37.refs_1_, bf16[1024,256]{1,0:T(8,128)(2,1)S(1)} %get-tuple-element.38.refs_2_, ...), custom_call_target="tpu_custom_call", output_to_operand_aliasing={{}: (13, {})} | custom-call | flops 4294967296 | bytes 2097152 | tf_op jit(solution)/shard_map/pass2/pallas_call | solution.py:300
  94.9 0.8 finish.1
  (30 shorter events, 1.1 us)
Async XLA Ops:
  0.6 32.8 %copy-start = (bf16[1024,256]{1,0:T(8,128)(2,1)S(1)}, bf16[1024,256]{1,0:T(8,128)(2,1)}, u32[]{:S(2)}) copy-start(bf16[1024,256]{1,0:T(8,128)(2,1)} %refs_0_.5) | copy-start | bytes 1572868
  0.6 32.8 %copy-start.5 = (s32[1024]{0:T(1024)S(1)}, s32[1024]{0:T(1024)}, u32[]{:S(2)}) copy-start(s32[1024]{0:T(1024)} %pos_ref.1) | copy-start | bytes 12292
  0.6 46.8 %collective-permute-start.14 = (bf16[1024,256]{1,0:T(8,128)(2,1)}, bf16[1024,256]{1,0:T(8,128)(2,1)S(1)}, u32[]{:S(2)}, u32[]{:S(2)}) collective-permute-start(bf16[1024,256]{1,0:T(8,128)(2,1)} %refs_0_.5), channel_id=1, source_target_pairs={{0,64},{32,96},{64,0},{96,32},{1,65},{33,97},{65,1},{97,33},{2,66}... | collective-permute-start | bytes 1572872 | tf_op jit(solution)/shard_map/ppermute | solution.py:341
  19.1 33.1 %all-to-all-start = ((f32[128,8,128]{2,1,0:T(8,128)}), f32[128,8,128]{2,1,0:T(8,128)S(1)}, u32[]{:S(2)}, u32[]{:S(2)}) async-start(f32[128,8,128]{2,1,0:T(8,128)} %get-tuple-element.23), calls=%async_computation | async-start | bytes 1048576 | tf_op jit(solution)/shard_map/all_to_all | solution.py:373
  29.9 13.6 %collective-permute-start = (bf16[256,256]{1,0:T(8,128)(2,1)S(1)}, bf16[256,256]{1,0:T(8,128)(2,1)S(1)}, u32[]{:S(2)}, u32[]{:S(2)}) collective-permute-start(bf16[256,256]{1,0:T(8,128)(2,1)S(1)} %get-tuple-element.25), channel_id=1, source_target_pairs={{0,8},{1,9},{2,10},{3,11},{4,12},{5,13},{6,14},{7,15},{8,0},{9,1},... | collective-permute-start | bytes 393224 | tf_op jit(solution)/shard_map/ppermute | solution.py:341
  31.0 13.8 %collective-permute-start.1 = (bf16[256,256]{1,0:T(8,128)(2,1)S(1)}, bf16[256,256]{1,0:T(8,128)(2,1)S(1)}, u32[]{:S(2)}, u32[]{:S(2)}) collective-permute-start(bf16[256,256]{1,0:T(8,128)(2,1)S(1)} %get-tuple-element.26), channel_id=1, source_target_pairs={{0,1},{1,0},{2,3},{3,2},{4,5},{5,4},{6,7},{7,6},{8,9},{9,8},{10,11... | collective-permute-start | bytes 393224 | tf_op jit(solution)/shard_map/ppermute | solution.py:341
  32.5 14.2 %collective-permute-start.2 = (bf16[256,256]{1,0:T(8,128)(2,1)S(1)}, bf16[256,256]{1,0:T(8,128)(2,1)S(1)}, u32[]{:S(2)}, u32[]{:S(2)}) collective-permute-start(bf16[256,256]{1,0:T(8,128)(2,1)S(1)} %get-tuple-element.27), channel_id=1, source_target_pairs={{0,9},{1,8},{2,11},{3,10},{4,13},{5,12},{6,15},{7,14},{8,1},{9,0},... | collective-permute-start | bytes 393224 | tf_op jit(solution)/shard_map/ppermute | solution.py:341
  37.7 10.2 %collective-permute-start.3 = (bf16[272,256]{1,0:T(8,128)(2,1)S(1)}, bf16[272,256]{1,0:T(8,128)(2,1)S(1)}, u32[]{:S(2)}, u32[]{:S(2)}) collective-permute-start(bf16[272,256]{1,0:T(8,128)(2,1)S(1)} %get-tuple-element.29), channel_id=1, source_target_pairs={{0,8},{1,9},{2,10},{3,11},{4,12},{5,13},{6,14},{7,15},{8,0},{9,1},... | collective-permute-start | bytes 417800 | tf_op jit(solution)/shard_map/ppermute | solution.py:341
  43.5 5.7 %collective-permute-start.4 = (bf16[272,256]{1,0:T(8,128)(2,1)S(1)}, bf16[272,256]{1,0:T(8,128)(2,1)S(1)}, u32[]{:S(2)}, u32[]{:S(2)}) collective-permute-start(bf16[272,256]{1,0:T(8,128)(2,1)S(1)} %get-tuple-element.30), channel_id=1, source_target_pairs={{0,1},{1,0},{2,3},{3,2},{4,5},{5,4},{6,7},{7,6},{8,9},{9,8},{10,11... | collective-permute-start | bytes 417800 | tf_op jit(solution)/shard_map/ppermute | solution.py:341
  44.8 0.7 copy-start.1
  45.5 6.8 %collective-permute-start.5 = (bf16[272,256]{1,0:T(8,128)(2,1)S(1)}, bf16[272,256]{1,0:T(8,128)(2,1)S(1)}, u32[]{:S(2)}, u32[]{:S(2)}) collective-permute-start(bf16[272,256]{1,0:T(8,128)(2,1)S(1)} %get-tuple-element.31), channel_id=1, source_target_pairs={{0,9},{1,8},{2,11},{3,10},{4,13},{5,12},{6,15},{7,14},{8,1},{9,0},... | collective-permute-start | bytes 417800 | tf_op jit(solution)/shard_map/ppermute | solution.py:341
  46.7 0.7 copy-start.3
  47.4 28.5 %collective-permute-start.13 = (bf16[1024,256]{1,0:T(8,128)(2,1)S(1)}, bf16[1024,256]{1,0:T(8,128)(2,1)S(1)}, u32[]{:S(2)}, u32[]{:S(2)}) collective-permute-start(bf16[1024,256]{1,0:T(8,128)(2,1)S(1)} %copy-done), channel_id=1, source_target_pairs={{0,32},{32,0},{64,96},{96,64},{1,33},{33,1},{65,97},{97,65},{2,34}... | collective-permute-start | bytes 1572872 | tf_op jit(solution)/shard_map/ppermute | solution.py:341
  47.4 28.6 %collective-permute-start.15 = (bf16[1024,256]{1,0:T(8,128)(2,1)S(1)}, bf16[1024,256]{1,0:T(8,128)(2,1)S(1)}, u32[]{:S(2)}, u32[]{:S(2)}) collective-permute-start(bf16[1024,256]{1,0:T(8,128)(2,1)S(1)} %collective-permute-done.14.u1), channel_id=1, source_target_pairs={{0,32},{32,0},{64,96},{96,64},{1,33},{33,1},{65,97},{97,65},{2,34}... | collective-permute-start | bytes 1572872 | tf_op jit(solution)/shard_map/ppermute | solution.py:341
  52.2 0.9 copy-start.2
  53.1 0.9 copy-start.4
  54.4 6.3 %collective-permute-start.6 = (bf16[272,256]{1,0:T(8,128)(2,1)S(1)}, bf16[272,256]{1,0:T(8,128)(2,1)S(1)}, u32[]{:S(2)}, u32[]{:S(2)}) collective-permute-start(bf16[272,256]{1,0:T(8,128)(2,1)S(1)} %get-tuple-element.33.refs_0_), channel_id=1, source_target_pairs={{0,24},{1,25},{2,26},{3,27},{4,28},{5,29},{6,30},{7,31},{8,16},{9,... | collective-permute-start | bytes 417800 | tf_op jit(solution)/shard_map/ppermute | solution.py:341
  57.0 7.6 %collective-permute-start.7 = (bf16[272,256]{1,0:T(8,128)(2,1)S(1)}, bf16[272,256]{1,0:T(8,128)(2,1)S(1)}, u32[]{:S(2)}, u32[]{:S(2)}) collective-permute-start(bf16[272,256]{1,0:T(8,128)(2,1)S(1)} %get-tuple-element.33.refs_0_), channel_id=1, source_target_pairs={{0,3},{1,2},{2,1},{3,0},{4,7},{5,6},{6,5},{7,4},{8,11},{9,10},{10,... | collective-permute-start | bytes 417800 | tf_op jit(solution)/shard_map/ppermute | solution.py:341
  59.2 8.4 %collective-permute-start.8 = (bf16[272,256]{1,0:T(8,128)(2,1)S(1)}, bf16[272,256]{1,0:T(8,128)(2,1)S(1)}, u32[]{:S(2)}, u32[]{:S(2)}) collective-permute-start(bf16[272,256]{1,0:T(8,128)(2,1)S(1)} %get-tuple-element.33.refs_0_), channel_id=1, source_target_pairs={{0,27},{1,26},{2,25},{3,24},{4,31},{5,30},{6,29},{7,28},{8,19},{9,... | collective-permute-start | bytes 417800 | tf_op jit(solution)/shard_map/ppermute | solution.py:341
  67.6 8.2 %collective-permute-start.9 = (f32[272,256]{1,0:T(8,128)S(1)}, f32[272,256]{1,0:T(8,128)S(1)}, u32[]{:S(2)}, u32[]{:S(2)}) collective-permute-start(f32[272,256]{1,0:T(8,128)S(1)} %add.2.refs_0_), channel_id=1, source_target_pairs={{0,4},{1,5},{2,6},{3,7},{4,0},{5,1},{6,2},{7,3},{8,12},{9,13},{10,... | collective-permute-start | bytes 835592 | tf_op jit(solution)/shard_map/ppermute | solution.py:341
  68.4 8.9 %collective-permute-start.16 = (s32[8,128]{1,0:T(8,128)S(1)}, s32[8,128]{1,0:T(8,128)S(1)}, u32[]{:S(2)}, u32[]{:S(2)}) collective-permute-start(s32[8,128]{1,0:T(8,128)S(1)} %bitcast.2), channel_id=1, source_target_pairs={{0,32},{32,0},{64,96},{96,64},{1,33},{33,1},{65,97},{97,65},{2,34}... | collective-permute-start | bytes 12296 | tf_op jit(solution)/shard_map/ppermute | solution.py:341
  68.5 12.6 %collective-permute-start.17 = (s32[8,128]{1,0:T(8,128)S(1)}, s32[8,128]{1,0:T(8,128)S(1)}, u32[]{:S(2)}, u32[]{:S(2)}) collective-permute-start(s32[8,128]{1,0:T(8,128)S(1)} %bitcast.3), channel_id=1, source_target_pairs={{0,64},{32,96},{64,0},{96,32},{1,65},{33,97},{65,1},{97,33},{2,66}... | collective-permute-start | bytes 12296 | tf_op jit(solution)/shard_map/ppermute | solution.py:341
  75.8 5.2 %collective-permute-start.18 = (s32[8,128]{1,0:T(8,128)S(1)}, s32[8,128]{1,0:T(8,128)S(1)}, u32[]{:S(2)}, u32[]{:S(2)}) collective-permute-start(s32[8,128]{1,0:T(8,128)S(1)} %bitcast.4), channel_id=1, source_target_pairs={{0,96},{32,64},{64,32},{96,0},{1,97},{33,65},{65,33},{97,1},{2,98}... | collective-permute-start | bytes 12296 | tf_op jit(solution)/shard_map/ppermute | solution.py:341
  75.9 19.0 %collective-permute-start.10 = (bf16[272,256]{1,0:T(8,128)(2,1)S(1)}, bf16[272,256]{1,0:T(8,128)(2,1)S(1)}, u32[]{:S(2)}, u32[]{:S(2)}) collective-permute-start(bf16[272,256]{1,0:T(8,128)(2,1)S(1)} %add.3.refs_0_), channel_id=1, source_target_pairs={{0,8},{1,9},{2,10},{3,11},{4,12},{5,13},{6,14},{7,15},{8,0},{9,1},... | collective-permute-start | bytes 417800 | tf_op jit(solution)/shard_map/ppermute | solution.py:341
  76.0 18.9 %collective-permute-start.11 = (bf16[272,256]{1,0:T(8,128)(2,1)S(1)}, bf16[272,256]{1,0:T(8,128)(2,1)S(1)}, u32[]{:S(2)}, u32[]{:S(2)}) collective-permute-start(bf16[272,256]{1,0:T(8,128)(2,1)S(1)} %add.3.refs_0_), channel_id=1, source_target_pairs={{0,1},{1,0},{2,3},{3,2},{4,5},{5,4},{6,7},{7,6},{8,9},{9,8},{10,11... | collective-permute-start | bytes 417800 | tf_op jit(solution)/shard_map/ppermute | solution.py:341
  77.3 17.6 %collective-permute-start.12 = (bf16[272,256]{1,0:T(8,128)(2,1)S(1)}, bf16[272,256]{1,0:T(8,128)(2,1)S(1)}, u32[]{:S(2)}, u32[]{:S(2)}) collective-permute-start(bf16[272,256]{1,0:T(8,128)(2,1)S(1)} %add.3.refs_0_), channel_id=1, source_target_pairs={{0,9},{1,8},{2,11},{3,10},{4,13},{5,12},{6,15},{7,14},{8,1},{9,0},... | collective-permute-start | bytes 417800 | tf_op jit(solution)/shard_map/ppermute | solution.py:341
